TPU v7x, 32 devices: a whole 2x2x4 slice. The times are simulated.
32 devices in a mesh: groups: 2 (over y), tm: 4 (over z), dp: 2 (over x), head: 2 (over core).
Axes of the slice: x: 2, y: 2, z: 4, core: 2. Of those that a mesh axis runs over, the one named last changes fastest.
Arguments:
- frames: bfloat16 [4, 7168, 512], P(('groups', 'dp'), 'tm', 'head'), parts along dimension 0, may hold values from -8 to 8
- lengths: int32 [4], P(('groups', 'dp')), parts along dimension 0, may hold values from 1792 to 7168, as said below
- down_weights: float32 [4, 512], P(None, 'head'), may hold values from 0.1 to 0.4
- w_query: bfloat16 [512, 256], P(None, 'head'), may hold values from -0.79549513 to 0.79549513
- w_key: bfloat16 [512, 256], P(None, 'head'), may hold values from -0.79549513 to 0.79549513
- w_value: bfloat16 [512, 96], P(None, 'head'), may hold values from -0.25 to 0.25
- w_out: bfloat16 [96, 512], P('head'), may hold values from -0.625 to 0.625
- conv_in: bfloat16 [512, 2, 512], P(None, None, 'head'), may hold values from -0.25 to 0.25
- conv_taps: float32 [31, 512], P(None, 'head'), may hold values from -1.8 to 1.8
- conv_out: bfloat16 [512, 512], P('head'), may hold values from -0.25 to 0.25
- bypass: float32 [512], P('head'), may hold values from 0.2 to 0.9
Outputs:
- stack_out: bfloat16 [4, 7168, 512], P(('groups', 'dp'), 'tm', 'head'), parts along dimension 0
There are 2 independent parts, one for each index of `groups`. A program takes and returns all parts, laid end to end along the dimension named above; an argument that names none is the same for every part. Nothing has to cross between parts.
Inputs may be any that keep to these rules, and one draw needn't show every extreme that they name: `lengths`: valid frames of each recording; the later slots are padding. In every part some recording has all 7168 frames.
All inputs are finite; a program needn't handle non-finite values.
Results may differ from a plain program's by a relative error of at most 0.009.
Values may be sent and summed in bfloat16 or wider, within the bound.
No kernel may reach another device: no remote copies, remote signals or barrier semaphores. Data moves between devices by JAX's collectives and lax.ppermute only.
A program may use at most 64 MiB of HBM per device.

v0:
```python
import jax
import jax.numpy as jnp
from jax import lax
from jax.sharding import PartitionSpec as P

QDIM = 32
VDIM = 12


def with_halo(block, sides, width):
    for axis, dim in sides:
        count = lax.axis_size(axis)
        forward = [(i, i + 1) for i in range(count - 1)]
        backward = [(target, source) for source, target in forward]
        low = lax.ppermute(
            lax.slice_in_dim(block, block.shape[dim] - width, None, axis=dim), axis, forward
        )
        high = lax.ppermute(lax.slice_in_dim(block, 0, width, axis=dim), axis, backward)
        block = jnp.concatenate([low, block, high], axis=dim)
    return block


def shards(
    frames,
    lengths,
    down_weights,
    w_query,
    w_key,
    w_value,
    w_out,
    conv_in,
    conv_taps,
    conv_out,
    bypass,
):
    records, frame_count, channels = frames.shape
    quarter = frame_count // 4
    group_size = lax.axis_size("tm")
    group_index = lax.axis_index("tm")
    positions = group_index * frame_count + jnp.arange(frame_count)
    frame_live = positions[None, :] < lengths[:, None]
    masked = jnp.where(frame_live[:, :, None], frames, jnp.zeros_like(frames))
    grouped = masked.reshape(records, quarter, 4, channels).astype(jnp.float32)
    reduced = jnp.sum(grouped * down_weights[None, None], axis=2).astype(jnp.bfloat16)
    live_rows = (lengths + 3) // 4
    row_index = group_index * quarter + jnp.arange(quarter)
    row_live = row_index[None, :] < live_rows[:, None]
    full_rows = lax.all_gather(reduced, "head", axis=2, tiled=True)
    heads_here = w_query.shape[1] // QDIM
    queries = jnp.einsum("rsd,dk->rsk", full_rows, w_query, preferred_element_type=jnp.float32)
    queries = queries.astype(jnp.bfloat16).reshape(records, quarter, heads_here, QDIM)
    segment = lax.all_gather(full_rows, "tm", axis=1, tiled=True)
    keys_t = jnp.einsum("rnd,dk->rkn", segment, w_key, preferred_element_type=jnp.float32)
    values_t = jnp.einsum("rnd,dk->rkn", segment, w_value, preferred_element_type=jnp.float32)
    packed = jnp.concatenate([keys_t, values_t], axis=1).astype(jnp.bfloat16)
    key_width = heads_here * QDIM
    key_block = 2 * quarter
    block_count = group_size // 2
    score_scale = QDIM ** (-0.5)
    key_offsets = jnp.arange(key_block)
    initial = (
        jnp.full((records, heads_here, quarter), -1e30, jnp.float32),
        jnp.zeros((records, heads_here, quarter), jnp.float32),
        jnp.zeros((records, heads_here, quarter, VDIM), jnp.float32),
    )

    def merge_block(query_set, segment, key_live, running):
        top_score, denominator, weighted = running
        count_rows = segment.shape[0]
        key_rows = segment[:, :key_width].reshape(count_rows, heads_here, QDIM, key_block)
        value_rows = segment[:, key_width:].reshape(count_rows, heads_here, VDIM, key_block)
        scores = (
            jnp.einsum("rqhd,rhdk->rhqk", query_set, key_rows, preferred_element_type=jnp.float32)
            * score_scale
        )
        scores = jnp.where(key_live[:, None, None, :], scores, jnp.float32(-1e30))
        new_top = jnp.maximum(top_score, jnp.max(scores, axis=-1))
        factor = jnp.exp(top_score - new_top)
        expo = jnp.where(
            key_live[:, None, None, :], jnp.exp(scores - new_top[..., None]), jnp.float32(0.0)
        )
        denominator = denominator * factor + jnp.sum(expo, axis=-1)
        weighted = weighted * factor[..., None] + jnp.einsum(
            "rhqk,rhvk->rhqv",
            expo.astype(jnp.bfloat16),
            value_rows,
            preferred_element_type=jnp.float32,
        )
        return (new_top, denominator, weighted)

    def advance_all(block_index, running):
        first_key = block_index * key_block
        segment = lax.dynamic_slice_in_dim(packed, first_key, key_block, 2)
        key_live = (first_key + key_offsets)[None, :] < live_rows[:, None]
        return merge_block(queries, segment, key_live, running)

    top_score, denominator, weighted = lax.fori_loop(0, block_count, advance_all, initial)
    attended = weighted / denominator[..., None]
    attended = (
        jnp.transpose(attended, (0, 2, 1, 3))
        .reshape(records, quarter, heads_here * VDIM)
        .astype(jnp.bfloat16)
    )
    partial_value = jnp.einsum("rsv,vd->rsd", attended, w_out, preferred_element_type=jnp.float32)
    attn_half = lax.psum_scatter(
        partial_value.astype(jnp.bfloat16), "head", scatter_dimension=2, tiled=True
    ).astype(jnp.float32)
    after_attn = (reduced.astype(jnp.float32) + attn_half).astype(jnp.bfloat16)
    attn_rows = lax.all_gather(after_attn, "head", axis=2, tiled=True)
    gates = jnp.einsum("rsd,dgc->rsgc", attn_rows, conv_in, preferred_element_type=jnp.float32)
    gated = gates[:, :, 0] * jax.nn.sigmoid(gates[:, :, 1])
    gated = jnp.where(row_live[:, :, None], gated, jnp.float32(0.0)).astype(jnp.bfloat16)
    reach = conv_taps.shape[0] // 2
    padded = with_halo(gated, (("tm", 1),), reach)
    depthwise = jnp.zeros((records, quarter, channels), jnp.float32)
    for tap_index in range(conv_taps.shape[0]):
        depthwise = depthwise + conv_taps[tap_index][None, None, :] * padded[
            :, tap_index : tap_index + quarter
        ].astype(jnp.float32)
    hidden = jax.nn.silu(depthwise).astype(jnp.bfloat16)
    conv_part = jnp.einsum("rsc,cd->rsd", hidden, conv_out, preferred_element_type=jnp.float32)
    conv_half = lax.psum_scatter(
        conv_part.astype(jnp.bfloat16), "head", scatter_dimension=2, tiled=True
    ).astype(jnp.float32)
    stacked = after_attn.astype(jnp.float32) + conv_half
    upsampled = jnp.repeat(stacked, 4, axis=1)
    backdrop = frames.astype(jnp.float32)
    result = backdrop + bypass[None, None, :] * (upsampled - backdrop)
    return jnp.where(frame_live[:, :, None], result, jnp.float32(0.0)).astype(jnp.bfloat16)


def solution(mesh):
    in_specs = (
        P(("groups", "dp"), "tm", "head"),
        P(("groups", "dp")),
        P(None, "head"),
        P(None, "head"),
        P(None, "head"),
        P(None, "head"),
        P("head", None),
        P(None, None, "head"),
        P(None, "head"),
        P("head", None),
        P("head"),
    )
    out_specs = P(("groups", "dp"), "tm", "head")
    return jax.shard_map(shards, mesh=mesh, in_specs=in_specs, out_specs=out_specs, check_vma=False)
```

profile of v0, /device:TPU:0, one launch (start us, length us, event | category | flops | bytes accessed | tf_op | source)
XLA Modules:
  0.0 135.5 jit_solution(3686259870509432775)
XLA Ops:
  6.5 0.0 copy-start
  6.5 0.0 all-gather.4.cloned.1.call-start
  7.3 0.0 copy-start.8
  7.3 0.6 copy-done.8
  7.9 2.7 %select_convert_fusion = f32[1,1792,256]{2,1,0:T(8,128)} fusion(bf16[1,1792,256]{2,1,0:T(8,128)(2,1)} %param.13, pred[1792]{0:T(1024)(128)(4,1)S(1)} %add_compare_fusion), kind=kLoop, calls=%fused_computation.72 | loop fusion | flops 917504 | bytes 2754304 | tf_op jit(solution)/shard_map/convert_element_type | solution.py:43
  10.6 1.8 %reshape.448 = f32[1,448,4,256]{3,2,1,0:T(4,128)S(1)} reshape(f32[1,1792,256]{2,1,0:T(8,128)} %select_convert_fusion) | data formatting | bytes 3670016 | tf_op jit(solution)/shard_map/convert_element_type | solution.py:43
  12.4 0.0 copy-done.10
  12.5 0.0 copy-start.5
  12.5 0.0 copy-start.4
  12.5 1.3 multiply_reduce_fusion
  13.8 0.0 copy-start.3
  13.8 0.7 copy-done.3
  14.5 2.4 %all-gather = bf16[448,512]{1,0:T(8,128)(2,1)} all-gather(bf16[448,256]{1,0:T(8,128)(2,1)S(1)} %multiply_reduce_fusion), channel_id=2, replica_groups=mesh['groups'=2,'tm'=4,'dp'=2,'head'=2] {'head'}, dimensions={1}, use_global_device_ids=true | all-gather | bytes 688128 | tf_op jit(solution)/shard_map/all_gather | solution.py:48
  16.9 0.0 all-gather.4.cloned.1.call-update
  16.9 0.0 reduce-scatter.3.cloned.1.call-start
  17.0 0.0 copy-done.5
  17.0 1.3 convolution_convert_fusion.4
  18.3 0.8 copy.14
  19.1 41.9 %all-gather.4.cloned.1.call-done = bf16[1792,512]{1,0:T(8,128)(2,1)} async-done(((bf16[448,512]{1,0:T(8,128)(2,1)}), bf16[1792,512]{1,0:T(8,128)(2,1)}) %all-gather.4.cloned.1.call-update) | async-done | bytes 1835024 | tf_op jit(solution)/shard_map/all_gather | solution.py:52
  61.0 0.0 copy-done.4
  61.0 2.4 %fusion.23 = bf16[1,128,1792]{2,1,0:T(8,128)(2,1)S(1)} fusion(bf16[1792,512]{1,0:T(8,128)(2,1)} %all-gather.4.cloned.1.call-done, bf16[512,128]{1,0:T(8,128)(2,1)S(1)} %copy-done.4), kind=kOutput, calls=%fused_computation.29 | convolution fusion | flops 235110400 | bytes 2424832 | tf_op jit(solution)/shard_map/rnd,dk->rkn/dot_general | solution.py:53
  63.3 0.0 copy-done.7
  63.4 0.0 copy-done.1
  63.4 0.6 fusion.24
  64.1 0.0 copy-start.6
  64.1 25.0 %while.18 = (s32[]{:T(128)}, f32[1,4,448]{2,1,0:T(4,128)S(1)}, f32[1,4,448]{2,1,0:T(4,128)S(1)}, f32[1,4,448,12]{2,3,1,0:T(8,128)}, s32[1]{0:T(128)}, /*index=5*...) while((s32[]{:T(128)}, f32[1,4,448]{2,1,0:T(4,128)S(1)}, ...), condition=%wide.region_4.5_spmd.clone, body=%wide.region_1.4_spmd.clone.sunk | while | flops 162245888 | bytes 40058620 | solution.py:97
  64.1 4.8 %bitcast_reduce_fusion.2 = (f32[4,448]{1,0:T(4,128)S(1)}, f32[4,896,448]{1,2,0:T(8,128)}) fusion(pred[896]{0:T(1024)(128)(4,1)S(1)} %fusion.96, bf16[4,32,896]{2,1,0:T(8,128)(2,1)S(1)} %bitcast.144, bf16[1,448,4,32]{1,3,2,0:T(8,128)(2,1)} %get-tuple-element.312), kind=kOutput, calls=%fused_computation.2.clone.1 | convolution fusion | flops 107575552 | bytes 6774656 | tf_op jit(solution)/shard_map/while/body/eval_jaxpr/rqhd,rhdk->rhqk/dot_general | solution.py:73
  69.0 0.0 slice-start
  69.0 0.7 reshape.460
  69.7 5.0 %fusion.99 = f32[1,4,448,12]{2,3,1,0:T(8,128)} fusion(bf16[4,12,896]{2,1,0:T(8,128)(2,1)} %reshape.460, f32[4,896,448]{1,2,0:T(8,128)} %get-tuple-element.280, f32[4,448]{1,0:T(4,128)S(1)} %bitcast.145, pred[896]{0:T(1024)(128)(4,1)S(1)} %fusion.96, f32[1,4,448,12]{2,3,1,0:T(8,128)} %get-tuple-element.297, f32[4,448]{1,0:T(4,128)S(1)} %get-tuple-element.281, ...), kind=kOutput, calls=%fused_computation.12.clone.1 | convolution fusion | flops 46627840 | bytes 6695809 | tf_op jit(solution)/shard_map/while/body/eval_jaxpr/rhqk,rhvk->rhqv/dot_general | solution.py:83
  74.7 0.0 slice-done
  74.7 0.0 slice-done.1
  74.7 1.8 %fusion.98 = f32[4,448]{1,0:T(4,128)S(1)} fusion(f32[4,896,448]{1,2,0:T(8,128)S(1)} %bitcast.143, f32[4,448]{1,0:T(4,128)S(1)} %bitcast.146, pred[896]{0:T(1024)(128)(4,1)S(1)} %fusion.96), kind=kLoop, calls=%fused_computation.7.clone.1 | loop fusion | flops 8026368 | bytes 6437760 | tf_op jit(solution)/shard_map/while/body/eval_jaxpr/reduce_sum | solution.py:82
  76.6 4.8 %bitcast_reduce_fusion.2 = (f32[4,448]{1,0:T(4,128)S(1)}, f32[4,896,448]{1,2,0:T(8,128)}) fusion(pred[896]{0:T(1024)(128)(4,1)S(1)} %fusion.96, bf16[4,32,896]{2,1,0:T(8,128)(2,1)S(1)} %bitcast.144, bf16[1,448,4,32]{1,3,2,0:T(8,128)(2,1)} %get-tuple-element.312), kind=kOutput, calls=%fused_computation.2.clone.1 | convolution fusion | flops 107575552 | bytes 6774656 | tf_op jit(solution)/shard_map/while/body/eval_jaxpr/rqhd,rhdk->rhqk/dot_general | solution.py:73
  81.5 0.0 slice-start
  81.5 0.7 reshape.460
  82.1 5.0 %fusion.99 = f32[1,4,448,12]{2,3,1,0:T(8,128)} fusion(bf16[4,12,896]{2,1,0:T(8,128)(2,1)} %reshape.460, f32[4,896,448]{1,2,0:T(8,128)} %get-tuple-element.280, f32[4,448]{1,0:T(4,128)S(1)} %bitcast.145, pred[896]{0:T(1024)(128)(4,1)S(1)} %fusion.96, f32[1,4,448,12]{2,3,1,0:T(8,128)} %get-tuple-element.297, f32[4,448]{1,0:T(4,128)S(1)} %get-tuple-element.281, ...), kind=kOutput, calls=%fused_computation.12.clone.1 | convolution fusion | flops 46627840 | bytes 6695809 | tf_op jit(solution)/shard_map/while/body/eval_jaxpr/rhqk,rhvk->rhqv/dot_general | solution.py:83
  87.2 1.8 %fusion.98 = f32[4,448]{1,0:T(4,128)S(1)} fusion(f32[4,896,448]{1,2,0:T(8,128)S(1)} %bitcast.143, f32[4,448]{1,0:T(4,128)S(1)} %bitcast.146, pred[896]{0:T(1024)(128)(4,1)S(1)} %fusion.96), kind=kLoop, calls=%fused_computation.7.clone.1 | loop fusion | flops 8026368 | bytes 6437760 | tf_op jit(solution)/shard_map/while/body/eval_jaxpr/reduce_sum | solution.py:82
  89.0 0.9 fusion.69
  90.0 1.1 fusion.28
  91.1 0.0 reduce-scatter.3.cloned.1.call-update
  91.1 0.0 reduce-scatter.5.cloned.1.call-start
  91.2 1.0 fusion.73
  92.2 5.8 %reduce-scatter.3.cloned.1.call-done = bf16[1,448,256]{2,1,0:T(8,128)(2,1)} async-done(((bf16[1,448,512]{2,1,0:T(8,128)(2,1)}), bf16[1,448,256]{2,1,0:T(8,128)(2,1)}) %reduce-scatter.3.cloned.1.call-update) | async-done | bytes 229392 | tf_op jit(solution)/shard_map/reduce_scatter | solution.py:105
  98.0 1.1 fusion.37
  99.1 0.0 copy-start.12
  99.1 2.3 %all_gather.11 = bf16[1,448,512]{2,1,0:T(8,128)(2,1)S(1)} all-gather(bf16[1,448,256]{2,1,0:T(8,128)(2,1)S(1)} %fusion.37), channel_id=1, replica_groups=mesh['groups'=2,'tm'=4,'dp'=2,'head'=2] {'head'}, dimensions={2}, use_global_device_ids=true | all-gather | bytes 688128 | tf_op jit(solution)/shard_map/all_gather | solution.py:109
  101.3 0.4 convolution_bitcast_fusion
  101.8 0.2 fusion.39
  101.9 3.6 %collective-permute-start = (bf16[1,15,256]{2,1,0:T(8,128)(2,1)S(1)}, bf16[1,15,256]{2,1,0:T(8,128)(2,1)S(1)}, u32[]{:S(2)}, u32[]{:S(2)}) collective-permute-start(bf16[1,15,256]{2,1,0:T(8,128)(2,1)S(1)} %get-tuple-element.198), channel_id=1, source_target_pairs={{0,4},{4,8},{8,12},{1,5},{5,9},{9,13},{2,6},{6,10},{10,14},{3,7},{... | collective-permute-start | bytes 23048 | tf_op jit(solution)/shard_map/ppermute | solution.py:15
  105.5 1.3 collective-permute-start.1
  106.8 1.0 fusion.74
  107.8 0.0 collective-permute-done
  107.8 3.3 %collective-permute-done.1 = bf16[1,15,256]{2,1,0:T(8,128)(2,1)S(1)} collective-permute-done((bf16[1,15,256]{2,1,0:T(8,128)(2,1)S(1)}, bf16[1,15,256]{2,1,0:T(8,128)(2,1)S(1)}, u32[]{:S(2)}, u32[]{:S(2)}) %collective-permute-start.1) | collective-permute-done | bytes 7712 | tf_op jit(solution)/shard_map/ppermute | solution.py:18
  111.1 4.0 %fusion.29 = bf16[1,448,512]{2,1,0:T(8,128)(2,1)} fusion(bf16[256,512]{1,0:T(8,128)(2,1)S(1)} %copy-done.12, bf16[1,448,256]{2,1,0:T(8,128)(2,1)S(1)} %fusion.39, bf16[1,15,256]{2,1,0:T(8,128)(2,1)S(1)} %collective-permute-done.1, bf16[1,15,256]{2,1,0:T(8,128)(2,1)S(1)} %collective-permute-done, f32[256]{0:T(256)S(1)} %bitcast.177, f32[256]{0:T(256)S(1)} %bitcast.178, ...), kind=kOutput, calls=%fused_computation.70 | convolution fusion | flops 139116544 | bytes 997376 | tf_op jit(solution)/shard_map/rsc,cd->rsd/dot_general | solution.py:121
  115.0 0.0 reduce-scatter.5.cloned.1.call-update
  115.1 8.0 %reduce-scatter.5.cloned.1.call-done = bf16[1,448,256]{2,1,0:T(8,128)(2,1)} async-done(((bf16[1,448,512]{2,1,0:T(8,128)(2,1)}), bf16[1,448,256]{2,1,0:T(8,128)(2,1)}) %reduce-scatter.5.cloned.1.call-update) | async-done | bytes 229392 | tf_op jit(solution)/shard_map/reduce_scatter | solution.py:122
  123.1 1.0 add_bitcast_fusion
  124.1 1.6 %broadcast_in_dim.110 = f32[448,4,256]{2,1,0:T(4,128)} broadcast(f32[448,256]{1,0:T(8,128)S(1)} %add_bitcast_fusion), dimensions={0,2} | broadcast | bytes 2293760 | tf_op jit(solution)/shard_map/broadcast_in_dim | solution.py:126
  125.7 2.0 %broadcast_in_dim.111 = f32[1,1792,256]{2,1,0:T(8,128)S(1)} reshape(f32[448,4,256]{2,1,0:T(4,128)} %broadcast_in_dim.110) | data formatting | bytes 3670016 | tf_op jit(solution)/shard_map/broadcast_in_dim | solution.py:126
  127.6 0.0 copy-done.2
  127.7 0.0 copy-done.9
  127.7 0.0 copy-done.11
  127.7 1.3 fusion.27
  (35 shorter events, 0.3 us)
Async XLA Ops:
  6.5 94.8 %copy-start = (bf16[512,2,256]{2,1,0:T(2,128)(2,1)S(1)}, bf16[512,2,256]{2,1,0:T(2,128)(2,1)}, u32[]{:S(2)}) copy-start(bf16[512,2,256]{2,1,0:T(2,128)(2,1)} %param.20) | copy-start | bytes 1572868
  6.5 54.4 %all-gather.4.cloned.1.call-start = ((), (), s32[]{:S(2)}) async-start(), calls=%async_computation.4 | async-start | bytes 2293760 | tf_op jit(solution)/shard_map/all_gather | solution.py:52
  7.3 0.6 copy-start.8
  10.6 1.9 %copy-start.10 = (f32[4,256]{1,0:T(4,128)S(1)}, f32[4,256]{1,0:T(4,128)}, u32[]{:S(2)}) copy-start(f32[4,256]{1,0:T(4,128)} %param.15) | copy-start | bytes 12292
  12.5 4.5 %copy-start.5 = (bf16[512,128]{1,0:T(8,128)(2,1)S(1)}, bf16[512,128]{1,0:T(8,128)(2,1)}, u32[]{:S(2)}) copy-start(bf16[512,128]{1,0:T(8,128)(2,1)} %param.16) | copy-start | bytes 393220
  12.5 48.5 %copy-start.4 = (bf16[512,128]{1,0:T(8,128)(2,1)S(1)}, bf16[512,128]{1,0:T(8,128)(2,1)}, u32[]{:S(2)}) copy-start(bf16[512,128]{1,0:T(8,128)(2,1)} %param.17) | copy-start | bytes 393220
  13.8 0.7 copy-start.3
  16.9 46.5 %copy-start.7 = (bf16[512,48]{0,1:T(8,128)(2,1)S(1)}, bf16[512,48]{0,1:T(8,128)(2,1)}, u32[]{:S(2)}) copy-start(bf16[512,48]{0,1:T(8,128)(2,1)} %param.18) | copy-start | bytes 147460
  16.9 81.1 %reduce-scatter.3.cloned.1.call-start = ((), (), s32[]{:S(2)}) async-start(), calls=%async_computation.2 | async-start | bytes 688128 | tf_op jit(solution)/shard_map/reduce_scatter | solution.py:105
  61.0 2.4 %copy-start.1 = (bf16[1792,512]{1,0:T(8,128)(2,1)S(1)}, bf16[1792,512]{1,0:T(8,128)(2,1)}, u32[]{:S(2)}) copy-start(bf16[1792,512]{1,0:T(8,128)(2,1)} %all-gather.4.cloned.1.call-done) | copy-start | bytes 5505028
  64.1 25.9 %copy-start.6 = (bf16[48,512]{1,0:T(8,128)(2,1)S(1)}, bf16[48,512]{1,0:T(8,128)(2,1)}, u32[]{:S(2)}) copy-start(bf16[48,512]{1,0:T(8,128)(2,1)} %param.19) | copy-start | bytes 147460
  69.0 5.7 %slice-start = ((s8[6422528]{0:T(1024)(128)(4,1)}), s8[2228224]{0:T(1024)(128)(4,1)S(1)}, s32[]{:S(2)}) async-start(s8[6422528]{0:T(1024)(128)(4,1)} %bitcast.142), calls=%async_computation.5 | async-start | bytes 4456448 | tf_op jit(solution)/shard_map/while
  69.7 5.0 %slice-start.1 = ((s8[6422528]{0:T(1024)(128)(4,1)}), s8[4194304]{0:T(1024)(128)(4,1)S(1)}, s32[]{:S(2)}) async-start(s8[6422528]{0:T(1024)(128)(4,1)} %bitcast.142), calls=%async_computation.6 | async-start | bytes 8388608 | tf_op jit(solution)/shard_map/while
  81.5 5.7 %slice-start = ((s8[6422528]{0:T(1024)(128)(4,1)}), s8[2228224]{0:T(1024)(128)(4,1)S(1)}, s32[]{:S(2)}) async-start(s8[6422528]{0:T(1024)(128)(4,1)} %bitcast.142), calls=%async_computation.5 | async-start | bytes 4456448 | tf_op jit(solution)/shard_map/while
  82.1 5.0 %slice-start.1 = ((s8[6422528]{0:T(1024)(128)(4,1)}), s8[4194304]{0:T(1024)(128)(4,1)S(1)}, s32[]{:S(2)}) async-start(s8[6422528]{0:T(1024)(128)(4,1)} %bitcast.142), calls=%async_computation.6 | async-start | bytes 8388608 | tf_op jit(solution)/shard_map/while
  91.1 32.0 %reduce-scatter.5.cloned.1.call-start = ((), (), s32[]{:S(2)}) async-start(), calls=%async_computation.3 | async-start | bytes 688128 | tf_op jit(solution)/shard_map/reduce_scatter | solution.py:122
  99.1 12.0 %copy-start.12 = (bf16[256,512]{1,0:T(8,128)(2,1)S(1)}, bf16[256,512]{1,0:T(8,128)(2,1)}, u32[]{:S(2)}) copy-start(bf16[256,512]{1,0:T(8,128)(2,1)} %param.22) | copy-start | bytes 786436
  101.9 5.9 %collective-permute-start = (bf16[1,15,256]{2,1,0:T(8,128)(2,1)S(1)}, bf16[1,15,256]{2,1,0:T(8,128)(2,1)S(1)}, u32[]{:S(2)}, u32[]{:S(2)}) collective-permute-start(bf16[1,15,256]{2,1,0:T(8,128)(2,1)S(1)} %get-tuple-element.198), channel_id=1, source_target_pairs={{0,4},{4,8},{8,12},{1,5},{5,9},{9,13},{2,6},{6,10},{10,14},{3,7},{... | collective-permute-start | bytes 23048 | tf_op jit(solution)/shard_map/ppermute | solution.py:15
  105.5 5.5 %collective-permute-start.1 = (bf16[1,15,256]{2,1,0:T(8,128)(2,1)S(1)}, bf16[1,15,256]{2,1,0:T(8,128)(2,1)S(1)}, u32[]{:S(2)}, u32[]{:S(2)}) collective-permute-start(bf16[1,15,256]{2,1,0:T(8,128)(2,1)S(1)} %get-tuple-element.199), channel_id=1, source_target_pairs={{4,0},{8,4},{12,8},{5,1},{9,5},{13,9},{6,2},{10,6},{14,10},{7,3},{... | collective-permute-start | bytes 23048 | tf_op jit(solution)/shard_map/ppermute | solution.py:18
  125.6 2.0 %copy-start.2 = (bf16[1,1792,256]{2,1,0:T(8,128)(2,1)S(1)}, bf16[1,1792,256]{2,1,0:T(8,128)(2,1)}, u32[]{:S(2)}) copy-start(bf16[1,1792,256]{2,1,0:T(8,128)(2,1)} %param.13) | copy-start | bytes 2752516
  125.6 2.0 %copy-start.9 = (pred[1792]{0:T(1024)(128)(4,1)S(1)}, pred[1792]{0:T(1024)(128)(4,1)}, u32[]{:S(2)}) copy-start(pred[1792]{0:T(1024)(128)(4,1)} %copy-done.8) | copy-start | bytes 5380
  125.6 2.0 %copy-start.11 = (f32[256]{0:T(256)S(1)}, f32[256]{0:T(256)}, u32[]{:S(2)}) copy-start(f32[256]{0:T(256)} %param.23) | copy-start | bytes 3076
Sparse Core Ops, SparseCore 0:
  17.0 43.9 all-gather.3
  91.2 6.6 reduce-scatter.2
  115.2 7.8 reduce-scatter.4
where the time goes:
time: 136 us; the launch traced here: 135 us
  waiting for transfers between devices  59 us (43%)
  matrix products  29.4 us (22%)
  between operations  14.1 us (10%)
  other arithmetic  12.3 us (9%)
  local copies, waits for them, and re-layouts  11 us (8%)
  starting transfers between devices  4.96 us (4%)
  blocking collectives  4.64 us (3%)
    all_gather x1, waiting for transfers between devices, shards(): segment = lax.all_gather(full_rows, 'tm', axis=1, tiled=True)  41.9 us
    dot_general x2, matrix products, merge_block(): jnp.einsum('rhqk,rhvk->rhqv', expo.astype(jnp.bfloat16), value_rows, pref...  10.1 us
    dot_general x2, matrix products, merge_block(): jnp.einsum('rqhd,rhdk->rhqk', query_set, key_rows, preferred_element_type...  9.57 us
    reduce_scatter x1, waiting for transfers between devices, shards(): lax.psum_scatter(conv_part.astype(jnp.bfloat16), 'head', scatter_dimensio...  8.03 us
    reduce_scatter x1, waiting for transfers between devices, shards(): lax.psum_scatter(partial_value.astype(jnp.bfloat16), 'head', scatter_dime...  5.76 us
    dot_general x1, matrix products, shards(): jnp.einsum('rsc,cd->rsd', hidden, conv_out, preferred_element_type=jnp.fl...  3.97 us
    reduce_sum x2, other arithmetic, merge_block(): denominator = denominator * factor + jnp.sum(expo, axis=-1)  3.65 us
    ppermute x1, starting transfers between devices, with_halo(): lax.ppermute(lax.slice_in_dim(block, block.shape[dim] - width, None, axis...  3.59 us
  transfers between devices with their start and end apart: 5, of which 4 were waited for; matrix products, arithmetic and copies ran while one was open for 3% of the time, Pallas kernels for 0%

commit v1 on v0

v1 whole, which is shorter than its diff:
```python
import functools
import math

import jax
import jax.numpy as jnp
from jax import lax
from jax.experimental import pallas as pl
from jax.experimental.pallas import tpu as pltpu
from jax.sharding import PartitionSpec as P

QDIM = 32
VDIM = 12
NEG = -1e30
F32 = jnp.float32
BF16 = jnp.bfloat16
VM = pl.BlockSpec(memory_space=pltpu.VMEM)
SM = pl.BlockSpec(memory_space=pltpu.SMEM)
HB = pl.BlockSpec(memory_space=pl.ANY)
NT = (((1,), (1,)), ((), ()))
TN = (((0,), (0,)), ((), ()))


def in_vmem(array):
    return pltpu.with_memory_space_constraint(array, pltpu.VMEM)


def call(kernel, outs, operands, specs, name, scratch=(), flops=0, moved=0, exps=0):
    out_specs = [VM] * len(outs)
    operands = [in_vmem(a) if s is VM else a for a, s in zip(operands, specs)]
    return pl.pallas_call(
        kernel,
        out_shape=outs,
        in_specs=specs,
        out_specs=out_specs,
        scratch_shapes=list(scratch),
        name=name,
        cost_estimate=pl.CostEstimate(flops=flops, bytes_accessed=moved, transcendentals=exps),
    )(*operands)


def dot(a, b, dims=None):
    if dims is None:
        return jnp.dot(a, b, preferred_element_type=F32)
    return lax.dot_general(a, b, dims, preferred_element_type=F32)


def halves(channels):
    here = lax.axis_index("head")
    mine = pl.ds(pl.multiple_of(here * channels, channels), channels)
    theirs = pl.ds(pl.multiple_of((1 - here) * channels, channels), channels)
    return mine, theirs


def down_kernel(parts, len_ref, frames_ref, weights_ref, out_ref, info_ref, raw, wide, sems):
    frame_count, channels = raw.shape
    tiles = channels // 128
    step = frame_count // parts
    rows = step // 4
    copies = [
        pltpu.make_async_copy(
            frames_ref.at[pl.ds(i * step, step)], raw.at[pl.ds(i * step, step)], sems.at[i]
        )
        for i in range(parts)
    ]
    for copy in copies:
        copy.start()
    length = len_ref[0]
    live_rows = lax.shift_right_logical(length + 3, 2)
    which = lax.broadcasted_iota(jnp.int32, info_ref.shape, 0)
    info_ref[...] = jnp.where(which == 0, live_rows, length)
    first = lax.axis_index("tm") * frame_count
    for i in range(parts):
        copies[i].wait()
        base = first + i * step
        row = base + 4 * lax.broadcasted_iota(jnp.int32, (rows, 128), 0)
        for tile in range(tiles):
            lanes = slice(tile * 128, tile * 128 + 128)
            wide[tile, i * step : (i + 1) * step] = raw[i * step : (i + 1) * step, lanes].astype(F32)
            total = None
            for j in range(4):
                part = wide[tile, pl.ds(i * step + j, rows, stride=4), :]
                part = jnp.where(row + j < length, part, 0.0) * weights_ref[j : j + 1, lanes]
                total = part if total is None else total + part
            out_ref[i * rows : (i + 1) * rows, lanes] = total.astype(BF16)


def pack_rows(quarter, width):
    return quarter + width * ((quarter + 127) // 128)


def kv_kernel(halo, mine_ref, theirs_ref, wk_ref, wvt_ref, pack_ref, head_ref, tail_ref):
    quarter, channels = mine_ref.shape
    width = wvt_ref.shape[0]
    mine, theirs = halves(channels)
    a, b = mine_ref[...], theirs_ref[...]
    keys = dot(a, wk_ref[mine, :]) + dot(b, wk_ref[theirs, :])
    pack_ref[:quarter, :] = keys.astype(BF16)
    values_t = dot(wvt_ref[:, mine], a, NT) + dot(wvt_ref[:, theirs], b, NT)
    values_t = values_t.astype(BF16)
    at = quarter
    for lane in range(0, quarter, 128):
        size = min(128, quarter - lane)
        if size < 128:
            pack_ref[at : at + width, :] = jnp.zeros((width, 128), BF16)
        pack_ref[at : at + width, :size] = values_t[:, lane : lane + size]
        at += width
    head_ref[:, :channels] = mine_ref[:halo, :]
    head_ref[:, channels:] = theirs_ref[:halo, :]
    tail_ref[:, :channels] = mine_ref[quarter - halo :, :]
    tail_ref[:, channels:] = theirs_ref[quarter - halo :, :]


def head_query(q_t, head):
    at = lax.broadcasted_iota(jnp.int32, q_t.shape, 0) // QDIM
    return jnp.where(at == head, q_t, 0.0).astype(BF16)


def head_values(pack, quarter, heads, head):
    width = heads * VDIM
    pieces = []
    at = quarter
    for lane in range(0, quarter, 128):
        size = min(128, quarter - lane)
        pieces.append(pack[at : at + width, :size].astype(F32))
        at += width
    values_t = jnp.concatenate(pieces, axis=1)
    row = lax.broadcasted_iota(jnp.int32, (width, quarter), 0)
    low, high = head * VDIM, (head + 1) * VDIM
    kept = jnp.where((row >= low) & (row < high), values_t, 0.0).astype(BF16)
    extra = lax.broadcasted_iota(jnp.int32, (16, quarter), 0)
    ones = jnp.where(extra == head, 1.0, 0.0).astype(BF16)
    return jnp.concatenate([kept, ones], axis=0)


def spread(rows, shape, heads):
    at = lax.broadcasted_iota(jnp.int32, shape, 0)
    out = jnp.broadcast_to(rows[0], shape)
    for head in range(1, heads):
        ours = (at >= head * VDIM) & (at < (head + 1) * VDIM) | (at == heads * VDIM + head)
        out = jnp.where(ours, jnp.broadcast_to(rows[head], shape), out)
    return out


def absorb(q_t, packs, sources, live_rows, quarter, heads, before, score_ref):
    queries = q_t.shape[1]
    row = lax.broadcasted_iota(jnp.int32, (quarter, queries), 0)
    tops, factors, total = [], [], None
    for head in range(heads):
        query = head_query(q_t, head)
        top = None if before is None else before[0][head]
        for i, (pack, source) in enumerate(zip(packs, sources)):
            scores = dot(pack[:quarter, :], query)
            scores = jnp.where(row < live_rows - source * quarter, scores, NEG)
            score_ref[i * quarter : (i + 1) * quarter, :] = scores
            best = jnp.max(scores, axis=0, keepdims=True)
            top = best if top is None else jnp.maximum(top, best)
        for i, pack in enumerate(packs):
            expo = jnp.exp2(score_ref[i * quarter : (i + 1) * quarter, :] - top).astype(BF16)
            part = dot(head_values(pack, quarter, heads, head), expo)
            total = part if total is None else total + part
        if before is not None:
            factors.append(jnp.exp2(before[0][head] - top))
        tops.append(top)
    if before is not None:
        total = total + before[1] * spread(factors, total.shape, heads)
    return tops, total


def finish(total, heads):
    width = heads * VDIM
    down = [total[width + head : width + head + 1, :] for head in range(heads)]
    return total[:width, :] / spread(down, (width, total.shape[1]), heads)


def open_kernel(heads, shifts, last, info_ref, mine_ref, theirs_ref, left_ref, right_ref, wq_ref, *rest):
    packs = rest[: len(shifts)]
    rows_ref, qt_ref, top_ref, sum_ref, score_ref = rest[len(shifts) :]
    quarter, channels = mine_ref.shape
    halo = left_ref.shape[0]
    queries = rows_ref.shape[0]
    rows_ref[:halo, :] = left_ref[...]
    rows_ref[halo : halo + quarter, :channels] = mine_ref[...]
    rows_ref[halo : halo + quarter, channels:] = theirs_ref[...]
    rows_ref[halo + quarter : 2 * halo + quarter, :] = right_ref[...]
    rows_ref[2 * halo + quarter :, :] = jnp.zeros((queries - 2 * halo - quarter, 2 * channels), BF16)
    mine, theirs = halves(channels)
    query = dot(rows_ref[:, :channels], wq_ref[mine, :]) + dot(rows_ref[:, channels:], wq_ref[theirs, :])
    q_t = jnp.transpose(query * (math.log2(math.e) / math.sqrt(QDIM)))
    qt_ref[...] = q_t
    here = lax.axis_index("tm")
    count = lax.axis_size("tm")
    sources = [lax.rem(here + shift + count, count) for shift in shifts]
    tops, total = absorb(
        q_t, packs, sources, info_ref[0:1, 0:1], quarter, heads, None, score_ref
    )
    for head in range(heads):
        top_ref[head : head + 1, :] = tops[head]
    sum_ref[...] = total


def more_kernel(heads, shifts, last, info_ref, qt_ref, top_in_ref, sum_in_ref, *rest):
    packs = rest[: len(shifts)]
    outs = rest[len(shifts) : -1]
    score_ref = rest[-1]
    quarter = score_ref.shape[0] // len(shifts)
    here = lax.axis_index("tm")
    count = lax.axis_size("tm")
    sources = [lax.rem(here + shift + count, count) for shift in shifts]
    before = ([top_in_ref[head : head + 1, :] for head in range(heads)], sum_in_ref[...])
    tops, total = absorb(
        qt_ref[...], packs, sources, info_ref[0:1, 0:1], quarter, heads, before, score_ref
    )
    if last:
        outs[0][...] = finish(total, heads).astype(BF16)
    else:
        for head in range(heads):
            outs[0][head : head + 1, :] = tops[head]
        outs[1][...] = total


def conv_kernel(
    halo, info_ref, rows_ref, mine_att_ref, their_att_ref, mine_out_ref, their_out_ref, conv_in_ref,
    taps_ref, after_ref, hidden_ref, gated,
):
    quarter, channels = hidden_ref.shape
    taps = taps_ref.shape[0]
    count = quarter + 2 * halo
    mine, theirs = halves(channels)
    attended = jnp.concatenate([mine_att_ref[...], their_att_ref[...]], axis=0)
    sides = []
    for side, lanes in ((mine, slice(0, channels)), (theirs, slice(channels, 2 * channels))):
        w_out = jnp.concatenate([mine_out_ref[:, side], their_out_ref[:, side]], axis=0)
        delta = dot(attended, w_out, TN)
        sides.append((rows_ref[:, lanes].astype(F32) + delta).astype(BF16)[:count])
    after_ref[...] = sides[0][halo : halo + quarter]
    gates = dot(sides[0], conv_in_ref[mine, :]) + dot(sides[1], conv_in_ref[theirs, :])
    value, gate = gates[:, :channels], gates[:, channels:]
    row = lax.broadcasted_iota(jnp.int32, (count, channels), 0)
    row = row + (lax.axis_index("tm") * quarter - halo)
    live = (row >= 0) & (row < info_ref[0:1, 0:1])
    mixed = jnp.where(live, value * jax.nn.sigmoid(gate), 0.0).astype(BF16).astype(F32)
    for tile in range(channels // 128):
        gated[tile] = mixed[:, tile * 128 : (tile + 1) * 128]
    block = 64
    start = halo - taps // 2
    for tile in range(channels // 128):
        lanes = slice(tile * 128, tile * 128 + 128)
        for base in range(0, quarter, block):
            total = None
            for k in range(taps):
                part = gated[tile, base + k + start : base + k + start + block, :] * taps_ref[k : k + 1, lanes]
                total = part if total is None else total + part
            hidden_ref[base : base + block, lanes] = (total * jax.nn.sigmoid(total)).astype(BF16)


def half_kernel(after_ref, hidden_ref, out_w_ref, base_ref):
    channels = hidden_ref.shape[1]
    mine, _ = halves(channels)
    base_ref[...] = after_ref[...].astype(F32) + dot(hidden_ref[...], out_w_ref[:, mine])


def last_kernel(info_ref, base_ref, hidden_ref, out_w_ref, frames_ref, bypass_ref, out_ref, tall):
    quarter, channels = base_ref.shape
    frame_count = frames_ref.shape[0]
    mine, _ = halves(channels)
    stacked = base_ref[...] + dot(hidden_ref[...], out_w_ref[:, mine])
    length = info_ref[1:2, 0:1]
    at = lax.broadcasted_iota(jnp.int32, (frame_count, 128), 0) + lax.axis_index("tm") * frame_count
    live = at < length
    for tile in range(channels // 128):
        lanes = slice(tile * 128, tile * 128 + 128)
        for j in range(4):
            tall[tile, pl.ds(j, quarter, stride=4), :] = stacked[:, lanes]
        backdrop = frames_ref[:, lanes].astype(F32)
        result = backdrop + bypass_ref[:, lanes] * (tall[tile] - backdrop)
        out_ref[:, lanes] = jnp.where(live, result, 0.0).astype(BF16)


def shards(
    frames,
    lengths,
    down_weights,
    w_query,
    w_key,
    w_value,
    w_out,
    conv_in,
    conv_taps,
    conv_out,
    bypass,
):
    records, frame_count, channels = frames.shape
    quarter = frame_count // 4
    heads = w_query.shape[1] // QDIM
    keys_wide = w_query.shape[1]
    count = lax.axis_size("tm")
    halo = -(-(conv_taps.shape[0] // 2) // 16) * 16
    queries = -(-(quarter + 2 * halo) // 128) * 128
    frames = frames.reshape(frame_count, channels)
    swap = [(0, 1), (1, 0)]

    def ring(array, by):
        return lax.ppermute(array, "tm", [(i, (i + by) % count) for i in range(count)])

    def vmem(shape, dtype):
        return pltpu.VMEM(shape, dtype)

    reduced, info = call(
        functools.partial(down_kernel, 4),
        [vmem((quarter, channels), BF16), vmem((8, 128), jnp.int32)],
        [lengths, frames, down_weights],
        [SM, HB, VM],
        "down",
        [
            pltpu.VMEM((frame_count, channels), BF16),
            pltpu.VMEM((channels // 128, frame_count, 128), F32),
            pltpu.SemaphoreType.DMA((4,)),
        ],
        flops=8 * frame_count * channels,
        moved=3 * frame_count * channels,
    )
    theirs = lax.ppermute(reduced, "head", swap)
    pack, head_rows, tail_rows = call(
        functools.partial(kv_kernel, halo),
        [
            vmem((pack_rows(quarter, heads * VDIM), keys_wide), BF16),
            vmem((halo, 2 * channels), BF16),
            vmem((halo, 2 * channels), BF16),
        ],
        [reduced, theirs, w_key, w_value.T],
        [VM] * 4,
        "keys_values",
        flops=4 * quarter * channels * (keys_wide + heads * VDIM),
        moved=8 * quarter * channels,
    )
    right = [pack]
    left = [pack]
    steps_right, steps_left = count // 2, (count - 1) // 2
    if steps_right:
        right.append(ring(pack, 1))
    if steps_left:
        left.append(ring(pack, -1))
    left_rows = ring(tail_rows, 1)
    right_rows = ring(head_rows, -1)
    for step in range(2, steps_right + 1):
        right.append(ring(right[-1], 1))
    for step in range(2, steps_left + 1):
        left.append(ring(left[-1], -1))
    their_w_out = lax.ppermute(w_out, "head", swap)
    their_conv_out = lax.ppermute(conv_out, "head", swap)

    stages = [[(0, pack)]]
    for step in range(1, steps_right + 1):
        stage = [(-step, right[step])]
        if step <= steps_left:
            stage.append((step, left[step]))
        stages.append(stage)
    if len(stages) > 1:
        stages = [stages[0] + stages[1]] + stages[2:]
    score_flops = 2 * quarter * queries * heads * (128 + 64)

    first = stages[0]
    rows, q_t, top, total = call(
        functools.partial(open_kernel, heads, [shift for shift, _ in first], False),
        [
            vmem((queries, 2 * channels), BF16),
            vmem((keys_wide, queries), F32),
            vmem((8, queries), F32),
            vmem((heads * VDIM + 16, queries), F32),
        ],
        [info, reduced, theirs, left_rows, right_rows, w_query] + [array for _, array in first],
        [VM] * (6 + len(first)),
        "attend_first",
        [pltpu.VMEM((len(first) * quarter, queries), F32)],
        flops=score_flops * len(first),
        moved=quarter * queries * 4,
        exps=quarter * queries * heads * len(first),
    )
    for index, stage in enumerate(stages[1:]):
        last = index == len(stages) - 2
        outs = [vmem((8, queries), F32), vmem((heads * VDIM + 16, queries), F32)]
        if last:
            outs = [vmem((heads * VDIM, queries), BF16)]
        state = call(
            functools.partial(more_kernel, heads, [shift for shift, _ in stage], last),
            outs,
            [info, q_t, top, total] + [array for _, array in stage],
            [VM] * (4 + len(stage)),
            "attend_more",
            [pltpu.VMEM((len(stage) * quarter, queries), F32)],
            flops=score_flops * len(stage),
            moved=quarter * queries * 4,
            exps=quarter * queries * heads * len(stage),
        )
        if last:
            attended = state[0]
        else:
            top, total = state
    their_attended = lax.ppermute(attended, "head", swap)
    after, hidden = call(
        functools.partial(conv_kernel, halo),
        [vmem((quarter, channels), BF16), vmem((quarter, channels), BF16)],
        [
            info, rows, attended, their_attended, w_out, their_w_out,
            conv_in.reshape(2 * channels, 2 * channels), conv_taps,
        ],
        [VM] * 8,
        "gate_conv",
        [pltpu.VMEM((channels // 128, quarter + 2 * halo, 128), F32)],
        flops=2 * queries * 2 * channels * (96 + 2 * channels),
        moved=quarter * channels * 8,
    )
    their_hidden = lax.ppermute(hidden, "head", swap)
    (base,) = call(
        half_kernel,
        [vmem((quarter, channels), F32)],
        [after, hidden, conv_out],
        [VM] * 3,
        "half_out",
        flops=2 * quarter * channels * channels,
        moved=quarter * channels * 4,
    )
    (out,) = call(
        last_kernel,
        [jax.ShapeDtypeStruct((frame_count, channels), BF16)],
        [info, base, their_hidden, their_conv_out, frames, bypass.reshape(1, channels)],
        [VM] * 6,
        "bypass",
        [pltpu.VMEM((channels // 128, frame_count, 128), F32)],
        flops=2 * quarter * channels * channels,
        moved=frame_count * channels * 4,
    )
    return out.reshape(records, frame_count, channels)


def solution(mesh):
    in_specs = (
        P(("groups", "dp"), "tm", "head"),
        P(("groups", "dp")),
        P(None, "head"),
        P(None, "head"),
        P(None, "head"),
        P(None, "head"),
        P("head", None),
        P(None, None, "head"),
        P(None, "head"),
        P("head", None),
        P("head"),
    )
    out_specs = P(("groups", "dp"), "tm", "head")
    return jax.shard_map(shards, mesh=mesh, in_specs=in_specs, out_specs=out_specs, check_vma=False)
```

time: 136 us -> 37.5 us (0.28)
  waiting for transfers between devices: 59 us -> 10.6 us
  matrix products: 29.4 us -> 0 us
  Pallas kernels: 0 us -> 13.8 us
  between operations: 14.1 us -> 0.77 us
  other arithmetic: 12.3 us -> 0 us
  local copies, waits for them, and re-layouts: 11 us -> 1.33 us
  starting transfers between devices: 4.96 us -> 10.7 us
  blocking collectives: 4.64 us -> 0 us
    all_gather x1 -> x0, waiting for transfers between devices: 41.9 us -> none  [shards(): segment = lax.all_gather(full_rows, 'tm', axis=1, tiled=True)]
    dot_general x10 -> x0, matrix products: 29.4 us -> none  [the longest x2 10.1 us: merge_block(): jnp.einsum('rhqk,rhvk->rhqv', expo.astype(jnp.bfloat16), value_rows, pref...]
    pallas_call x0 -> x7, Pallas kernels: none -> 13.8 us  [call(): pl.pallas_call(kernel, out_shape=outs, in_specs=specs, out_specs=out_spec...]
    reduce_scatter x2 -> x0, waiting for transfers between devices: 13.8 us -> none  [the longest x1 8.03 us: shards(): lax.psum_scatter(conv_part.astype(jnp.bfloat16), 'head', scatter_dimensio...]
    ppermute x2 -> x10, waiting for transfers between devices: 3.26 us -> 10.6 us  [the longest x5 8.67 us: ring(): lax.ppermute(array, 'tm', [(i, (i + by) % count) for i in range(count)])]
    convert_element_type x5 -> x0, other arithmetic: 6.21 us -> none  [the longest x1 2.74 us: shards(): grouped = masked.reshape(records, quarter, 4, channels).astype(jnp.float32)]
    ppermute x2 -> x10, starting transfers between devices: 4.88 us -> 10.7 us  [the longest x5 9.35 us: ring(): lax.ppermute(array, 'tm', [(i, (i + by) % count) for i in range(count)])]
    reduce_sum x3 -> x0, other arithmetic: 4.95 us -> none  [the longest x2 3.65 us: merge_block(): denominator = denominator * factor + jnp.sum(expo, axis=-1)]
  transfers between devices with their start and end apart: 5 -> 10, of which waited for: 4 -> 6; matrix products, arithmetic and copies ran while one was open for 3% -> 0% of each run, Pallas kernels for 0% -> 25%
where the time goes in v1:
time: 37.5 us; the launch traced here: 37.2 us
  Pallas kernels  13.8 us (37%)
  starting transfers between devices  10.7 us (29%)
  waiting for transfers between devices  10.6 us (28%)
  local copies, waits for them, and re-layouts  1.33 us (4%)
  between operations  0.77 us (2%)
    pallas_call x7, Pallas kernels, call(): pl.pallas_call(kernel, out_shape=outs, in_specs=specs, out_specs=out_spec...  13.8 us
    ppermute x5, starting transfers between devices, ring(): lax.ppermute(array, 'tm', [(i, (i + by) % count) for i in range(count)])  9.35 us
    ppermute x5, waiting for transfers between devices, ring(): lax.ppermute(array, 'tm', [(i, (i + by) % count) for i in range(count)])  8.67 us
    unnamed x19, local copies, waits for them, and re-layouts  1.33 us
    ppermute x1, waiting for transfers between devices, shards(): theirs = lax.ppermute(reduced, 'head', swap)  1.12 us
  transfers between devices with their start and end apart: 10, of which 6 were waited for; matrix products, arithmetic and copies ran while one was open for 0% of the time, Pallas kernels for 25%

profile of v1, /device:TPU:0, one launch (start us, length us, event | category | flops | bytes accessed | tf_op | source)
XLA Modules:
  0.0 37.2 jit_solution(14333985181109303791)
XLA Ops:
  0.7 0.0 copy-start.5
  0.7 0.7 %copy-done.5 = f32[4,256]{1,0:T(4,128)S(1)} copy-done((f32[4,256]{1,0:T(4,128)S(1)}, f32[4,256]{1,0:T(4,128)}, u32[]{:S(2)}) %copy-start.5) | copy-done | bytes 4120
  1.3 0.0 copy-start.1
  1.3 0.0 copy-start.3
  1.3 1.5 %down.1 = (bf16[448,256]{1,0:T(8,128)(2,1)S(1)}, s32[8,128]{1,0:T(8,128)S(1)}) custom-call(s32[1]{0:T(128)S(6)} %copy.13.len_ref, bf16[1792,256]{1,0:T(8,128)(2,1)} %bitcast.6, f32[4,256]{1,0:T(4,128)S(1)} %copy-done.5), custom_call_target="tpu_custom_call" | custom-call | flops 3670016 | bytes 1376256 | tf_op jit(solution)/shard_map/down/pallas_call | solution.py:30
  2.8 0.6 %collective-permute-start = (bf16[448,256]{1,0:T(8,128)(2,1)S(1)}, bf16[448,256]{1,0:T(8,128)(2,1)S(1)}, u32[]{:S(2)}, u32[]{:S(2)}) collective-permute-start(bf16[448,256]{1,0:T(8,128)(2,1)S(1)} %get-tuple-element.17.mine_ref), channel_id=1, source_target_pairs={{0,1},{1,0},{2,3},{3,2},{4,5},{5,4},{6,7},{7,6},{8,9},{9,8},{10,11... | collective-permute-start | bytes 688136 | tf_op jit(solution)/shard_map/ppermute | solution.py:322
  3.4 1.1 %collective-permute-done.theirs_ref = bf16[448,256]{1,0:T(8,128)(2,1)S(1)} collective-permute-done((bf16[448,256]{1,0:T(8,128)(2,1)S(1)}, bf16[448,256]{1,0:T(8,128)(2,1)S(1)}, u32[]{:S(2)}, u32[]{:S(2)}) %collective-permute-start) | collective-permute-done | bytes 229408 | tf_op jit(solution)/shard_map/ppermute | solution.py:322
  4.5 0.0 copy-done.1
  4.5 0.0 copy-done.3
  4.5 0.0 copy-start.2
  4.5 0.0 copy-start.7
  4.5 0.4 %keys_values.1 = (bf16[640,128]{1,0:T(8,128)(2,1)S(1)}, bf16[16,512]{1,0:T(8,128)(2,1)S(1)}, bf16[16,512]{1,0:T(8,128)(2,1)S(1)}) custom-call(bf16[448,256]{1,0:T(8,128)(2,1)S(1)} %get-tuple-element.17.mine_ref, bf16[448,256]{1,0:T(8,128)(2,1)S(1)} %collective-permute-done.theirs_ref, bf16[512,128]{1,0:T(8,128)(2,1)S(1)} %copy-done.1, ...), custom_call_target="tpu_custom_call" | custom-call | flops 80740352 | bytes 917504 | tf_op jit(solution)/shard_map/keys_values/pallas_call | solution.py:30
  4.9 3.0 %collective-permute-start.3 = (bf16[640,128]{1,0:T(8,128)(2,1)S(1)}, bf16[640,128]{1,0:T(8,128)(2,1)S(1)}, u32[]{:S(2)}, u32[]{:S(2)}) collective-permute-start(bf16[640,128]{1,0:T(8,128)(2,1)S(1)} %get-tuple-element.20.rest_0_), channel_id=1, source_target_pairs={{0,4},{4,8},{8,12},{12,0},{1,5},{5,9},{9,13},{13,1},{2,6},{6,10},{... | collective-permute-start | bytes 491528 | tf_op jit(solution)/shard_map/ppermute | solution.py:303
  7.9 2.1 %collective-permute-start.4 = (bf16[640,128]{1,0:T(8,128)(2,1)S(1)}, bf16[640,128]{1,0:T(8,128)(2,1)S(1)}, u32[]{:S(2)}, u32[]{:S(2)}) collective-permute-start(bf16[640,128]{1,0:T(8,128)(2,1)S(1)} %get-tuple-element.20.rest_0_), channel_id=1, source_target_pairs={{0,12},{4,0},{8,4},{12,8},{1,13},{5,1},{9,5},{13,9},{2,14},{6,2},{... | collective-permute-start | bytes 491528 | tf_op jit(solution)/shard_map/ppermute | solution.py:303
  10.0 5.0 %collective-permute-done.3.rest_1_ = bf16[640,128]{1,0:T(8,128)(2,1)S(1)} collective-permute-done((bf16[640,128]{1,0:T(8,128)(2,1)S(1)}, bf16[640,128]{1,0:T(8,128)(2,1)S(1)}, u32[]{:S(2)}, u32[]{:S(2)}) %collective-permute-start.3) | collective-permute-done | bytes 163872 | tf_op jit(solution)/shard_map/ppermute | solution.py:303
  15.0 0.0 collective-permute-start.5
  15.0 3.5 %collective-permute-start.1 = (bf16[16,512]{1,0:T(8,128)(2,1)S(1)}, bf16[16,512]{1,0:T(8,128)(2,1)S(1)}, u32[]{:S(2)}, u32[]{:S(2)}) collective-permute-start(bf16[16,512]{1,0:T(8,128)(2,1)S(1)} %get-tuple-element.18), channel_id=1, source_target_pairs={{0,4},{4,8},{8,12},{12,0},{1,5},{5,9},{9,13},{13,1},{2,6},{6,10},{... | collective-permute-start | bytes 49160 | tf_op jit(solution)/shard_map/ppermute | solution.py:303
  18.5 0.8 %collective-permute-start.2 = (bf16[16,512]{1,0:T(8,128)(2,1)S(1)}, bf16[16,512]{1,0:T(8,128)(2,1)S(1)}, u32[]{:S(2)}, u32[]{:S(2)}) collective-permute-start(bf16[16,512]{1,0:T(8,128)(2,1)S(1)} %get-tuple-element.19), channel_id=1, source_target_pairs={{0,12},{4,0},{8,4},{12,8},{1,13},{5,1},{9,5},{13,9},{2,14},{6,2},{... | collective-permute-start | bytes 49160 | tf_op jit(solution)/shard_map/ppermute | solution.py:303
  19.3 0.0 copy-done.2
  19.3 0.0 collective-permute-start.7
  19.3 3.5 %collective-permute-done.1.left_ref = bf16[16,512]{1,0:T(8,128)(2,1)S(1)} collective-permute-done((bf16[16,512]{1,0:T(8,128)(2,1)S(1)}, bf16[16,512]{1,0:T(8,128)(2,1)S(1)}, u32[]{:S(2)}, u32[]{:S(2)}) %collective-permute-start.1) | collective-permute-done | bytes 16416 | tf_op jit(solution)/shard_map/ppermute | solution.py:303
  22.8 0.1 collective-permute-done.2.right_ref
  22.9 0.0 collective-permute-done.4.rest_2_
  22.9 0.0 copy-done.7
  22.9 4.7 %attend_first.1 = (bf16[512,512]{1,0:T(8,128)(2,1)S(1)}, f32[128,512]{1,0:T(8,128)S(1)}, f32[8,512]{1,0:T(8,128)S(1)}, f32[64,512]{1,0:T(8,128)S(1)}) custom-call(s32[8,128]{1,0:T(8,128)S(1)} %get-tuple-element.16.info_ref, bf16[448,256]{1,0:T(8,128)(2,1)S(1)} %get-tuple-element.17.mine_ref, bf16[448,256]{1,0:T(8,128)(2,1)S(1)} %collective-permute-done.theirs_ref, ...), custom_call_target="tpu_custom_call" | custom-call | flops 1056964608 | bytes 917504 | tf_op jit(solution)/shard_map/attend_first/pallas_call | solution.py:30
  27.6 0.0 collective-permute-done.5.rest_0_
  27.6 0.0 copy-start.8
  27.6 1.8 %attend_more.1.mine_att_ref = bf16[48,512]{1,0:T(8,128)(2,1)S(1)} custom-call(s32[8,128]{1,0:T(8,128)S(1)} %get-tuple-element.16.info_ref, f32[128,512]{1,0:T(8,128)S(1)} %get-tuple-element.22.qt_ref, f32[8,512]{1,0:T(8,128)S(1)} %get-tuple-element.23.top_in_ref, f32[64,512]{1,0:T(8,128)S(1)} %get-tuple-element.24.sum_in_ref, ...), custom_call_target="tpu_custom_call" | custom-call | flops 352321536 | bytes 917504 | tf_op jit(solution)/shard_map/attend_more/pallas_call | solution.py:30
  29.4 0.1 collective-permute-start.6
  29.5 0.5 %collective-permute-start.9 = (bf16[256,512]{1,0:T(8,128)(2,1)}, bf16[256,512]{1,0:T(8,128)(2,1)}, u32[]{:S(2)}, u32[]{:S(2)}) collective-permute-start(bf16[256,512]{1,0:T(8,128)(2,1)} %out_w_ref.1), channel_id=1, source_target_pairs={{0,1},{1,0},{2,3},{3,2},{4,5},{5,4},{6,7},{7,6},{8,9},{9,8},{10,11... | collective-permute-start | bytes 786440 | tf_op jit(solution)/shard_map/ppermute | solution.py:350
  30.0 0.0 copy-done.8
  30.0 0.0 copy-start.4
  30.0 0.1 copy.12
  30.1 0.0 collective-permute-done.7.their_out_ref
  30.1 0.6 %collective-permute-done.6.their_att_ref = bf16[48,512]{1,0:T(8,128)(2,1)S(1)} collective-permute-done((bf16[48,512]{1,0:T(8,128)(2,1)S(1)}, bf16[48,512]{1,0:T(8,128)(2,1)S(1)}, u32[]{:S(2)}, u32[]{:S(2)}) %collective-permute-start.6) | collective-permute-done | bytes 49184 | tf_op jit(solution)/shard_map/ppermute | solution.py:399
  30.7 0.0 copy-done.4
  30.7 0.0 copy-start
  30.7 1.8 %gate_conv.1 = (bf16[448,256]{1,0:T(8,128)(2,1)S(1)}, bf16[448,256]{1,0:T(8,128)(2,1)S(1)}) custom-call(s32[8,128]{1,0:T(8,128)S(1)} %get-tuple-element.16.info_ref, bf16[512,512]{1,0:T(8,128)(2,1)S(1)} %get-tuple-element.21.rows_ref, bf16[48,512]{1,0:T(8,128)(2,1)S(1)} %attend_more.1.mine_att_ref, bf16[48,512]{1,0:T(8,128)(2,1)S(1)} %collective-permute-done.6.their_att_ref, ...), custom_call_target="tpu_custom_call" | custom-call | flops 318767104 | bytes 917504 | tf_op jit(solution)/shard_map/gate_conv/pallas_call | solution.py:30
  32.5 0.2 collective-permute-start.8
  32.7 1.2 %half_out.1.base_ref = f32[448,256]{1,0:T(8,128)S(1)} custom-call(bf16[448,256]{1,0:T(8,128)(2,1)S(1)} %get-tuple-element.25.after_ref, bf16[448,256]{1,0:T(8,128)(2,1)S(1)} %get-tuple-element.26.hidden_ref, bf16[256,512]{1,0:T(8,128)(2,1)} %out_w_ref.1), custom_call_target="tpu_custom_call" | custom-call | flops 58720256 | bytes 458752 | tf_op jit(solution)/shard_map/half_out/pallas_call | solution.py:30
  33.9 0.0 copy-start.6
  33.9 0.0 collective-permute-done.9.out_w_ref
  33.9 0.2 collective-permute-done.8.hidden_ref
  34.0 0.0 copy-done
  34.0 0.5 %copy-done.6 = f32[256]{0:T(256)S(1)} copy-done((f32[256]{0:T(256)S(1)}, f32[256]{0:T(256)}, u32[]{:S(2)}) %copy-start.6) | copy-done | bytes 1048
  34.5 2.6 %bypass.1 = bf16[1792,256]{1,0:T(8,128)(2,1)} custom-call(s32[8,128]{1,0:T(8,128)S(1)} %get-tuple-element.16.info_ref, f32[448,256]{1,0:T(8,128)S(1)} %half_out.1.base_ref, bf16[448,256]{1,0:T(8,128)(2,1)S(1)} %collective-permute-done.8.hidden_ref, bf16[256,512]{1,0:T(8,128)(2,1)} %collective-permute-done.9.out_w_ref, bf16[1792,256]{1,0:T(8,128)(2,1)S(1)} %bitcast.7, ...), custom_call_target="tpu_custom_call" | custom-call | flops 58720256 | bytes 1835008 | tf_op jit(solution)/shard_map/bypass/pallas_call | solution.py:30
Async XLA Ops:
  0.7 0.7 %copy-start.5 = (f32[4,256]{1,0:T(4,128)S(1)}, f32[4,256]{1,0:T(4,128)}, u32[]{:S(2)}) copy-start(f32[4,256]{1,0:T(4,128)} %weights_ref.1) | copy-start | bytes 12292
  1.3 3.2 %copy-start.1 = (bf16[512,128]{1,0:T(8,128)(2,1)S(1)}, bf16[512,128]{1,0:T(8,128)(2,1)}, u32[]{:S(2)}) copy-start(bf16[512,128]{1,0:T(8,128)(2,1)} %wk_ref.1) | copy-start | bytes 393220
  1.3 3.2 %copy-start.3 = (bf16[512,48]{0,1:T(8,128)(2,1)S(1)}, bf16[512,48]{0,1:T(8,128)(2,1)}, u32[]{:S(2)}) copy-start(bf16[512,48]{0,1:T(8,128)(2,1)} %param.16) | copy-start | bytes 147460
  2.8 1.7 %collective-permute-start = (bf16[448,256]{1,0:T(8,128)(2,1)S(1)}, bf16[448,256]{1,0:T(8,128)(2,1)S(1)}, u32[]{:S(2)}, u32[]{:S(2)}) collective-permute-start(bf16[448,256]{1,0:T(8,128)(2,1)S(1)} %get-tuple-element.17.mine_ref), channel_id=1, source_target_pairs={{0,1},{1,0},{2,3},{3,2},{4,5},{5,4},{6,7},{7,6},{8,9},{9,8},{10,11... | collective-permute-start | bytes 688136 | tf_op jit(solution)/shard_map/ppermute | solution.py:322
  4.5 14.8 %copy-start.2 = (bf16[48,512]{1,0:T(8,128)(2,1)S(1)}, bf16[48,512]{1,0:T(8,128)(2,1)}, u32[]{:S(2)}) copy-start(bf16[48,512]{1,0:T(8,128)(2,1)} %mine_out_ref.1) | copy-start | bytes 147460
  4.5 18.4 %copy-start.7 = (bf16[512,128]{1,0:T(8,128)(2,1)S(1)}, bf16[512,128]{1,0:T(8,128)(2,1)}, u32[]{:S(2)}) copy-start(bf16[512,128]{1,0:T(8,128)(2,1)} %wq_ref.1) | copy-start | bytes 393220
  4.9 10.1 %collective-permute-start.3 = (bf16[640,128]{1,0:T(8,128)(2,1)S(1)}, bf16[640,128]{1,0:T(8,128)(2,1)S(1)}, u32[]{:S(2)}, u32[]{:S(2)}) collective-permute-start(bf16[640,128]{1,0:T(8,128)(2,1)S(1)} %get-tuple-element.20.rest_0_), channel_id=1, source_target_pairs={{0,4},{4,8},{8,12},{12,0},{1,5},{5,9},{9,13},{13,1},{2,6},{6,10},{... | collective-permute-start | bytes 491528 | tf_op jit(solution)/shard_map/ppermute | solution.py:303
  7.9 15.0 %collective-permute-start.4 = (bf16[640,128]{1,0:T(8,128)(2,1)S(1)}, bf16[640,128]{1,0:T(8,128)(2,1)S(1)}, u32[]{:S(2)}, u32[]{:S(2)}) collective-permute-start(bf16[640,128]{1,0:T(8,128)(2,1)S(1)} %get-tuple-element.20.rest_0_), channel_id=1, source_target_pairs={{0,12},{4,0},{8,4},{12,8},{1,13},{5,1},{9,5},{13,9},{2,14},{6,2},{... | collective-permute-start | bytes 491528 | tf_op jit(solution)/shard_map/ppermute | solution.py:303
  15.0 12.6 %collective-permute-start.5 = (bf16[640,128]{1,0:T(8,128)(2,1)S(1)}, bf16[640,128]{1,0:T(8,128)(2,1)S(1)}, u32[]{:S(2)}, u32[]{:S(2)}) collective-permute-start(bf16[640,128]{1,0:T(8,128)(2,1)S(1)} %collective-permute-done.3.rest_1_), channel_id=1, source_target_pairs={{0,4},{4,8},{8,12},{12,0},{1,5},{5,9},{9,13},{13,1},{2,6},{6,10},{... | collective-permute-start | bytes 491528 | tf_op jit(solution)/shard_map/ppermute | solution.py:303
  15.0 7.8 %collective-permute-start.1 = (bf16[16,512]{1,0:T(8,128)(2,1)S(1)}, bf16[16,512]{1,0:T(8,128)(2,1)S(1)}, u32[]{:S(2)}, u32[]{:S(2)}) collective-permute-start(bf16[16,512]{1,0:T(8,128)(2,1)S(1)} %get-tuple-element.18), channel_id=1, source_target_pairs={{0,4},{4,8},{8,12},{12,0},{1,5},{5,9},{9,13},{13,1},{2,6},{6,10},{... | collective-permute-start | bytes 49160 | tf_op jit(solution)/shard_map/ppermute | solution.py:303
  18.5 4.4 %collective-permute-start.2 = (bf16[16,512]{1,0:T(8,128)(2,1)S(1)}, bf16[16,512]{1,0:T(8,128)(2,1)S(1)}, u32[]{:S(2)}, u32[]{:S(2)}) collective-permute-start(bf16[16,512]{1,0:T(8,128)(2,1)S(1)} %get-tuple-element.19), channel_id=1, source_target_pairs={{0,12},{4,0},{8,4},{12,8},{1,13},{5,1},{9,5},{13,9},{2,14},{6,2},{... | collective-permute-start | bytes 49160 | tf_op jit(solution)/shard_map/ppermute | solution.py:303
  19.3 10.8 %collective-permute-start.7 = (bf16[48,512]{1,0:T(8,128)(2,1)S(1)}, bf16[48,512]{1,0:T(8,128)(2,1)S(1)}, u32[]{:S(2)}, u32[]{:S(2)}) collective-permute-start(bf16[48,512]{1,0:T(8,128)(2,1)S(1)} %copy-done.2), channel_id=1, source_target_pairs={{0,1},{1,0},{2,3},{3,2},{4,5},{5,4},{6,7},{7,6},{8,9},{9,8},{10,11... | collective-permute-start | bytes 147464 | tf_op jit(solution)/shard_map/ppermute | solution.py:349
  27.6 2.4 %copy-start.8 = (bf16[512,2,256]{2,1,0:T(2,128)(2,1)S(1)}, bf16[512,2,256]{2,1,0:T(2,128)(2,1)}, u32[]{:S(2)}) copy-start(bf16[512,2,256]{2,1,0:T(2,128)(2,1)} %param.18) | copy-start | bytes 1572868
  29.4 1.3 %collective-permute-start.6 = (bf16[48,512]{1,0:T(8,128)(2,1)S(1)}, bf16[48,512]{1,0:T(8,128)(2,1)S(1)}, u32[]{:S(2)}, u32[]{:S(2)}) collective-permute-start(bf16[48,512]{1,0:T(8,128)(2,1)S(1)} %attend_more.1.mine_att_ref), channel_id=1, source_target_pairs={{0,1},{1,0},{2,3},{3,2},{4,5},{5,4},{6,7},{7,6},{8,9},{9,8},{10,11... | collective-permute-start | bytes 147464 | tf_op jit(solution)/shard_map/ppermute | solution.py:399
  29.5 4.4 %collective-permute-start.9 = (bf16[256,512]{1,0:T(8,128)(2,1)}, bf16[256,512]{1,0:T(8,128)(2,1)}, u32[]{:S(2)}, u32[]{:S(2)}) collective-permute-start(bf16[256,512]{1,0:T(8,128)(2,1)} %out_w_ref.1), channel_id=1, source_target_pairs={{0,1},{1,0},{2,3},{3,2},{4,5},{5,4},{6,7},{7,6},{8,9},{9,8},{10,11... | collective-permute-start | bytes 786440 | tf_op jit(solution)/shard_map/ppermute | solution.py:350
  30.0 0.8 %copy-start.4 = (f32[31,256]{1,0:T(8,128)S(1)}, f32[31,256]{1,0:T(8,128)}, u32[]{:S(2)}) copy-start(f32[31,256]{1,0:T(8,128)} %taps_ref.1) | copy-start | bytes 95236
  30.7 3.3 %copy-start = (bf16[1,1792,256]{2,1,0:T(8,128)(2,1)S(1)}, bf16[1,1792,256]{2,1,0:T(8,128)(2,1)}, u32[]{:S(2)}) copy-start(bf16[1,1792,256]{2,1,0:T(8,128)(2,1)} %param.11) | copy-start | bytes 2752516
  32.5 1.6 %collective-permute-start.8 = (bf16[448,256]{1,0:T(8,128)(2,1)S(1)}, bf16[448,256]{1,0:T(8,128)(2,1)S(1)}, u32[]{:S(2)}, u32[]{:S(2)}) collective-permute-start(bf16[448,256]{1,0:T(8,128)(2,1)S(1)} %get-tuple-element.26.hidden_ref), channel_id=1, source_target_pairs={{0,1},{1,0},{2,3},{3,2},{4,5},{5,4},{6,7},{7,6},{8,9},{9,8},{10,11... | collective-permute-start | bytes 688136 | tf_op jit(solution)/shard_map/ppermute | solution.py:413
  33.9 0.7 %copy-start.6 = (f32[256]{0:T(256)S(1)}, f32[256]{0:T(256)}, u32[]{:S(2)}) copy-start(f32[256]{0:T(256)} %param.21) | copy-start | bytes 3076

commit v2 on v1

--- a/solution.py
+++ b/solution.py
@@ -24,8 +24,8 @@
     return pltpu.with_memory_space_constraint(array, pltpu.VMEM)
 
 
-def call(kernel, outs, operands, specs, name, scratch=(), flops=0, moved=0, exps=0):
-    out_specs = [VM] * len(outs)
+def call(kernel, outs, operands, specs, name, scratch=(), out_specs=None, flops=0, moved=0, exps=0):
+    out_specs = out_specs or [VM] * len(outs)
     operands = [in_vmem(a) if s is VM else a for a, s in zip(operands, specs)]
     return pl.pallas_call(
         kernel,
@@ -51,7 +51,7 @@
     return mine, theirs
 
 
-def down_kernel(parts, len_ref, frames_ref, weights_ref, out_ref, info_ref, raw, wide, sems):
+def down_kernel(parts, len_ref, frames_ref, weights_hbm, out_ref, info_ref, raw, wide, weights_ref, sems):
     frame_count, channels = raw.shape
     tiles = channels // 128
     step = frame_count // parts
@@ -62,6 +62,8 @@
         )
         for i in range(parts)
     ]
+    weights_copy = pltpu.make_async_copy(weights_hbm, weights_ref, sems.at[parts])
+    weights_copy.start()
     for copy in copies:
         copy.start()
     length = len_ref[0]
@@ -69,6 +71,7 @@
     which = lax.broadcasted_iota(jnp.int32, info_ref.shape, 0)
     info_ref[...] = jnp.where(which == 0, live_rows, length)
     first = lax.axis_index("tm") * frame_count
+    weights_copy.wait()
     for i in range(parts):
         copies[i].wait()
         base = first + i * step
@@ -84,30 +87,41 @@
             out_ref[i * rows : (i + 1) * rows, lanes] = total.astype(BF16)
 
 
-def pack_rows(quarter, width):
+def kv_rows(quarter, width):
     return quarter + width * ((quarter + 127) // 128)
 
 
-def kv_kernel(halo, mine_ref, theirs_ref, wk_ref, wvt_ref, pack_ref, head_ref, tail_ref):
+def put_edge(pack_ref, at, halo, rows):
+    for i in range(rows.shape[1] // 128):
+        pack_ref[at + i * halo : at + (i + 1) * halo, :] = rows[:, i * 128 : (i + 1) * 128]
+    return at + halo * (rows.shape[1] // 128)
+
+
+def get_edge(pack_ref, at, halo, width):
+    pieces = [pack_ref[at + i * halo : at + (i + 1) * halo, :] for i in range(width // 128)]
+    return jnp.concatenate(pieces, axis=1)
+
+
+def kv_kernel(halo, mine_ref, theirs_ref, wk_ref, wvt_ref, right_ref, left_ref):
     quarter, channels = mine_ref.shape
     width = wvt_ref.shape[0]
     mine, theirs = halves(channels)
     a, b = mine_ref[...], theirs_ref[...]
     keys = dot(a, wk_ref[mine, :]) + dot(b, wk_ref[theirs, :])
-    pack_ref[:quarter, :] = keys.astype(BF16)
+    keys = keys.astype(BF16)
     values_t = dot(wvt_ref[:, mine], a, NT) + dot(wvt_ref[:, theirs], b, NT)
     values_t = values_t.astype(BF16)
-    at = quarter
-    for lane in range(0, quarter, 128):
-        size = min(128, quarter - lane)
-        if size < 128:
-            pack_ref[at : at + width, :] = jnp.zeros((width, 128), BF16)
-        pack_ref[at : at + width, :size] = values_t[:, lane : lane + size]
-        at += width
-    head_ref[:, :channels] = mine_ref[:halo, :]
-    head_ref[:, channels:] = theirs_ref[:halo, :]
-    tail_ref[:, :channels] = mine_ref[quarter - halo :, :]
-    tail_ref[:, channels:] = theirs_ref[quarter - halo :, :]
+    for pack_ref, edge in ((right_ref, slice(quarter - halo, quarter)), (left_ref, slice(0, halo))):
+        pack_ref[:quarter, :] = keys
+        at = quarter
+        for lane in range(0, quarter, 128):
+            size = min(128, quarter - lane)
+            if size < 128:
+                pack_ref[at : at + width, :] = jnp.zeros((width, 128), BF16)
+            pack_ref[at : at + width, :size] = values_t[:, lane : lane + size]
+            at += width
+        at = put_edge(pack_ref, at, halo, mine_ref[edge, :])
+        put_edge(pack_ref, at, halo, theirs_ref[edge, :])
 
 
 def head_query(q_t, head):
@@ -172,16 +186,16 @@
     return total[:width, :] / spread(down, (width, total.shape[1]), heads)
 
 
-def open_kernel(heads, shifts, last, info_ref, mine_ref, theirs_ref, left_ref, right_ref, wq_ref, *rest):
+def open_kernel(heads, halo, shifts, info_ref, mine_ref, theirs_ref, wq_ref, *rest):
     packs = rest[: len(shifts)]
     rows_ref, qt_ref, top_ref, sum_ref, score_ref = rest[len(shifts) :]
     quarter, channels = mine_ref.shape
-    halo = left_ref.shape[0]
+    edge = kv_rows(quarter, heads * VDIM)
     queries = rows_ref.shape[0]
-    rows_ref[:halo, :] = left_ref[...]
+    rows_ref[:halo, :] = get_edge(packs[1], edge, halo, 2 * channels)
     rows_ref[halo : halo + quarter, :channels] = mine_ref[...]
     rows_ref[halo : halo + quarter, channels:] = theirs_ref[...]
-    rows_ref[halo + quarter : 2 * halo + quarter, :] = right_ref[...]
+    rows_ref[halo + quarter : 2 * halo + quarter, :] = get_edge(packs[2], edge, halo, 2 * channels)
     rows_ref[2 * halo + quarter :, :] = jnp.zeros((queries - 2 * halo - quarter, 2 * channels), BF16)
     mine, theirs = halves(channels)
     query = dot(rows_ref[:, :channels], wq_ref[mine, :]) + dot(rows_ref[:, channels:], wq_ref[theirs, :])
@@ -259,21 +273,34 @@
     base_ref[...] = after_ref[...].astype(F32) + dot(hidden_ref[...], out_w_ref[:, mine])
 
 
-def last_kernel(info_ref, base_ref, hidden_ref, out_w_ref, frames_ref, bypass_ref, out_ref, tall):
+def last_kernel(
+    parts, info_ref, base_ref, hidden_ref, out_w_ref, frames_ref, bypass_ref, out_ref, tall, flat, sems
+):
     quarter, channels = base_ref.shape
-    frame_count = frames_ref.shape[0]
+    rows = quarter // parts
+    step = 4 * rows
     mine, _ = halves(channels)
-    stacked = base_ref[...] + dot(hidden_ref[...], out_w_ref[:, mine])
+    weights = out_w_ref[:, mine]
     length = info_ref[1:2, 0:1]
-    at = lax.broadcasted_iota(jnp.int32, (frame_count, 128), 0) + lax.axis_index("tm") * frame_count
-    live = at < length
-    for tile in range(channels // 128):
-        lanes = slice(tile * 128, tile * 128 + 128)
-        for j in range(4):
-            tall[tile, pl.ds(j, quarter, stride=4), :] = stacked[:, lanes]
-        backdrop = frames_ref[:, lanes].astype(F32)
-        result = backdrop + bypass_ref[:, lanes] * (tall[tile] - backdrop)
-        out_ref[:, lanes] = jnp.where(live, result, 0.0).astype(BF16)
+    row = lax.broadcasted_iota(jnp.int32, (step, 128), 0) + lax.axis_index("tm") * 4 * quarter
+    copies = []
+    for i in range(parts):
+        part = slice(i * rows, (i + 1) * rows)
+        span = slice(i * step, (i + 1) * step)
+        stacked = base_ref[part, :] + dot(hidden_ref[part, :], weights)
+        live = row + i * step < length
+        for tile in range(channels // 128):
+            lanes = slice(tile * 128, tile * 128 + 128)
+            for j in range(4):
+                tall[tile, pl.ds(i * step + j, rows, stride=4), :] = stacked[:, lanes]
+            backdrop = frames_ref[span, lanes].astype(F32)
+            result = backdrop + bypass_ref[:, lanes] * (tall[tile, span] - backdrop)
+            flat[span, lanes] = jnp.where(live, result, 0.0).astype(BF16)
+        window = pl.ds(i * step, step)
+        copies.append(pltpu.make_async_copy(flat.at[window], out_ref.at[window], sems.at[i]))
+        copies[-1].start()
+    for copy in copies:
+        copy.wait()
 
 
 def shards(
@@ -309,39 +336,31 @@
         functools.partial(down_kernel, 4),
         [vmem((quarter, channels), BF16), vmem((8, 128), jnp.int32)],
         [lengths, frames, down_weights],
-        [SM, HB, VM],
+        [SM, HB, HB],
         "down",
         [
             pltpu.VMEM((frame_count, channels), BF16),
             pltpu.VMEM((channels // 128, frame_count, 128), F32),
-            pltpu.SemaphoreType.DMA((4,)),
+            pltpu.VMEM(down_weights.shape, F32),
+            pltpu.SemaphoreType.DMA((5,)),
         ],
         flops=8 * frame_count * channels,
         moved=3 * frame_count * channels,
     )
     theirs = lax.ppermute(reduced, "head", swap)
-    pack, head_rows, tail_rows = call(
+    edge_rows = halo * 2 * channels // 128
+    to_right, to_left = call(
         functools.partial(kv_kernel, halo),
-        [
-            vmem((pack_rows(quarter, heads * VDIM), keys_wide), BF16),
-            vmem((halo, 2 * channels), BF16),
-            vmem((halo, 2 * channels), BF16),
-        ],
+        [vmem((kv_rows(quarter, heads * VDIM) + edge_rows, keys_wide), BF16)] * 2,
         [reduced, theirs, w_key, w_value.T],
         [VM] * 4,
         "keys_values",
         flops=4 * quarter * channels * (keys_wide + heads * VDIM),
         moved=8 * quarter * channels,
     )
-    right = [pack]
-    left = [pack]
+    right = [to_right, ring(to_right, 1)]
+    left = [to_left, ring(to_left, -1)]
     steps_right, steps_left = count // 2, (count - 1) // 2
-    if steps_right:
-        right.append(ring(pack, 1))
-    if steps_left:
-        left.append(ring(pack, -1))
-    left_rows = ring(tail_rows, 1)
-    right_rows = ring(head_rows, -1)
     for step in range(2, steps_right + 1):
         right.append(ring(right[-1], 1))
     for step in range(2, steps_left + 1):
@@ -349,27 +368,25 @@
     their_w_out = lax.ppermute(w_out, "head", swap)
     their_conv_out = lax.ppermute(conv_out, "head", swap)
 
-    stages = [[(0, pack)]]
-    for step in range(1, steps_right + 1):
+    stages = [[(0, to_right), (-1, right[1]), (1, left[1])]]
+    for step in range(2, steps_right + 1):
         stage = [(-step, right[step])]
         if step <= steps_left:
             stage.append((step, left[step]))
         stages.append(stage)
-    if len(stages) > 1:
-        stages = [stages[0] + stages[1]] + stages[2:]
     score_flops = 2 * quarter * queries * heads * (128 + 64)
 
     first = stages[0]
     rows, q_t, top, total = call(
-        functools.partial(open_kernel, heads, [shift for shift, _ in first], False),
+        functools.partial(open_kernel, heads, halo, [shift for shift, _ in first]),
         [
             vmem((queries, 2 * channels), BF16),
             vmem((keys_wide, queries), F32),
             vmem((8, queries), F32),
             vmem((heads * VDIM + 16, queries), F32),
         ],
-        [info, reduced, theirs, left_rows, right_rows, w_query] + [array for _, array in first],
-        [VM] * (6 + len(first)),
+        [info, reduced, theirs, w_query] + [array for _, array in first],
+        [VM] * (4 + len(first)),
         "attend_first",
         [pltpu.VMEM((len(first) * quarter, queries), F32)],
         flops=score_flops * len(first),
@@ -421,12 +438,17 @@
         moved=quarter * channels * 4,
     )
     (out,) = call(
-        last_kernel,
+        functools.partial(last_kernel, 4),
         [jax.ShapeDtypeStruct((frame_count, channels), BF16)],
         [info, base, their_hidden, their_conv_out, frames, bypass.reshape(1, channels)],
         [VM] * 6,
         "bypass",
-        [pltpu.VMEM((channels // 128, frame_count, 128), F32)],
+        [
+            pltpu.VMEM((channels // 128, frame_count, 128), F32),
+            pltpu.VMEM((frame_count, channels), BF16),
+            pltpu.SemaphoreType.DMA((4,)),
+        ],
+        out_specs=[HB],
         flops=2 * quarter * channels * channels,
         moved=frame_count * channels * 4,
     )

time: 37.5 us -> 32.5 us (0.87)
  starting transfers between devices: 10.7 us -> 6.4 us
  local copies, waits for them, and re-layouts: 1.33 us -> 0.65 us
    ppermute x5 -> x3, starting transfers between devices: 9.35 us -> 5.08 us  [ring(): lax.ppermute(array, 'tm', [(i, (i + by) % count) for i in range(count)])]
    unnamed x19 -> x17, local copies, waits for them, and re-layouts: 1.33 us -> 0.65 us
    ppermute x5 -> x3, waiting for transfers between devices: 8.67 us -> 8.74 us  [ring(): lax.ppermute(array, 'tm', [(i, (i + by) % count) for i in range(count)])]
  transfers between devices with their start and end apart: 10 -> 8, of which waited for: 6 -> 6; matrix products, arithmetic and copies ran while one was open for 0% -> 0% of each run, Pallas kernels for 25% -> 29%
where the time goes in v2:
time: 32.5 us; the launch traced here: 32.2 us
  Pallas kernels  13.8 us (42%)
  waiting for transfers between devices  10.6 us (33%)
  starting transfers between devices  6.4 us (20%)
  between operations  0.77 us (2%)
  local copies, waits for them, and re-layouts  0.65 us (2%)
    pallas_call x7, Pallas kernels, call(): pl.pallas_call(kernel, out_shape=outs, in_specs=specs, out_specs=out_spec...  13.8 us
    ppermute x3, waiting for transfers between devices, ring(): lax.ppermute(array, 'tm', [(i, (i + by) % count) for i in range(count)])  8.74 us
    ppermute x3, starting transfers between devices, ring(): lax.ppermute(array, 'tm', [(i, (i + by) % count) for i in range(count)])  5.08 us
    ppermute x1, waiting for transfers between devices, shards(): theirs = lax.ppermute(reduced, 'head', swap)  1.12 us
  transfers between devices with their start and end apart: 8, of which 6 were waited for; matrix products, arithmetic and copies ran while one was open for 0% of the time, Pallas kernels for 29%

profile of v2, /device:TPU:0, one launch (start us, length us, event | category | flops | bytes accessed | tf_op | source)
XLA Modules:
  0.0 32.2 jit_solution(11525509601338674090)
XLA Ops:
  0.7 0.0 copy-start.1
  0.7 0.0 copy-start.3
  0.7 1.5 %down.1 = (bf16[448,256]{1,0:T(8,128)(2,1)S(1)}, s32[8,128]{1,0:T(8,128)S(1)}) custom-call(s32[1]{0:T(128)S(6)} %copy.13.len_ref, bf16[1792,256]{1,0:T(8,128)(2,1)} %bitcast.6, f32[4,256]{1,0:T(4,128)} %weights_hbm.1), custom_call_target="tpu_custom_call" | custom-call | flops 3670016 | bytes 1376256 | tf_op jit(solution)/shard_map/down/pallas_call | solution.py:30
  2.2 0.6 %collective-permute-start = (bf16[448,256]{1,0:T(8,128)(2,1)S(1)}, bf16[448,256]{1,0:T(8,128)(2,1)S(1)}, u32[]{:S(2)}, u32[]{:S(2)}) collective-permute-start(bf16[448,256]{1,0:T(8,128)(2,1)S(1)} %get-tuple-element.16.mine_ref), channel_id=1, source_target_pairs={{0,1},{1,0},{2,3},{3,2},{4,5},{5,4},{6,7},{7,6},{8,9},{9,8},{10,11... | collective-permute-start | bytes 688136 | tf_op jit(solution)/shard_map/ppermute | solution.py:350
  2.7 1.1 %collective-permute-done.theirs_ref = bf16[448,256]{1,0:T(8,128)(2,1)S(1)} collective-permute-done((bf16[448,256]{1,0:T(8,128)(2,1)S(1)}, bf16[448,256]{1,0:T(8,128)(2,1)S(1)}, u32[]{:S(2)}, u32[]{:S(2)}) %collective-permute-start) | collective-permute-done | bytes 229408 | tf_op jit(solution)/shard_map/ppermute | solution.py:350
  3.9 0.0 copy-done.1
  3.9 0.0 copy-done.3
  3.9 0.0 copy-start.2
  3.9 0.0 copy-start.6
  3.9 0.4 %keys_values.1 = (bf16[704,128]{1,0:T(8,128)(2,1)S(1)}, bf16[704,128]{1,0:T(8,128)(2,1)S(1)}) custom-call(bf16[448,256]{1,0:T(8,128)(2,1)S(1)} %get-tuple-element.16.mine_ref, bf16[448,256]{1,0:T(8,128)(2,1)S(1)} %collective-permute-done.theirs_ref, bf16[512,128]{1,0:T(8,128)(2,1)S(1)} %copy-done.1, bf16[48,512]{1,0:T(8,128)(2,1)S(1)} %bitcast.9), custom_call_target="tpu_custom_call" | custom-call | flops 80740352 | bytes 917504 | tf_op jit(solution)/shard_map/keys_values/pallas_call | solution.py:30
  4.3 3.0 %collective-permute-start.1 = (bf16[704,128]{1,0:T(8,128)(2,1)S(1)}, bf16[704,128]{1,0:T(8,128)(2,1)S(1)}, u32[]{:S(2)}, u32[]{:S(2)}) collective-permute-start(bf16[704,128]{1,0:T(8,128)(2,1)S(1)} %get-tuple-element.17.rest_0_), channel_id=1, source_target_pairs={{0,4},{4,8},{8,12},{12,0},{1,5},{5,9},{9,13},{13,1},{2,6},{6,10},{... | collective-permute-start | bytes 540680 | tf_op jit(solution)/shard_map/ppermute | solution.py:330
  7.2 2.1 %collective-permute-start.2 = (bf16[704,128]{1,0:T(8,128)(2,1)S(1)}, bf16[704,128]{1,0:T(8,128)(2,1)S(1)}, u32[]{:S(2)}, u32[]{:S(2)}) collective-permute-start(bf16[704,128]{1,0:T(8,128)(2,1)S(1)} %get-tuple-element.18), channel_id=1, source_target_pairs={{0,12},{4,0},{8,4},{12,8},{1,13},{5,1},{9,5},{13,9},{2,14},{6,2},{... | collective-permute-start | bytes 540680 | tf_op jit(solution)/shard_map/ppermute | solution.py:330
  9.3 5.4 %collective-permute-done.1.rest_1_ = bf16[704,128]{1,0:T(8,128)(2,1)S(1)} collective-permute-done((bf16[704,128]{1,0:T(8,128)(2,1)S(1)}, bf16[704,128]{1,0:T(8,128)(2,1)S(1)}, u32[]{:S(2)}, u32[]{:S(2)}) %collective-permute-start.1) | collective-permute-done | bytes 180256 | tf_op jit(solution)/shard_map/ppermute | solution.py:330
  14.7 0.0 collective-permute-start.3
  14.7 0.0 copy-done.2
  14.7 0.0 collective-permute-start.5
  14.7 2.7 %collective-permute-done.2.rest_2_ = bf16[704,128]{1,0:T(8,128)(2,1)S(1)} collective-permute-done((bf16[704,128]{1,0:T(8,128)(2,1)S(1)}, bf16[704,128]{1,0:T(8,128)(2,1)S(1)}, u32[]{:S(2)}, u32[]{:S(2)}) %collective-permute-start.2) | collective-permute-done | bytes 180256 | tf_op jit(solution)/shard_map/ppermute | solution.py:330
  17.4 0.0 copy-done.6
  17.4 4.7 %attend_first.1 = (bf16[512,512]{1,0:T(8,128)(2,1)S(1)}, f32[128,512]{1,0:T(8,128)S(1)}, f32[8,512]{1,0:T(8,128)S(1)}, f32[64,512]{1,0:T(8,128)S(1)}) custom-call(s32[8,128]{1,0:T(8,128)S(1)} %get-tuple-element.15.info_ref, bf16[448,256]{1,0:T(8,128)(2,1)S(1)} %get-tuple-element.16.mine_ref, bf16[448,256]{1,0:T(8,128)(2,1)S(1)} %collective-permute-done.theirs_ref, ...), custom_call_target="tpu_custom_call" | custom-call | flops 1056964608 | bytes 917504 | tf_op jit(solution)/shard_map/attend_first/pallas_call | solution.py:30
  22.1 0.7 %collective-permute-done.3.rest_0_ = bf16[704,128]{1,0:T(8,128)(2,1)S(1)} collective-permute-done((bf16[704,128]{1,0:T(8,128)(2,1)S(1)}, bf16[704,128]{1,0:T(8,128)(2,1)S(1)}, u32[]{:S(2)}, u32[]{:S(2)}) %collective-permute-start.3) | collective-permute-done | bytes 180256 | tf_op jit(solution)/shard_map/ppermute | solution.py:330
  22.8 0.0 copy-start.7
  22.8 1.8 %attend_more.1.mine_att_ref = bf16[48,512]{1,0:T(8,128)(2,1)S(1)} custom-call(s32[8,128]{1,0:T(8,128)S(1)} %get-tuple-element.15.info_ref, f32[128,512]{1,0:T(8,128)S(1)} %get-tuple-element.20.qt_ref, f32[8,512]{1,0:T(8,128)S(1)} %get-tuple-element.21.top_in_ref, f32[64,512]{1,0:T(8,128)S(1)} %get-tuple-element.22.sum_in_ref, ...), custom_call_target="tpu_custom_call" | custom-call | flops 352321536 | bytes 917504 | tf_op jit(solution)/shard_map/attend_more/pallas_call | solution.py:30
  24.6 0.1 collective-permute-start.4
  24.6 0.5 %collective-permute-start.7 = (bf16[256,512]{1,0:T(8,128)(2,1)}, bf16[256,512]{1,0:T(8,128)(2,1)}, u32[]{:S(2)}, u32[]{:S(2)}) collective-permute-start(bf16[256,512]{1,0:T(8,128)(2,1)} %out_w_ref.1), channel_id=1, source_target_pairs={{0,1},{1,0},{2,3},{3,2},{4,5},{5,4},{6,7},{7,6},{8,9},{9,8},{10,11... | collective-permute-start | bytes 786440 | tf_op jit(solution)/shard_map/ppermute | solution.py:369
  25.1 0.0 copy-done.7
  25.1 0.0 copy-start.4
  25.1 0.1 copy.12
  25.2 0.0 collective-permute-done.5.their_out_ref
  25.2 0.6 %collective-permute-done.4.their_att_ref = bf16[48,512]{1,0:T(8,128)(2,1)S(1)} collective-permute-done((bf16[48,512]{1,0:T(8,128)(2,1)S(1)}, bf16[48,512]{1,0:T(8,128)(2,1)S(1)}, u32[]{:S(2)}, u32[]{:S(2)}) %collective-permute-start.4) | collective-permute-done | bytes 49184 | tf_op jit(solution)/shard_map/ppermute | solution.py:416
  25.9 0.0 copy-done.4
  25.9 0.0 copy-start
  25.9 1.8 %gate_conv.1 = (bf16[448,256]{1,0:T(8,128)(2,1)S(1)}, bf16[448,256]{1,0:T(8,128)(2,1)S(1)}) custom-call(s32[8,128]{1,0:T(8,128)S(1)} %get-tuple-element.15.info_ref, bf16[512,512]{1,0:T(8,128)(2,1)S(1)} %get-tuple-element.19.rows_ref, bf16[48,512]{1,0:T(8,128)(2,1)S(1)} %attend_more.1.mine_att_ref, bf16[48,512]{1,0:T(8,128)(2,1)S(1)} %collective-permute-done.4.their_att_ref, ...), custom_call_target="tpu_custom_call" | custom-call | flops 318767104 | bytes 917504 | tf_op jit(solution)/shard_map/gate_conv/pallas_call | solution.py:30
  27.7 0.2 collective-permute-start.6
  27.8 1.2 %half_out.1.base_ref = f32[448,256]{1,0:T(8,128)S(1)} custom-call(bf16[448,256]{1,0:T(8,128)(2,1)S(1)} %get-tuple-element.23.after_ref, bf16[448,256]{1,0:T(8,128)(2,1)S(1)} %get-tuple-element.24.hidden_ref, bf16[256,512]{1,0:T(8,128)(2,1)} %out_w_ref.1), custom_call_target="tpu_custom_call" | custom-call | flops 58720256 | bytes 458752 | tf_op jit(solution)/shard_map/half_out/pallas_call | solution.py:30
  29.0 0.0 copy-start.5
  29.0 0.0 collective-permute-done.7.out_w_ref
  29.1 0.2 collective-permute-done.6.hidden_ref
  29.2 0.0 copy-done
  29.2 0.5 %copy-done.5 = f32[256]{0:T(256)S(1)} copy-done((f32[256]{0:T(256)S(1)}, f32[256]{0:T(256)}, u32[]{:S(2)}) %copy-start.5) | copy-done | bytes 1048
  29.7 2.5 %bypass.1 = bf16[1792,256]{1,0:T(8,128)(2,1)} custom-call(s32[8,128]{1,0:T(8,128)S(1)} %get-tuple-element.15.info_ref, f32[448,256]{1,0:T(8,128)S(1)} %half_out.1.base_ref, bf16[448,256]{1,0:T(8,128)(2,1)S(1)} %collective-permute-done.6.hidden_ref, bf16[256,512]{1,0:T(8,128)(2,1)} %collective-permute-done.7.out_w_ref, bf16[1792,256]{1,0:T(8,128)(2,1)S(1)} %bitcast.7, ...), custom_call_target="tpu_custom_call" | custom-call | flops 58720256 | bytes 1835008 | tf_op jit(solution)/shard_map/bypass/pallas_call | solution.py:30
Async XLA Ops:
  0.7 3.2 %copy-start.1 = (bf16[512,128]{1,0:T(8,128)(2,1)S(1)}, bf16[512,128]{1,0:T(8,128)(2,1)}, u32[]{:S(2)}) copy-start(bf16[512,128]{1,0:T(8,128)(2,1)} %wk_ref.1) | copy-start | bytes 393220
  0.7 3.2 %copy-start.3 = (bf16[512,48]{0,1:T(8,128)(2,1)S(1)}, bf16[512,48]{0,1:T(8,128)(2,1)}, u32[]{:S(2)}) copy-start(bf16[512,48]{0,1:T(8,128)(2,1)} %param.16) | copy-start | bytes 147460
  2.2 1.7 %collective-permute-start = (bf16[448,256]{1,0:T(8,128)(2,1)S(1)}, bf16[448,256]{1,0:T(8,128)(2,1)S(1)}, u32[]{:S(2)}, u32[]{:S(2)}) collective-permute-start(bf16[448,256]{1,0:T(8,128)(2,1)S(1)} %get-tuple-element.16.mine_ref), channel_id=1, source_target_pairs={{0,1},{1,0},{2,3},{3,2},{4,5},{5,4},{6,7},{7,6},{8,9},{9,8},{10,11... | collective-permute-start | bytes 688136 | tf_op jit(solution)/shard_map/ppermute | solution.py:350
  3.9 10.9 %copy-start.2 = (bf16[48,512]{1,0:T(8,128)(2,1)S(1)}, bf16[48,512]{1,0:T(8,128)(2,1)}, u32[]{:S(2)}) copy-start(bf16[48,512]{1,0:T(8,128)(2,1)} %mine_out_ref.1) | copy-start | bytes 147460
  3.9 13.6 %copy-start.6 = (bf16[512,128]{1,0:T(8,128)(2,1)S(1)}, bf16[512,128]{1,0:T(8,128)(2,1)}, u32[]{:S(2)}) copy-start(bf16[512,128]{1,0:T(8,128)(2,1)} %wq_ref.1) | copy-start | bytes 393220
  4.3 10.5 %collective-permute-start.1 = (bf16[704,128]{1,0:T(8,128)(2,1)S(1)}, bf16[704,128]{1,0:T(8,128)(2,1)S(1)}, u32[]{:S(2)}, u32[]{:S(2)}) collective-permute-start(bf16[704,128]{1,0:T(8,128)(2,1)S(1)} %get-tuple-element.17.rest_0_), channel_id=1, source_target_pairs={{0,4},{4,8},{8,12},{12,0},{1,5},{5,9},{9,13},{13,1},{2,6},{6,10},{... | collective-permute-start | bytes 540680 | tf_op jit(solution)/shard_map/ppermute | solution.py:330
  7.2 10.2 %collective-permute-start.2 = (bf16[704,128]{1,0:T(8,128)(2,1)S(1)}, bf16[704,128]{1,0:T(8,128)(2,1)S(1)}, u32[]{:S(2)}, u32[]{:S(2)}) collective-permute-start(bf16[704,128]{1,0:T(8,128)(2,1)S(1)} %get-tuple-element.18), channel_id=1, source_target_pairs={{0,12},{4,0},{8,4},{12,8},{1,13},{5,1},{9,5},{13,9},{2,14},{6,2},{... | collective-permute-start | bytes 540680 | tf_op jit(solution)/shard_map/ppermute | solution.py:330
  14.7 8.1 %collective-permute-start.3 = (bf16[704,128]{1,0:T(8,128)(2,1)S(1)}, bf16[704,128]{1,0:T(8,128)(2,1)S(1)}, u32[]{:S(2)}, u32[]{:S(2)}) collective-permute-start(bf16[704,128]{1,0:T(8,128)(2,1)S(1)} %collective-permute-done.1.rest_1_), channel_id=1, source_target_pairs={{0,4},{4,8},{8,12},{12,0},{1,5},{5,9},{9,13},{13,1},{2,6},{6,10},{... | collective-permute-start | bytes 540680 | tf_op jit(solution)/shard_map/ppermute | solution.py:330
  14.7 10.5 %collective-permute-start.5 = (bf16[48,512]{1,0:T(8,128)(2,1)S(1)}, bf16[48,512]{1,0:T(8,128)(2,1)S(1)}, u32[]{:S(2)}, u32[]{:S(2)}) collective-permute-start(bf16[48,512]{1,0:T(8,128)(2,1)S(1)} %copy-done.2), channel_id=1, source_target_pairs={{0,1},{1,0},{2,3},{3,2},{4,5},{5,4},{6,7},{7,6},{8,9},{9,8},{10,11... | collective-permute-start | bytes 147464 | tf_op jit(solution)/shard_map/ppermute | solution.py:368
  22.8 2.4 %copy-start.7 = (bf16[512,2,256]{2,1,0:T(2,128)(2,1)S(1)}, bf16[512,2,256]{2,1,0:T(2,128)(2,1)}, u32[]{:S(2)}) copy-start(bf16[512,2,256]{2,1,0:T(2,128)(2,1)} %param.18) | copy-start | bytes 1572868
  24.6 1.3 %collective-permute-start.4 = (bf16[48,512]{1,0:T(8,128)(2,1)S(1)}, bf16[48,512]{1,0:T(8,128)(2,1)S(1)}, u32[]{:S(2)}, u32[]{:S(2)}) collective-permute-start(bf16[48,512]{1,0:T(8,128)(2,1)S(1)} %attend_more.1.mine_att_ref), channel_id=1, source_target_pairs={{0,1},{1,0},{2,3},{3,2},{4,5},{5,4},{6,7},{7,6},{8,9},{9,8},{10,11... | collective-permute-start | bytes 147464 | tf_op jit(solution)/shard_map/ppermute | solution.py:416
  24.6 4.4 %collective-permute-start.7 = (bf16[256,512]{1,0:T(8,128)(2,1)}, bf16[256,512]{1,0:T(8,128)(2,1)}, u32[]{:S(2)}, u32[]{:S(2)}) collective-permute-start(bf16[256,512]{1,0:T(8,128)(2,1)} %out_w_ref.1), channel_id=1, source_target_pairs={{0,1},{1,0},{2,3},{3,2},{4,5},{5,4},{6,7},{7,6},{8,9},{9,8},{10,11... | collective-permute-start | bytes 786440 | tf_op jit(solution)/shard_map/ppermute | solution.py:369
  25.1 0.8 %copy-start.4 = (f32[31,256]{1,0:T(8,128)S(1)}, f32[31,256]{1,0:T(8,128)}, u32[]{:S(2)}) copy-start(f32[31,256]{1,0:T(8,128)} %taps_ref.1) | copy-start | bytes 95236
  25.9 3.3 %copy-start = (bf16[1,1792,256]{2,1,0:T(8,128)(2,1)S(1)}, bf16[1,1792,256]{2,1,0:T(8,128)(2,1)}, u32[]{:S(2)}) copy-start(bf16[1,1792,256]{2,1,0:T(8,128)(2,1)} %param.11) | copy-start | bytes 2752516
  27.7 1.6 %collective-permute-start.6 = (bf16[448,256]{1,0:T(8,128)(2,1)S(1)}, bf16[448,256]{1,0:T(8,128)(2,1)S(1)}, u32[]{:S(2)}, u32[]{:S(2)}) collective-permute-start(bf16[448,256]{1,0:T(8,128)(2,1)S(1)} %get-tuple-element.24.hidden_ref), channel_id=1, source_target_pairs={{0,1},{1,0},{2,3},{3,2},{4,5},{5,4},{6,7},{7,6},{8,9},{9,8},{10,11... | collective-permute-start | bytes 688136 | tf_op jit(solution)/shard_map/ppermute | solution.py:430
  29.0 0.7 %copy-start.5 = (f32[256]{0:T(256)S(1)}, f32[256]{0:T(256)}, u32[]{:S(2)}) copy-start(f32[256]{0:T(256)} %param.21) | copy-start | bytes 3076

commit v3 on v2

--- a/solution.py
+++ b/solution.py
@@ -14,19 +14,21 @@
 F32 = jnp.float32
 BF16 = jnp.bfloat16
 VM = pl.BlockSpec(memory_space=pltpu.VMEM)
+HB = pl.BlockSpec(memory_space=pltpu.HBM)
 SM = pl.BlockSpec(memory_space=pltpu.SMEM)
-HB = pl.BlockSpec(memory_space=pl.ANY)
 NT = (((1,), (1,)), ((), ()))
 TN = (((0,), (0,)), ((), ()))
 
 
-def in_vmem(array):
-    return pltpu.with_memory_space_constraint(array, pltpu.VMEM)
+def placed(array, spec):
+    if spec is SM:
+        return array
+    return pltpu.with_memory_space_constraint(array, pltpu.VMEM if spec is VM else pltpu.HBM)
 
 
 def call(kernel, outs, operands, specs, name, scratch=(), out_specs=None, flops=0, moved=0, exps=0):
     out_specs = out_specs or [VM] * len(outs)
-    operands = [in_vmem(a) if s is VM else a for a, s in zip(operands, specs)]
+    operands = [placed(a, s) for a, s in zip(operands, specs)]
     return pl.pallas_call(
         kernel,
         out_shape=outs,
@@ -34,6 +36,7 @@
         out_specs=out_specs,
         scratch_shapes=list(scratch),
         name=name,
+        compiler_params=pltpu.CompilerParams(vmem_limit_bytes=24 * 2**20),
         cost_estimate=pl.CostEstimate(flops=flops, bytes_accessed=moved, transcendentals=exps),
     )(*operands)
 
@@ -124,23 +127,37 @@
         put_edge(pack_ref, at, halo, theirs_ref[edge, :])
 
 
-def head_query(q_t, head):
+def head_query(q_t, head, ones):
     at = lax.broadcasted_iota(jnp.int32, q_t.shape, 0) // QDIM
-    return jnp.where(at == head, q_t, 0.0).astype(BF16)
-
-
-def head_values(pack, quarter, heads, head):
-    width = heads * VDIM
+    return jnp.concatenate([jnp.where(at == head, q_t, 0.0).astype(BF16), ones], axis=0)
+
+
+def one_row(queries):
+    at = lax.broadcasted_iota(jnp.int32, (128, queries), 0)
+    return jnp.where(at == 0, 1.0, 0.0).astype(BF16)
+
+
+def masked_keys(pack, quarter, first_row, live_rows):
+    row = lax.broadcasted_iota(jnp.int32, (quarter, 128), 0) + first_row
+    lane = lax.broadcasted_iota(jnp.int32, (quarter, 128), 1)
+    bias = jnp.where((lane == 0) & (row >= live_rows), NEG, 0.0).astype(BF16)
+    return jnp.concatenate([pack[:quarter, :], bias], axis=1)
+
+
+def all_values(pack, quarter, width):
     pieces = []
     at = quarter
     for lane in range(0, quarter, 128):
         size = min(128, quarter - lane)
         pieces.append(pack[at : at + width, :size].astype(F32))
         at += width
-    values_t = jnp.concatenate(pieces, axis=1)
+    return jnp.concatenate(pieces, axis=1)
+
+
+def head_values(values_t, head):
+    width, quarter = values_t.shape
     row = lax.broadcasted_iota(jnp.int32, (width, quarter), 0)
-    low, high = head * VDIM, (head + 1) * VDIM
-    kept = jnp.where((row >= low) & (row < high), values_t, 0.0).astype(BF16)
+    kept = jnp.where((row >= head * VDIM) & (row < (head + 1) * VDIM), values_t, 0.0).astype(BF16)
     extra = lax.broadcasted_iota(jnp.int32, (16, quarter), 0)
     ones = jnp.where(extra == head, 1.0, 0.0).astype(BF16)
     return jnp.concatenate([kept, ones], axis=0)
@@ -150,45 +167,37 @@
     at = lax.broadcasted_iota(jnp.int32, shape, 0)
     out = jnp.broadcast_to(rows[0], shape)
     for head in range(1, heads):
-        ours = (at >= head * VDIM) & (at < (head + 1) * VDIM) | (at == heads * VDIM + head)
+        ours = (at >= head * VDIM) & (at < (head + 1) * VDIM)
         out = jnp.where(ours, jnp.broadcast_to(rows[head], shape), out)
     return out
 
 
-def absorb(q_t, packs, sources, live_rows, quarter, heads, before, score_ref):
-    queries = q_t.shape[1]
-    row = lax.broadcasted_iota(jnp.int32, (quarter, queries), 0)
-    tops, factors, total = [], [], None
-    for head in range(heads):
-        query = head_query(q_t, head)
-        top = None if before is None else before[0][head]
-        for i, (pack, source) in enumerate(zip(packs, sources)):
-            scores = dot(pack[:quarter, :], query)
-            scores = jnp.where(row < live_rows - source * quarter, scores, NEG)
-            score_ref[i * quarter : (i + 1) * quarter, :] = scores
-            best = jnp.max(scores, axis=0, keepdims=True)
-            top = best if top is None else jnp.maximum(top, best)
-        for i, pack in enumerate(packs):
-            expo = jnp.exp2(score_ref[i * quarter : (i + 1) * quarter, :] - top).astype(BF16)
-            part = dot(head_values(pack, quarter, heads, head), expo)
+def absorb(total, q_t, packs, sources, live_rows, quarter, heads):
+    ones = one_row(q_t.shape[1])
+    for pack, source in zip(packs, sources):
+        keys = masked_keys(pack, quarter, source * quarter, live_rows)
+        values_t = all_values(pack, quarter, heads * VDIM)
+        for head in range(heads):
+            expo = jnp.exp2(dot(keys, head_query(q_t, head, ones))).astype(BF16)
+            part = dot(head_values(values_t, head), expo)
             total = part if total is None else total + part
-        if before is not None:
-            factors.append(jnp.exp2(before[0][head] - top))
-        tops.append(top)
-    if before is not None:
-        total = total + before[1] * spread(factors, total.shape, heads)
-    return tops, total
+    return total
 
 
 def finish(total, heads):
     width = heads * VDIM
     down = [total[width + head : width + head + 1, :] for head in range(heads)]
-    return total[:width, :] / spread(down, (width, total.shape[1]), heads)
+    return (total[:width, :] / spread(down, (width, total.shape[1]), heads)).astype(BF16)
+
+
+def sources_of(shifts):
+    here, count = lax.axis_index("tm"), lax.axis_size("tm")
+    return [lax.rem(here + shift + count, count) for shift in shifts]
 
 
 def open_kernel(heads, halo, shifts, info_ref, mine_ref, theirs_ref, wq_ref, *rest):
     packs = rest[: len(shifts)]
-    rows_ref, qt_ref, top_ref, sum_ref, score_ref = rest[len(shifts) :]
+    rows_ref, qt_ref, sum_ref = rest[-3:]
     quarter, channels = mine_ref.shape
     edge = kv_rows(quarter, heads * VDIM)
     queries = rows_ref.shape[0]
@@ -201,35 +210,65 @@
     query = dot(rows_ref[:, :channels], wq_ref[mine, :]) + dot(rows_ref[:, channels:], wq_ref[theirs, :])
     q_t = jnp.transpose(query * (math.log2(math.e) / math.sqrt(QDIM)))
     qt_ref[...] = q_t
-    here = lax.axis_index("tm")
-    count = lax.axis_size("tm")
-    sources = [lax.rem(here + shift + count, count) for shift in shifts]
-    tops, total = absorb(
-        q_t, packs, sources, info_ref[0:1, 0:1], quarter, heads, None, score_ref
-    )
-    for head in range(heads):
-        top_ref[head : head + 1, :] = tops[head]
-    sum_ref[...] = total
-
-
-def more_kernel(heads, shifts, last, info_ref, qt_ref, top_in_ref, sum_in_ref, *rest):
+    sum_ref[...] = absorb(None, q_t, packs, sources_of(shifts), info_ref[0:1, 0:1], quarter, heads)
+
+
+def more_kernel(heads, quarter, shifts, info_ref, qt_ref, sum_in_ref, *rest):
     packs = rest[: len(shifts)]
-    outs = rest[len(shifts) : -1]
-    score_ref = rest[-1]
-    quarter = score_ref.shape[0] // len(shifts)
-    here = lax.axis_index("tm")
-    count = lax.axis_size("tm")
-    sources = [lax.rem(here + shift + count, count) for shift in shifts]
-    before = ([top_in_ref[head : head + 1, :] for head in range(heads)], sum_in_ref[...])
-    tops, total = absorb(
-        qt_ref[...], packs, sources, info_ref[0:1, 0:1], quarter, heads, before, score_ref
-    )
-    if last:
-        outs[0][...] = finish(total, heads).astype(BF16)
-    else:
-        for head in range(heads):
-            outs[0][head : head + 1, :] = tops[head]
-        outs[1][...] = total
+    sum_ref = rest[-1]
+    sum_ref[...] = absorb(
+        sum_in_ref[...], qt_ref[...], packs, sources_of(shifts), info_ref[0:1, 0:1], quarter, heads
+    )
+
+
+def close_kernel(heads, quarter, shifts, everything, info_ref, qt_ref, sum_in_ref, *rest):
+    packs = rest[: len(shifts) + len(everything)]
+    out_ref, held, total_ref = rest[-3:]
+    live_rows = info_ref[0:1, 0:1]
+    width = heads * VDIM
+    total = absorb(
+        sum_in_ref[...], qt_ref[...], packs[: len(shifts)], sources_of(shifts), live_rows, quarter, heads
+    )
+    out_ref[...] = finish(total, heads)
+    down = total[width : width + heads, :]
+    safe = jnp.where((down > 2.0**-60) & (down < 2.0**100), 0.0, 1.0)
+
+    @pl.when(jnp.max(safe) > 0.0)
+    def _():
+        count = lax.axis_size("tm")
+        for i, (pack, shift) in enumerate(zip(packs, list(shifts) + list(everything))):
+            held[i] = pack[...]
+        firsts = sources_of(list(shifts) + list(everything))
+        q_t = qt_ref[...]
+        ones = one_row(q_t.shape[1])
+        total_ref[...] = jnp.zeros_like(total_ref)
+
+        def first_row(i):
+            first = firsts[0]
+            for j in range(1, count):
+                first = jnp.where(i == j, firsts[j], first)
+            return first * quarter
+
+        def one_head(head, carry):
+            query = head_query(q_t, head, ones)
+
+            def scores(i):
+                return dot(masked_keys(held.at[i], quarter, first_row(i), live_rows), query)
+
+            def highest(i, top):
+                return jnp.maximum(top, jnp.max(scores(i), axis=0, keepdims=True))
+
+            top = lax.fori_loop(0, count, highest, jnp.full((1, q_t.shape[1]), NEG, F32))
+
+            def add(i, carry):
+                expo = jnp.exp2(scores(i) - top).astype(BF16)
+                total_ref[...] += dot(head_values(all_values(held.at[i], quarter, width), head), expo)
+                return carry
+
+            return lax.fori_loop(0, count, add, carry)
+
+        lax.fori_loop(0, heads, one_head, 0)
+        out_ref[...] = finish(total_ref[...], heads)
 
 
 def conv_kernel(
@@ -332,14 +371,17 @@
     def vmem(shape, dtype):
         return pltpu.VMEM(shape, dtype)
 
-    reduced, info = call(
+    reduced, info, kept_frames = call(
         functools.partial(down_kernel, 4),
-        [vmem((quarter, channels), BF16), vmem((8, 128), jnp.int32)],
+        [
+            vmem((quarter, channels), BF16),
+            vmem((8, 128), jnp.int32),
+            vmem((frame_count, channels), BF16),
+        ],
         [lengths, frames, down_weights],
         [SM, HB, HB],
         "down",
         [
-            pltpu.VMEM((frame_count, channels), BF16),
             pltpu.VMEM((channels // 128, frame_count, 128), F32),
             pltpu.VMEM(down_weights.shape, F32),
             pltpu.SemaphoreType.DMA((5,)),
@@ -367,6 +409,9 @@
         left.append(ring(left[-1], -1))
     their_w_out = lax.ppermute(w_out, "head", swap)
     their_conv_out = lax.ppermute(conv_out, "head", swap)
+    gate_weights = conv_in.reshape(2 * channels, 2 * channels)
+    weights_row = bypass.reshape(1, channels)
+    early = [their_w_out, their_conv_out, gate_weights, weights_row, conv_taps, w_out, conv_out]
 
     stages = [[(0, to_right), (-1, right[1]), (1, left[1])]]
     for step in range(2, steps_right + 1):
@@ -377,49 +422,54 @@
     score_flops = 2 * quarter * queries * heads * (128 + 64)
 
     first = stages[0]
-    rows, q_t, top, total = call(
+    width = heads * VDIM
+    rows, q_t, total = call(
         functools.partial(open_kernel, heads, halo, [shift for shift, _ in first]),
         [
             vmem((queries, 2 * channels), BF16),
             vmem((keys_wide, queries), F32),
-            vmem((8, queries), F32),
-            vmem((heads * VDIM + 16, queries), F32),
+            vmem((width + 16, queries), F32),
         ],
-        [info, reduced, theirs, w_query] + [array for _, array in first],
-        [VM] * (4 + len(first)),
+        [info, reduced, theirs, w_query] + [array for _, array in first] + early,
+        [VM] * (4 + len(first) + len(early)),
         "attend_first",
-        [pltpu.VMEM((len(first) * quarter, queries), F32)],
         flops=score_flops * len(first),
         moved=quarter * queries * 4,
         exps=quarter * queries * heads * len(first),
     )
-    for index, stage in enumerate(stages[1:]):
-        last = index == len(stages) - 2
-        outs = [vmem((8, queries), F32), vmem((heads * VDIM + 16, queries), F32)]
-        if last:
-            outs = [vmem((heads * VDIM, queries), BF16)]
-        state = call(
-            functools.partial(more_kernel, heads, [shift for shift, _ in stage], last),
-            outs,
-            [info, q_t, top, total] + [array for _, array in stage],
-            [VM] * (4 + len(stage)),
+    for stage in stages[1:-1]:
+        (total,) = call(
+            functools.partial(more_kernel, heads, quarter, [shift for shift, _ in stage]),
+            [vmem((width + 16, queries), F32)],
+            [info, q_t, total] + [array for _, array in stage],
+            [VM] * (3 + len(stage)),
             "attend_more",
-            [pltpu.VMEM((len(stage) * quarter, queries), F32)],
             flops=score_flops * len(stage),
             moved=quarter * queries * 4,
             exps=quarter * queries * heads * len(stage),
         )
-        if last:
-            attended = state[0]
-        else:
-            top, total = state
+    stage = stages[-1]
+    others = [pair for group in stages[:-1] for pair in group]
+    (attended,) = call(
+        functools.partial(
+            close_kernel, heads, quarter, [shift for shift, _ in stage], [shift for shift, _ in others]
+        ),
+        [vmem((width, queries), BF16)],
+        [info, q_t, total] + [array for _, array in stage + others],
+        [VM] * (3 + count),
+        "attend_last",
+        [pltpu.VMEM((count,) + to_right.shape, BF16), pltpu.VMEM((width + 16, queries), F32)],
+        flops=score_flops * len(stage),
+        moved=quarter * queries * 4,
+        exps=quarter * queries * heads * len(stage),
+    )
     their_attended = lax.ppermute(attended, "head", swap)
     after, hidden = call(
         functools.partial(conv_kernel, halo),
         [vmem((quarter, channels), BF16), vmem((quarter, channels), BF16)],
         [
             info, rows, attended, their_attended, w_out, their_w_out,
-            conv_in.reshape(2 * channels, 2 * channels), conv_taps,
+            gate_weights, conv_taps,
         ],
         [VM] * 8,
         "gate_conv",
@@ -440,7 +490,7 @@
     (out,) = call(
         functools.partial(last_kernel, 4),
         [jax.ShapeDtypeStruct((frame_count, channels), BF16)],
-        [info, base, their_hidden, their_conv_out, frames, bypass.reshape(1, channels)],
+        [info, base, their_hidden, their_conv_out, kept_frames, weights_row],
         [VM] * 6,
         "bypass",
         [

time: 32.5 us -> 42.3 us (1.30)
  Pallas kernels: 13.8 us -> 22.5 us
  waiting for transfers between devices: 10.6 us -> 12.1 us
    pallas_call x7, Pallas kernels: 13.8 us -> 22.5 us  [call(): pl.pallas_call(kernel, out_shape=outs, in_specs=specs, out_specs=out_spec...]
    ppermute x3, waiting for transfers between devices: 8.74 us -> 7.63 us  [ring(): lax.ppermute(array, 'tm', [(i, (i + by) % count) for i in range(count)])]
    ppermute x1, waiting for transfers between devices: 0.01 us -> 1.1 us  [shards(): their_w_out = lax.ppermute(w_out, 'head', swap)]
    ppermute x1, waiting for transfers between devices: 0.16 us -> 1.1 us  [shards(): their_hidden = lax.ppermute(hidden, 'head', swap)]
    ppermute x1, waiting for transfers between devices: 0.61 us -> 1.22 us  [shards(): their_attended = lax.ppermute(attended, 'head', swap)]
  transfers between devices with their start and end apart: 8 -> 8, of which waited for: 6 -> 7; matrix products, arithmetic and copies ran while one was open for 0% -> 0% of each run, Pallas kernels for 29% -> 11%
where the time goes in v3:
time: 42.3 us; the launch traced here: 42.2 us
  Pallas kernels  22.5 us (53%)
  waiting for transfers between devices  12.1 us (29%)
  starting transfers between devices  6.02 us (14%)
  local copies, waits for them, and re-layouts  0.79 us (2%)
  between operations  0.78 us (2%)
    pallas_call x7, Pallas kernels, call(): pl.pallas_call(kernel, out_shape=outs, in_specs=specs, out_specs=out_spec...  22.5 us
    ppermute x3, waiting for transfers between devices, ring(): lax.ppermute(array, 'tm', [(i, (i + by) % count) for i in range(count)])  7.63 us
    ppermute x3, starting transfers between devices, ring(): lax.ppermute(array, 'tm', [(i, (i + by) % count) for i in range(count)])  5.08 us
    ppermute x1, waiting for transfers between devices, shards(): their_attended = lax.ppermute(attended, 'head', swap)  1.22 us
    ppermute x1, waiting for transfers between devices, shards(): their_hidden = lax.ppermute(hidden, 'head', swap)  1.1 us
    ppermute x1, waiting for transfers between devices, shards(): their_w_out = lax.ppermute(w_out, 'head', swap)  1.1 us
    ppermute x1, waiting for transfers between devices, shards(): theirs = lax.ppermute(reduced, 'head', swap)  1.03 us
  transfers between devices with their start and end apart: 8, of which 7 were waited for; matrix products, arithmetic and copies ran while one was open for 0% of the time, Pallas kernels for 11%

profile of v3, /device:TPU:0, one launch (start us, length us, event | category | flops | bytes accessed | tf_op | source)
XLA Modules:
  0.0 42.2 jit_solution(1806668911746826821)
XLA Ops:
  0.7 0.0 copy-start
  0.7 0.0 copy-start.1
  0.7 0.0 copy-start.3
  0.7 1.5 %down.1 = (bf16[448,256]{1,0:T(8,128)(2,1)S(1)}, s32[8,128]{1,0:T(8,128)S(1)}, bf16[1792,256]{1,0:T(8,128)(2,1)S(1)}) custom-call(s32[1]{0:T(128)S(6)} %copy.13.len_ref, bf16[1792,256]{1,0:T(8,128)(2,1)} %bitcast.11, f32[4,256]{1,0:T(4,128)} %weights_hbm.1), custom_call_target="tpu_custom_call" | custom-call | flops 3670016 | bytes 1376256 | tf_op jit(solution)/shard_map/down/pallas_call | solution.py:32
  2.2 0.0 copy-start.7
  2.2 0.6 %collective-permute-start = (bf16[448,256]{1,0:T(8,128)(2,1)S(1)}, bf16[448,256]{1,0:T(8,128)(2,1)S(1)}, u32[]{:S(2)}, u32[]{:S(2)}) collective-permute-start(bf16[448,256]{1,0:T(8,128)(2,1)S(1)} %get-tuple-element.16.mine_ref), channel_id=1, source_target_pairs={{0,1},{1,0},{2,3},{3,2},{4,5},{5,4},{6,7},{7,6},{8,9},{9,8},{10,11... | collective-permute-start | bytes 688136 | tf_op jit(solution)/shard_map/ppermute | solution.py:392
  2.8 0.0 copy-done
  2.8 0.1 collective-permute-start.4
  2.9 1.0 %collective-permute-done.theirs_ref = bf16[448,256]{1,0:T(8,128)(2,1)S(1)} collective-permute-done((bf16[448,256]{1,0:T(8,128)(2,1)S(1)}, bf16[448,256]{1,0:T(8,128)(2,1)S(1)}, u32[]{:S(2)}, u32[]{:S(2)}) %collective-permute-start) | collective-permute-done | bytes 229408 | tf_op jit(solution)/shard_map/ppermute | solution.py:392
  3.9 0.0 copy-done.1
  3.9 0.0 copy-done.3
  3.9 0.0 copy-start.2
  3.9 0.4 keys_values.1
  4.3 3.0 %collective-permute-start.1 = (bf16[704,128]{1,0:T(8,128)(2,1)S(1)}, bf16[704,128]{1,0:T(8,128)(2,1)S(1)}, u32[]{:S(2)}, u32[]{:S(2)}) collective-permute-start(bf16[704,128]{1,0:T(8,128)(2,1)S(1)} %get-tuple-element.17.rest_0_.rest_1_), channel_id=1, source_target_pairs={{0,4},{4,8},{8,12},{12,0},{1,5},{5,9},{9,13},{13,1},{2,6},{6,10},{... | collective-permute-start | bytes 540680 | tf_op jit(solution)/shard_map/ppermute | solution.py:369
  7.3 2.1 %collective-permute-start.2 = (bf16[704,128]{1,0:T(8,128)(2,1)S(1)}, bf16[704,128]{1,0:T(8,128)(2,1)S(1)}, u32[]{:S(2)}, u32[]{:S(2)}) collective-permute-start(bf16[704,128]{1,0:T(8,128)(2,1)S(1)} %get-tuple-element.18), channel_id=1, source_target_pairs={{0,12},{4,0},{8,4},{12,8},{1,13},{5,1},{9,5},{13,9},{2,14},{6,2},{... | collective-permute-start | bytes 540680 | tf_op jit(solution)/shard_map/ppermute | solution.py:369
  9.4 5.4 %collective-permute-done.1.rest_1_.rest_2_ = bf16[704,128]{1,0:T(8,128)(2,1)S(1)} collective-permute-done((bf16[704,128]{1,0:T(8,128)(2,1)S(1)}, bf16[704,128]{1,0:T(8,128)(2,1)S(1)}, u32[]{:S(2)}, u32[]{:S(2)}) %collective-permute-start.1) | collective-permute-done | bytes 180256 | tf_op jit(solution)/shard_map/ppermute | solution.py:369
  14.8 0.0 collective-permute-start.5
  14.8 0.0 copy-done.2
  14.8 0.0 collective-permute-start.3
  14.8 0.0 copy-done.7
  14.8 0.0 copy-start.4
  14.8 0.0 copy-start.6
  14.8 0.1 copy.12
  14.9 1.1 %collective-permute-done.3.rest_3_.their_out_ref = bf16[48,512]{1,0:T(8,128)(2,1)S(1)} collective-permute-done((bf16[48,512]{1,0:T(8,128)(2,1)S(1)}, bf16[48,512]{1,0:T(8,128)(2,1)S(1)}, u32[]{:S(2)}, u32[]{:S(2)}) %collective-permute-start.3) | collective-permute-done | bytes 49184 | tf_op jit(solution)/shard_map/ppermute | solution.py:410
  16.0 0.0 collective-permute-done.4.rest_4_.out_w_ref
  16.0 1.5 %collective-permute-done.2.rest_2_.rest_3_ = bf16[704,128]{1,0:T(8,128)(2,1)S(1)} collective-permute-done((bf16[704,128]{1,0:T(8,128)(2,1)S(1)}, bf16[704,128]{1,0:T(8,128)(2,1)S(1)}, u32[]{:S(2)}, u32[]{:S(2)}) %collective-permute-start.2) | collective-permute-done | bytes 180256 | tf_op jit(solution)/shard_map/ppermute | solution.py:369
  17.4 0.0 copy-start.5
  17.5 0.0 copy-done.4
  17.5 0.0 copy-done.6
  17.5 0.7 %copy-done.5 = f32[256]{0:T(256)S(1)} copy-done((f32[256]{0:T(256)S(1)}, f32[256]{0:T(256)}, u32[]{:S(2)}) %copy-start.5) | copy-done | bytes 1048
  18.1 3.9 %attend_first.1 = (bf16[512,512]{1,0:T(8,128)(2,1)S(1)}, f32[128,512]{1,0:T(8,128)S(1)}, f32[64,512]{1,0:T(8,128)S(1)}) custom-call(s32[8,128]{1,0:T(8,128)S(1)} %get-tuple-element.15.info_ref, bf16[448,256]{1,0:T(8,128)(2,1)S(1)} %get-tuple-element.16.mine_ref, bf16[448,256]{1,0:T(8,128)(2,1)S(1)} %collective-permute-done.theirs_ref, ...), custom_call_target="tpu_custom_call" | custom-call | flops 1056964608 | bytes 917504 | tf_op jit(solution)/shard_map/attend_first/pallas_call | solution.py:32
  22.0 0.8 %collective-permute-done.5.rest_0_ = bf16[704,128]{1,0:T(8,128)(2,1)S(1)} collective-permute-done((bf16[704,128]{1,0:T(8,128)(2,1)S(1)}, bf16[704,128]{1,0:T(8,128)(2,1)S(1)}, u32[]{:S(2)}, u32[]{:S(2)}) %collective-permute-start.5) | collective-permute-done | bytes 180256 | tf_op jit(solution)/shard_map/ppermute | solution.py:369
  22.8 13.2 %attend_last.1.mine_att_ref = bf16[48,512]{1,0:T(8,128)(2,1)S(1)} custom-call(s32[8,128]{1,0:T(8,128)S(1)} %get-tuple-element.15.info_ref, f32[128,512]{1,0:T(8,128)S(1)} %get-tuple-element.20.qt_ref, f32[64,512]{1,0:T(8,128)S(1)} %get-tuple-element.21.sum_in_ref, bf16[704,128]{1,0:T(8,128)(2,1)S(1)} %collective-permute-done.5.rest_0_, ...), custom_call_target="tpu_custom_call" | custom-call | flops 352321536 | bytes 917504 | tf_op jit(solution)/shard_map/attend_last/pallas_call | solution.py:32
  36.0 0.1 collective-permute-start.6
  36.1 1.2 %collective-permute-done.6.their_att_ref = bf16[48,512]{1,0:T(8,128)(2,1)S(1)} collective-permute-done((bf16[48,512]{1,0:T(8,128)(2,1)S(1)}, bf16[48,512]{1,0:T(8,128)(2,1)S(1)}, u32[]{:S(2)}, u32[]{:S(2)}) %collective-permute-start.6) | collective-permute-done | bytes 49184 | tf_op jit(solution)/shard_map/ppermute | solution.py:466
  37.3 1.8 %gate_conv.1 = (bf16[448,256]{1,0:T(8,128)(2,1)S(1)}, bf16[448,256]{1,0:T(8,128)(2,1)S(1)}) custom-call(s32[8,128]{1,0:T(8,128)S(1)} %get-tuple-element.15.info_ref, bf16[512,512]{1,0:T(8,128)(2,1)S(1)} %get-tuple-element.19.rows_ref, bf16[48,512]{1,0:T(8,128)(2,1)S(1)} %attend_last.1.mine_att_ref, bf16[48,512]{1,0:T(8,128)(2,1)S(1)} %collective-permute-done.6.their_att_ref, ...), custom_call_target="tpu_custom_call" | custom-call | flops 318767104 | bytes 917504 | tf_op jit(solution)/shard_map/gate_conv/pallas_call | solution.py:32
  39.1 0.2 collective-permute-start.7
  39.3 0.2 half_out.1.base_ref
  39.5 1.1 %collective-permute-done.7.hidden_ref = bf16[448,256]{1,0:T(8,128)(2,1)S(1)} collective-permute-done((bf16[448,256]{1,0:T(8,128)(2,1)S(1)}, bf16[448,256]{1,0:T(8,128)(2,1)S(1)}, u32[]{:S(2)}, u32[]{:S(2)}) %collective-permute-start.7) | collective-permute-done | bytes 229408 | tf_op jit(solution)/shard_map/ppermute | solution.py:480
  40.6 1.6 %bypass.1 = bf16[1792,256]{1,0:T(8,128)(2,1)} custom-call(s32[8,128]{1,0:T(8,128)S(1)} %get-tuple-element.15.info_ref, f32[448,256]{1,0:T(8,128)S(1)} %half_out.1.base_ref, bf16[448,256]{1,0:T(8,128)(2,1)S(1)} %collective-permute-done.7.hidden_ref, bf16[256,512]{1,0:T(8,128)(2,1)S(1)} %collective-permute-done.4.rest_4_.out_w_ref, ...), custom_call_target="tpu_custom_call" | custom-call | flops 58720256 | bytes 1835008 | tf_op jit(solution)/shard_map/bypass/pallas_call | solution.py:32
Async XLA Ops:
  0.7 2.1 %copy-start = (bf16[256,512]{1,0:T(8,128)(2,1)S(1)}, bf16[256,512]{1,0:T(8,128)(2,1)}, u32[]{:S(2)}) copy-start(bf16[256,512]{1,0:T(8,128)(2,1)} %out_w_ref.1) | copy-start | bytes 786436
  0.7 3.2 %copy-start.1 = (bf16[512,128]{1,0:T(8,128)(2,1)S(1)}, bf16[512,128]{1,0:T(8,128)(2,1)}, u32[]{:S(2)}) copy-start(bf16[512,128]{1,0:T(8,128)(2,1)} %wk_ref.1) | copy-start | bytes 393220
  0.7 3.2 %copy-start.3 = (bf16[512,48]{0,1:T(8,128)(2,1)S(1)}, bf16[512,48]{0,1:T(8,128)(2,1)}, u32[]{:S(2)}) copy-start(bf16[512,48]{0,1:T(8,128)(2,1)} %param.16) | copy-start | bytes 147460
  2.2 12.6 %copy-start.7 = (bf16[512,2,256]{2,1,0:T(2,128)(2,1)S(1)}, bf16[512,2,256]{2,1,0:T(2,128)(2,1)}, u32[]{:S(2)}) copy-start(bf16[512,2,256]{2,1,0:T(2,128)(2,1)} %param.18) | copy-start | bytes 1572868
  2.2 1.7 %collective-permute-start = (bf16[448,256]{1,0:T(8,128)(2,1)S(1)}, bf16[448,256]{1,0:T(8,128)(2,1)S(1)}, u32[]{:S(2)}, u32[]{:S(2)}) collective-permute-start(bf16[448,256]{1,0:T(8,128)(2,1)S(1)} %get-tuple-element.16.mine_ref), channel_id=1, source_target_pairs={{0,1},{1,0},{2,3},{3,2},{4,5},{5,4},{6,7},{7,6},{8,9},{9,8},{10,11... | collective-permute-start | bytes 688136 | tf_op jit(solution)/shard_map/ppermute | solution.py:392
  2.8 13.2 %collective-permute-start.4 = (bf16[256,512]{1,0:T(8,128)(2,1)S(1)}, bf16[256,512]{1,0:T(8,128)(2,1)S(1)}, u32[]{:S(2)}, u32[]{:S(2)}) collective-permute-start(bf16[256,512]{1,0:T(8,128)(2,1)S(1)} %copy-done), channel_id=1, source_target_pairs={{0,1},{1,0},{2,3},{3,2},{4,5},{5,4},{6,7},{7,6},{8,9},{9,8},{10,11... | collective-permute-start | bytes 786440 | tf_op jit(solution)/shard_map/ppermute | solution.py:411
  3.9 10.9 %copy-start.2 = (bf16[48,512]{1,0:T(8,128)(2,1)S(1)}, bf16[48,512]{1,0:T(8,128)(2,1)}, u32[]{:S(2)}) copy-start(bf16[48,512]{1,0:T(8,128)(2,1)} %mine_out_ref.1) | copy-start | bytes 147460
  4.3 10.5 %collective-permute-start.1 = (bf16[704,128]{1,0:T(8,128)(2,1)S(1)}, bf16[704,128]{1,0:T(8,128)(2,1)S(1)}, u32[]{:S(2)}, u32[]{:S(2)}) collective-permute-start(bf16[704,128]{1,0:T(8,128)(2,1)S(1)} %get-tuple-element.17.rest_0_.rest_1_), channel_id=1, source_target_pairs={{0,4},{4,8},{8,12},{12,0},{1,5},{5,9},{9,13},{13,1},{2,6},{6,10},{... | collective-permute-start | bytes 540680 | tf_op jit(solution)/shard_map/ppermute | solution.py:369
  7.3 10.2 %collective-permute-start.2 = (bf16[704,128]{1,0:T(8,128)(2,1)S(1)}, bf16[704,128]{1,0:T(8,128)(2,1)S(1)}, u32[]{:S(2)}, u32[]{:S(2)}) collective-permute-start(bf16[704,128]{1,0:T(8,128)(2,1)S(1)} %get-tuple-element.18), channel_id=1, source_target_pairs={{0,12},{4,0},{8,4},{12,8},{1,13},{5,1},{9,5},{13,9},{2,14},{6,2},{... | collective-permute-start | bytes 540680 | tf_op jit(solution)/shard_map/ppermute | solution.py:369
  14.8 8.1 %collective-permute-start.5 = (bf16[704,128]{1,0:T(8,128)(2,1)S(1)}, bf16[704,128]{1,0:T(8,128)(2,1)S(1)}, u32[]{:S(2)}, u32[]{:S(2)}) collective-permute-start(bf16[704,128]{1,0:T(8,128)(2,1)S(1)} %collective-permute-done.1.rest_1_.rest_2_), channel_id=1, source_target_pairs={{0,4},{4,8},{8,12},{12,0},{1,5},{5,9},{9,13},{13,1},{2,6},{6,10},{... | collective-permute-start | bytes 540680 | tf_op jit(solution)/shard_map/ppermute | solution.py:369
  14.8 1.2 %collective-permute-start.3 = (bf16[48,512]{1,0:T(8,128)(2,1)S(1)}, bf16[48,512]{1,0:T(8,128)(2,1)S(1)}, u32[]{:S(2)}, u32[]{:S(2)}) collective-permute-start(bf16[48,512]{1,0:T(8,128)(2,1)S(1)} %copy-done.2), channel_id=1, source_target_pairs={{0,1},{1,0},{2,3},{3,2},{4,5},{5,4},{6,7},{7,6},{8,9},{9,8},{10,11... | collective-permute-start | bytes 147464 | tf_op jit(solution)/shard_map/ppermute | solution.py:410
  14.8 2.7 %copy-start.4 = (f32[31,256]{1,0:T(8,128)S(1)}, f32[31,256]{1,0:T(8,128)}, u32[]{:S(2)}) copy-start(f32[31,256]{1,0:T(8,128)} %taps_ref.1) | copy-start | bytes 95236
  14.8 2.7 %copy-start.6 = (bf16[512,128]{1,0:T(8,128)(2,1)S(1)}, bf16[512,128]{1,0:T(8,128)(2,1)}, u32[]{:S(2)}) copy-start(bf16[512,128]{1,0:T(8,128)(2,1)} %wq_ref.1) | copy-start | bytes 393220
  17.4 0.7 %copy-start.5 = (f32[256]{0:T(256)S(1)}, f32[256]{0:T(256)}, u32[]{:S(2)}) copy-start(f32[256]{0:T(256)} %param.21) | copy-start | bytes 3076
  36.0 1.3 %collective-permute-start.6 = (bf16[48,512]{1,0:T(8,128)(2,1)S(1)}, bf16[48,512]{1,0:T(8,128)(2,1)S(1)}, u32[]{:S(2)}, u32[]{:S(2)}) collective-permute-start(bf16[48,512]{1,0:T(8,128)(2,1)S(1)} %attend_last.1.mine_att_ref), channel_id=1, source_target_pairs={{0,1},{1,0},{2,3},{3,2},{4,5},{5,4},{6,7},{7,6},{8,9},{9,8},{10,11... | collective-permute-start | bytes 147464 | tf_op jit(solution)/shard_map/ppermute | solution.py:466
  39.1 1.6 %collective-permute-start.7 = (bf16[448,256]{1,0:T(8,128)(2,1)S(1)}, bf16[448,256]{1,0:T(8,128)(2,1)S(1)}, u32[]{:S(2)}, u32[]{:S(2)}) collective-permute-start(bf16[448,256]{1,0:T(8,128)(2,1)S(1)} %get-tuple-element.23.hidden_ref), channel_id=1, source_target_pairs={{0,1},{1,0},{2,3},{3,2},{4,5},{5,4},{6,7},{7,6},{8,9},{9,8},{10,11... | collective-permute-start | bytes 688136 | tf_op jit(solution)/shard_map/ppermute | solution.py:480

commit v4 on v3

--- a/solution.py
+++ b/solution.py
@@ -26,7 +26,7 @@
     return pltpu.with_memory_space_constraint(array, pltpu.VMEM if spec is VM else pltpu.HBM)
 
 
-def call(kernel, outs, operands, specs, name, scratch=(), out_specs=None, flops=0, moved=0, exps=0):
+def call(kernel, outs, operands, specs, scratch=(), out_specs=None, flops=0, moved=0, exps=0):
     out_specs = out_specs or [VM] * len(outs)
     operands = [placed(a, s) for a, s in zip(operands, specs)]
     return pl.pallas_call(
@@ -35,7 +35,6 @@
         in_specs=specs,
         out_specs=out_specs,
         scratch_shapes=list(scratch),
-        name=name,
         compiler_params=pltpu.CompilerParams(vmem_limit_bytes=24 * 2**20),
         cost_estimate=pl.CostEstimate(flops=flops, bytes_accessed=moved, transcendentals=exps),
     )(*operands)
@@ -90,8 +89,13 @@
             out_ref[i * rows : (i + 1) * rows, lanes] = total.astype(BF16)
 
 
-def kv_rows(quarter, width):
-    return quarter + width * ((quarter + 127) // 128)
+def pack_plan(quarter, width):
+    full, rest = divmod(quarter, 128)
+    folded = 2 * rest == 128 and width % 16 == 0
+    last = 0 if rest == 0 else (-(-width // 32) * 16 if folded else width)
+    rows = quarter + full * width + last
+    first = min(quarter, -(-rows // 32) * 16)
+    return first, rows - first, folded
 
 
 def put_edge(pack_ref, at, halo, rows):
@@ -105,61 +109,69 @@
     return jnp.concatenate(pieces, axis=1)
 
 
-def kv_kernel(halo, mine_ref, theirs_ref, wk_ref, wvt_ref, right_ref, left_ref):
+def kv_kernel(halo, mine_ref, theirs_ref, wk_ref, wvt_ref, first_ref, second_ref, left_ref, right_ref):
     quarter, channels = mine_ref.shape
     width = wvt_ref.shape[0]
+    first, second, folded = pack_plan(quarter, width)
     mine, theirs = halves(channels)
     a, b = mine_ref[...], theirs_ref[...]
     keys = dot(a, wk_ref[mine, :]) + dot(b, wk_ref[theirs, :])
     keys = keys.astype(BF16)
     values_t = dot(wvt_ref[:, mine], a, NT) + dot(wvt_ref[:, theirs], b, NT)
-    values_t = values_t.astype(BF16)
-    for pack_ref, edge in ((right_ref, slice(quarter - halo, quarter)), (left_ref, slice(0, halo))):
-        pack_ref[:quarter, :] = keys
-        at = quarter
-        for lane in range(0, quarter, 128):
-            size = min(128, quarter - lane)
-            if size < 128:
-                pack_ref[at : at + width, :] = jnp.zeros((width, 128), BF16)
-            pack_ref[at : at + width, :size] = values_t[:, lane : lane + size]
+    for pack_ref in (first_ref, left_ref):
+        pack_ref[:first, :] = keys[:first, :]
+    for pack_ref in (second_ref, right_ref):
+        pack_ref[: quarter - first, :] = keys[first:, :]
+        at = quarter - first
+        for lane in range(0, quarter - 127, 128):
+            pack_ref[at : at + width, :] = values_t[:, lane : lane + 128].astype(BF16)
             at += width
-        at = put_edge(pack_ref, at, halo, mine_ref[edge, :])
-        put_edge(pack_ref, at, halo, theirs_ref[edge, :])
-
-
-def head_query(q_t, head, ones):
+        if quarter % 128:
+            tail = values_t[:, quarter - quarter % 128 :]
+            if folded:
+                tail = jnp.concatenate([tail[: width // 2, :], tail[width // 2 :, :]], axis=1)
+            tail = jnp.concatenate([tail, jnp.zeros((second - at - tail.shape[0], tail.shape[1]), F32)], axis=0)
+            if tail.shape[1] < 128:
+                tail = jnp.concatenate([tail, jnp.zeros((tail.shape[0], 128 - tail.shape[1]), F32)], axis=1)
+            pack_ref[at:second, :] = tail.astype(BF16)
+    at = put_edge(right_ref, second, halo, mine_ref[quarter - halo :, :])
+    put_edge(right_ref, at, halo, theirs_ref[quarter - halo :, :])
+    at = put_edge(left_ref, first, halo, mine_ref[:halo, :])
+    put_edge(left_ref, at, halo, theirs_ref[:halo, :])
+
+
+def head_query(q_t, head):
     at = lax.broadcasted_iota(jnp.int32, q_t.shape, 0) // QDIM
-    return jnp.concatenate([jnp.where(at == head, q_t, 0.0).astype(BF16), ones], axis=0)
-
-
-def one_row(queries):
-    at = lax.broadcasted_iota(jnp.int32, (128, queries), 0)
-    return jnp.where(at == 0, 1.0, 0.0).astype(BF16)
-
-
-def masked_keys(pack, quarter, first_row, live_rows):
-    row = lax.broadcasted_iota(jnp.int32, (quarter, 128), 0) + first_row
-    lane = lax.broadcasted_iota(jnp.int32, (quarter, 128), 1)
-    bias = jnp.where((lane == 0) & (row >= live_rows), NEG, 0.0).astype(BF16)
-    return jnp.concatenate([pack[:quarter, :], bias], axis=1)
-
-
-def all_values(pack, quarter, width):
+    return jnp.where(at == head, q_t, 0.0).astype(BF16)
+
+
+def all_keys(pack, first, quarter):
+    return jnp.concatenate([pack[0][:first, :], pack[1][: quarter - first, :]], axis=0)
+
+
+def all_values(ref, at, end, quarter, width):
+    folded = pack_plan(quarter, width)[2]
     pieces = []
-    at = quarter
-    for lane in range(0, quarter, 128):
-        size = min(128, quarter - lane)
-        pieces.append(pack[at : at + width, :size].astype(F32))
+    for _ in range(0, quarter - 127, 128):
+        pieces.append(ref[at : at + width, :].astype(F32))
         at += width
+    rest = quarter % 128
+    if rest:
+        tail = ref[at:end, :].astype(F32)
+        if folded:
+            half = width // 2
+            tail = jnp.concatenate([tail[:half, :rest], tail[:half, rest : 2 * rest]], axis=0)
+        pieces.append(tail[:width, :rest])
     return jnp.concatenate(pieces, axis=1)
 
 
-def head_values(values_t, head):
+def head_values(values_t, head, live_keys):
     width, quarter = values_t.shape
     row = lax.broadcasted_iota(jnp.int32, (width, quarter), 0)
     kept = jnp.where((row >= head * VDIM) & (row < (head + 1) * VDIM), values_t, 0.0).astype(BF16)
     extra = lax.broadcasted_iota(jnp.int32, (16, quarter), 0)
-    ones = jnp.where(extra == head, 1.0, 0.0).astype(BF16)
+    key = lax.broadcasted_iota(jnp.int32, (16, quarter), 1)
+    ones = jnp.where((extra == head) & (key < live_keys), 1.0, 0.0).astype(BF16)
     return jnp.concatenate([kept, ones], axis=0)
 
 
@@ -173,15 +185,31 @@
 
 
 def absorb(total, q_t, packs, sources, live_rows, quarter, heads):
-    ones = one_row(q_t.shape[1])
+    queries = q_t.shape[1]
+    tiles = [slice(at, min(at + 512, queries)) for at in range(0, queries, 512)]
+    totals = [None if total is None else total[:, tile] for tile in tiles]
+    asked = [head_query(q_t, head) for head in range(heads)]
+    units = []
+    first, second, _ = pack_plan(quarter, heads * VDIM)
     for pack, source in zip(packs, sources):
-        keys = masked_keys(pack, quarter, source * quarter, live_rows)
-        values_t = all_values(pack, quarter, heads * VDIM)
+        keys = all_keys(pack, first, quarter)
+        values_t = all_values(pack[1], quarter - first, second, quarter, heads * VDIM)
         for head in range(heads):
-            expo = jnp.exp2(dot(keys, head_query(q_t, head, ones))).astype(BF16)
-            part = dot(head_values(values_t, head), expo)
-            total = part if total is None else total + part
-    return total
+            values = head_values(values_t, head, live_rows - source * quarter)
+            units += [(keys, values, head, i) for i in range(len(tiles))]
+
+    def scores(unit):
+        keys, _, head, i = unit
+        return dot(keys, asked[head][:, tiles[i]])
+
+    ahead = scores(units[0])
+    for at, (_, values, _, i) in enumerate(units):
+        now = ahead
+        if at + 1 < len(units):
+            ahead = scores(units[at + 1])
+        part = dot(values, jnp.exp2(now).astype(BF16))
+        totals[i] = part if totals[i] is None else totals[i] + part
+    return jnp.concatenate(totals, axis=1)
 
 
 def finish(total, heads):
@@ -195,26 +223,62 @@
     return [lax.rem(here + shift + count, count) for shift in shifts]
 
 
-def open_kernel(heads, halo, shifts, info_ref, mine_ref, theirs_ref, wq_ref, *rest):
-    packs = rest[: len(shifts)]
+def pairs_of(refs):
+    return list(zip(refs[::2], refs[1::2]))
+
+
+def scaled_queries(mine_rows, their_rows, wq_ref, channels):
+    mine, theirs = halves(channels)
+    query = dot(mine_rows, wq_ref[mine, :]) + dot(their_rows, wq_ref[theirs, :])
+    return jnp.transpose(query * (math.log2(math.e) / math.sqrt(QDIM)))
+
+
+def own_kernel(heads, info_ref, mine_ref, theirs_ref, wq_ref, first_ref, second_ref, *rest):
+    qt_ref, sum_ref = rest[-2:]
+    quarter, channels = mine_ref.shape
+    queries = qt_ref.shape[1]
+    blank = jnp.zeros((queries - quarter, channels), BF16)
+    q_t = scaled_queries(
+        jnp.concatenate([mine_ref[...], blank], axis=0),
+        jnp.concatenate([theirs_ref[...], blank], axis=0),
+        wq_ref,
+        channels,
+    )
+    qt_ref[...] = q_t
+    total = absorb(
+        None, q_t, [(first_ref, second_ref)], sources_of([0]), info_ref[0:1, 0:1], quarter, heads
+    )
+    lane = lax.broadcasted_iota(jnp.int32, total.shape, 1)
+    sum_ref[...] = jnp.where(lane < quarter, total, 0.0)
+
+
+def open_kernel(heads, halo, shifts, info_ref, mine_ref, theirs_ref, wq_ref, qt_in_ref, sum_in_ref, *rest):
+    packs = pairs_of(rest[: 2 * len(shifts)])
     rows_ref, qt_ref, sum_ref = rest[-3:]
     quarter, channels = mine_ref.shape
-    edge = kv_rows(quarter, heads * VDIM)
+    first, second, _ = pack_plan(quarter, heads * VDIM)
     queries = rows_ref.shape[0]
-    rows_ref[:halo, :] = get_edge(packs[1], edge, halo, 2 * channels)
-    rows_ref[halo : halo + quarter, :channels] = mine_ref[...]
-    rows_ref[halo : halo + quarter, channels:] = theirs_ref[...]
-    rows_ref[halo + quarter : 2 * halo + quarter, :] = get_edge(packs[2], edge, halo, 2 * channels)
-    rows_ref[2 * halo + quarter :, :] = jnp.zeros((queries - 2 * halo - quarter, 2 * channels), BF16)
-    mine, theirs = halves(channels)
-    query = dot(rows_ref[:, :channels], wq_ref[mine, :]) + dot(rows_ref[:, channels:], wq_ref[theirs, :])
-    q_t = jnp.transpose(query * (math.log2(math.e) / math.sqrt(QDIM)))
+    late = quarter - quarter % 128
+    rows_ref[:quarter, :channels] = mine_ref[...]
+    rows_ref[:quarter, channels:] = theirs_ref[...]
+    rows_ref[quarter : quarter + halo, :] = get_edge(packs[1][1], second, halo, 2 * channels)
+    rows_ref[quarter + halo : quarter + 2 * halo, :] = get_edge(packs[2][0], first, halo, 2 * channels)
+    rows_ref[quarter + 2 * halo :, :] = jnp.zeros((queries - 2 * halo - quarter, 2 * channels), BF16)
+    q_late = scaled_queries(rows_ref[late:, :channels], rows_ref[late:, channels:], wq_ref, channels)
+    q_t = jnp.concatenate([qt_in_ref[:, :late], q_late], axis=1)
     qt_ref[...] = q_t
-    sum_ref[...] = absorb(None, q_t, packs, sources_of(shifts), info_ref[0:1, 0:1], quarter, heads)
+    live_rows = info_ref[0:1, 0:1]
+    sources = sources_of(shifts)
+    total = absorb(sum_in_ref[...], q_t, packs[1:], sources[1:], live_rows, quarter, heads)
+    edge = absorb(None, q_late, packs[:1], sources[:1], live_rows, quarter, heads)
+    lane = lax.broadcasted_iota(jnp.int32, edge.shape, 1) + late
+    edge = jnp.where(lane < quarter, 0.0, edge)
+    sum_ref[:, :late] = total[:, :late]
+    sum_ref[:, late:] = total[:, late:] + edge
 
 
 def more_kernel(heads, quarter, shifts, info_ref, qt_ref, sum_in_ref, *rest):
-    packs = rest[: len(shifts)]
+    packs = pairs_of(rest[: 2 * len(shifts)])
     sum_ref = rest[-1]
     sum_ref[...] = absorb(
         sum_in_ref[...], qt_ref[...], packs, sources_of(shifts), info_ref[0:1, 0:1], quarter, heads
@@ -222,7 +286,7 @@
 
 
 def close_kernel(heads, quarter, shifts, everything, info_ref, qt_ref, sum_in_ref, *rest):
-    packs = rest[: len(shifts) + len(everything)]
+    packs = pairs_of(rest[: 2 * len(shifts) + 2 * len(everything)])
     out_ref, held, total_ref = rest[-3:]
     live_rows = info_ref[0:1, 0:1]
     width = heads * VDIM
@@ -236,11 +300,13 @@
     @pl.when(jnp.max(safe) > 0.0)
     def _():
         count = lax.axis_size("tm")
+        first, second, _ = pack_plan(quarter, width)
         for i, (pack, shift) in enumerate(zip(packs, list(shifts) + list(everything))):
-            held[i] = pack[...]
+            held[i, :first, :] = pack[0][:first, :]
+            held[i, first:, :] = pack[1][:second, :]
         firsts = sources_of(list(shifts) + list(everything))
         q_t = qt_ref[...]
-        ones = one_row(q_t.shape[1])
+        row = lax.broadcasted_iota(jnp.int32, (quarter, q_t.shape[1]), 0)
         total_ref[...] = jnp.zeros_like(total_ref)
 
         def first_row(i):
@@ -250,10 +316,10 @@
             return first * quarter
 
         def one_head(head, carry):
-            query = head_query(q_t, head, ones)
+            query = head_query(q_t, head)
 
             def scores(i):
-                return dot(masked_keys(held.at[i], quarter, first_row(i), live_rows), query)
+                return jnp.where(row < live_rows - first_row(i), dot(held[i, :quarter, :], query), NEG)
 
             def highest(i, top):
                 return jnp.maximum(top, jnp.max(scores(i), axis=0, keepdims=True))
@@ -262,7 +328,9 @@
 
             def add(i, carry):
                 expo = jnp.exp2(scores(i) - top).astype(BF16)
-                total_ref[...] += dot(head_values(all_values(held.at[i], quarter, width), head), expo)
+                values = all_values(held.at[i], quarter, first + second, quarter, width)
+                values = head_values(values, head, live_rows - first_row(i))
+                total_ref[...] += dot(values, expo)
                 return carry
 
             return lax.fori_loop(0, count, add, carry)
@@ -285,15 +353,19 @@
         w_out = jnp.concatenate([mine_out_ref[:, side], their_out_ref[:, side]], axis=0)
         delta = dot(attended, w_out, TN)
         sides.append((rows_ref[:, lanes].astype(F32) + delta).astype(BF16)[:count])
-    after_ref[...] = sides[0][halo : halo + quarter]
+    after_ref[...] = sides[0][:quarter]
     gates = dot(sides[0], conv_in_ref[mine, :]) + dot(sides[1], conv_in_ref[theirs, :])
     value, gate = gates[:, :channels], gates[:, channels:]
     row = lax.broadcasted_iota(jnp.int32, (count, channels), 0)
-    row = row + (lax.axis_index("tm") * quarter - halo)
+    row = jnp.where((row >= quarter) & (row < quarter + halo), row - (quarter + halo), row)
+    row = jnp.where(row >= quarter + halo, row - halo, row) + lax.axis_index("tm") * quarter
     live = (row >= 0) & (row < info_ref[0:1, 0:1])
     mixed = jnp.where(live, value * jax.nn.sigmoid(gate), 0.0).astype(BF16).astype(F32)
     for tile in range(channels // 128):
-        gated[tile] = mixed[:, tile * 128 : (tile + 1) * 128]
+        lanes = slice(tile * 128, tile * 128 + 128)
+        gated[tile, :halo] = mixed[quarter : quarter + halo, lanes]
+        gated[tile, halo : halo + quarter] = mixed[:quarter, lanes]
+        gated[tile, halo + quarter :] = mixed[quarter + halo :, lanes]
     block = 64
     start = halo - taps // 2
     for tile in range(channels // 128):
@@ -306,10 +378,13 @@
             hidden_ref[base : base + block, lanes] = (total * jax.nn.sigmoid(total)).astype(BF16)
 
 
-def half_kernel(after_ref, hidden_ref, out_w_ref, base_ref):
+def half_kernel(after_ref, hidden_ref, out_w_ref, bypass_hbm, base_ref, bypass_ref, sem):
+    copy = pltpu.make_async_copy(bypass_hbm, bypass_ref, sem.at[0])
+    copy.start()
     channels = hidden_ref.shape[1]
     mine, _ = halves(channels)
     base_ref[...] = after_ref[...].astype(F32) + dot(hidden_ref[...], out_w_ref[:, mine])
+    copy.wait()
 
 
 def last_kernel(
@@ -380,7 +455,6 @@
         ],
         [lengths, frames, down_weights],
         [SM, HB, HB],
-        "down",
         [
             pltpu.VMEM((channels // 128, frame_count, 128), F32),
             pltpu.VMEM(down_weights.shape, F32),
@@ -390,75 +464,92 @@
         moved=3 * frame_count * channels,
     )
     theirs = lax.ppermute(reduced, "head", swap)
+    width = heads * VDIM
     edge_rows = halo * 2 * channels // 128
-    to_right, to_left = call(
+    first_rows, second_rows, _ = pack_plan(quarter, width)
+    first, second, first_left, second_right = call(
         functools.partial(kv_kernel, halo),
-        [vmem((kv_rows(quarter, heads * VDIM) + edge_rows, keys_wide), BF16)] * 2,
+        [
+            vmem((first_rows, keys_wide), BF16),
+            vmem((second_rows, keys_wide), BF16),
+            vmem((first_rows + edge_rows, keys_wide), BF16),
+            vmem((second_rows + edge_rows, keys_wide), BF16),
+        ],
         [reduced, theirs, w_key, w_value.T],
         [VM] * 4,
-        "keys_values",
-        flops=4 * quarter * channels * (keys_wide + heads * VDIM),
+        flops=4 * quarter * channels * (keys_wide + width),
         moved=8 * quarter * channels,
     )
-    right = [to_right, ring(to_right, 1)]
-    left = [to_left, ring(to_left, -1)]
-    steps_right, steps_left = count // 2, (count - 1) // 2
-    for step in range(2, steps_right + 1):
-        right.append(ring(right[-1], 1))
-    for step in range(2, steps_left + 1):
-        left.append(ring(left[-1], -1))
+    reach = count // 2
+    right_first, left_second = [ring(first, 1)], [ring(second, -1)]
+    right_second, left_first = [ring(second_right, 1)], [ring(first_left, -1)]
+    for step in range(2, reach + 1):
+        right_first.append(ring(right_first[-1], 1))
+        left_second.append(ring(left_second[-1], -1))
+        if step < reach:
+            right_second.append(ring(right_second[-1], 1))
+            left_first.append(ring(left_first[-1], -1))
     their_w_out = lax.ppermute(w_out, "head", swap)
     their_conv_out = lax.ppermute(conv_out, "head", swap)
     gate_weights = conv_in.reshape(2 * channels, 2 * channels)
-    weights_row = bypass.reshape(1, channels)
-    early = [their_w_out, their_conv_out, gate_weights, weights_row, conv_taps, w_out, conv_out]
-
-    stages = [[(0, to_right), (-1, right[1]), (1, left[1])]]
-    for step in range(2, steps_right + 1):
-        stage = [(-step, right[step])]
-        if step <= steps_left:
-            stage.append((step, left[step]))
-        stages.append(stage)
+    early = [their_w_out, their_conv_out, gate_weights, conv_taps, w_out, conv_out]
+
+    stages = [[(0, first, second), (-1, right_first[0], right_second[0]), (1, left_first[0], left_second[0])]]
+    for step in range(2, reach):
+        at = step - 1
+        stages.append([(-step, right_first[at], right_second[at]), (step, left_first[at], left_second[at])])
+    stages.append([(reach, right_first[-1], left_second[-1])])
     score_flops = 2 * quarter * queries * heads * (128 + 64)
 
-    first = stages[0]
-    width = heads * VDIM
+    def arrays(stage):
+        return [array for pack in stage for array in pack[1:]]
+
+    def shifts(stage):
+        return [pack[0] for pack in stage]
+
+    q_t, total = call(
+        functools.partial(own_kernel, heads),
+        [vmem((keys_wide, queries), F32), vmem((width + 16, queries), F32)],
+        [info, reduced, theirs, w_query, first, second] + early,
+        [VM] * (6 + len(early)),
+        flops=score_flops,
+        moved=quarter * queries * 4,
+        exps=quarter * queries * heads,
+    )
     rows, q_t, total = call(
-        functools.partial(open_kernel, heads, halo, [shift for shift, _ in first]),
+        functools.partial(open_kernel, heads, halo, shifts(stages[0])),
         [
             vmem((queries, 2 * channels), BF16),
             vmem((keys_wide, queries), F32),
             vmem((width + 16, queries), F32),
         ],
-        [info, reduced, theirs, w_query] + [array for _, array in first] + early,
-        [VM] * (4 + len(first) + len(early)),
-        "attend_first",
-        flops=score_flops * len(first),
+        [info, reduced, theirs, w_query, q_t, total] + arrays(stages[0]),
+        [VM] * (6 + 2 * len(stages[0])),
+        flops=score_flops * len(stages[0]),
         moved=quarter * queries * 4,
-        exps=quarter * queries * heads * len(first),
+        exps=quarter * queries * heads * len(stages[0]),
     )
     for stage in stages[1:-1]:
         (total,) = call(
-            functools.partial(more_kernel, heads, quarter, [shift for shift, _ in stage]),
+            functools.partial(more_kernel, heads, quarter, shifts(stage)),
             [vmem((width + 16, queries), F32)],
-            [info, q_t, total] + [array for _, array in stage],
-            [VM] * (3 + len(stage)),
-            "attend_more",
+            [info, q_t, total] + arrays(stage),
+            [VM] * (3 + 2 * len(stage)),
             flops=score_flops * len(stage),
             moved=quarter * queries * 4,
             exps=quarter * queries * heads * len(stage),
         )
     stage = stages[-1]
-    others = [pair for group in stages[:-1] for pair in group]
+    others = [pack for group in stages[:-1] for pack in group]
     (attended,) = call(
-        functools.partial(
-            close_kernel, heads, quarter, [shift for shift, _ in stage], [shift for shift, _ in others]
-        ),
+        functools.partial(close_kernel, heads, quarter, shifts(stage), shifts(others)),
         [vmem((width, queries), BF16)],
-        [info, q_t, total] + [array for _, array in stage + others],
-        [VM] * (3 + count),
-        "attend_last",
-        [pltpu.VMEM((count,) + to_right.shape, BF16), pltpu.VMEM((width + 16, queries), F32)],
+        [info, q_t, total] + arrays(stage + others),
+        [VM] * (3 + 2 * count),
+        [
+            pltpu.VMEM((count, first_rows + second_rows, keys_wide), BF16),
+            pltpu.VMEM((width + 16, queries), F32),
+        ],
         flops=score_flops * len(stage),
         moved=quarter * queries * 4,
         exps=quarter * queries * heads * len(stage),
@@ -472,27 +563,25 @@
             gate_weights, conv_taps,
         ],
         [VM] * 8,
-        "gate_conv",
         [pltpu.VMEM((channels // 128, quarter + 2 * halo, 128), F32)],
         flops=2 * queries * 2 * channels * (96 + 2 * channels),
         moved=quarter * channels * 8,
     )
     their_hidden = lax.ppermute(hidden, "head", swap)
-    (base,) = call(
+    base, kept_bypass = call(
         half_kernel,
-        [vmem((quarter, channels), F32)],
-        [after, hidden, conv_out],
-        [VM] * 3,
-        "half_out",
+        [vmem((quarter, channels), F32), vmem((1, channels), F32)],
+        [after, hidden, conv_out, bypass.reshape(1, channels)],
+        [VM, VM, VM, HB],
+        [pltpu.SemaphoreType.DMA((1,))],
         flops=2 * quarter * channels * channels,
         moved=quarter * channels * 4,
     )
     (out,) = call(
         functools.partial(last_kernel, 4),
         [jax.ShapeDtypeStruct((frame_count, channels), BF16)],
-        [info, base, their_hidden, their_conv_out, kept_frames, weights_row],
+        [info, base, their_hidden, their_conv_out, kept_frames, kept_bypass],
         [VM] * 6,
-        "bypass",
         [
             pltpu.VMEM((channels // 128, frame_count, 128), F32),
             pltpu.VMEM((frame_count, channels), BF16),

time: 42.3 us -> 46.5 us (1.099)
  starting transfers between devices: 6.02 us -> 14.5 us
  waiting for transfers between devices: 12.1 us -> 8.09 us
  Pallas kernels: 22.5 us -> 22 us
    ppermute x3 -> x6, starting transfers between devices: 5.08 us -> 13.1 us  [ring(): lax.ppermute(array, 'tm', [(i, (i + by) % count) for i in range(count)])]
    ppermute x3 -> x6, waiting for transfers between devices: 7.63 us -> 5.64 us  [ring(): lax.ppermute(array, 'tm', [(i, (i + by) % count) for i in range(count)])]
    ppermute x1, waiting for transfers between devices: 1.1 us -> 0.01 us  [shards(): their_w_out = lax.ppermute(w_out, 'head', swap)]
    pallas_call x7 -> x8, Pallas kernels: 22.5 us -> 22 us  [call(): pl.pallas_call(kernel, out_shape=outs, in_specs=specs, out_specs=out_spec...]
    ppermute x1, waiting for transfers between devices: 1.1 us -> 0.63 us  [shards(): their_hidden = lax.ppermute(hidden, 'head', swap)]
  transfers between devices with their start and end apart: 8 -> 11, of which waited for: 7 -> 5; matrix products, arithmetic and copies ran while one was open for 0% -> 0% of each run, Pallas kernels for 11% -> 10%
where the time goes in v4:
time: 46.5 us; the launch traced here: 46.3 us
  Pallas kernels  22 us (47%)
  starting transfers between devices  14.5 us (31%)
  waiting for transfers between devices  8.09 us (17%)
  local copies, waits for them, and re-layouts  0.93 us (2%)
  between operations  0.79 us (2%)
    pallas_call x8, Pallas kernels, call(): pl.pallas_call(kernel, out_shape=outs, in_specs=specs, out_specs=out_spec...  22 us
    ppermute x6, starting transfers between devices, ring(): lax.ppermute(array, 'tm', [(i, (i + by) % count) for i in range(count)])  13.1 us
    ppermute x6, waiting for transfers between devices, ring(): lax.ppermute(array, 'tm', [(i, (i + by) % count) for i in range(count)])  5.64 us
    ppermute x1, waiting for transfers between devices, shards(): their_attended = lax.ppermute(attended, 'head', swap)  1.22 us
  transfers between devices with their start and end apart: 11, of which 5 were waited for; matrix products, arithmetic and copies ran while one was open for 0% of the time, Pallas kernels for 10%

profile of v4, /device:TPU:0, one launch (start us, length us, event | category | flops | bytes accessed | tf_op | source)
XLA Modules:
  0.0 46.3 jit_solution(14549700981091866340)
XLA Ops:
  0.7 0.0 copy-start
  0.7 0.0 copy-start.1
  0.7 0.0 copy-start.3
  0.7 0.0 copy-start.5
  0.7 1.5 %shard_map.109 = (bf16[448,256]{1,0:T(8,128)(2,1)S(1)}, s32[8,128]{1,0:T(8,128)S(1)}, bf16[1792,256]{1,0:T(8,128)(2,1)S(1)}) custom-call(s32[1]{0:T(128)S(6)} %copy.13.len_ref, bf16[1792,256]{1,0:T(8,128)(2,1)} %bitcast.9, f32[4,256]{1,0:T(4,128)} %weights_hbm.1), custom_call_target="tpu_custom_call" | custom-call | flops 3670016 | bytes 1376256 | tf_op jit(solution)/shard_map/pallas_call | solution.py:32
  2.2 0.0 copy-start.6
  2.2 0.6 %collective-permute-start = (bf16[448,256]{1,0:T(8,128)(2,1)S(1)}, bf16[448,256]{1,0:T(8,128)(2,1)S(1)}, u32[]{:S(2)}, u32[]{:S(2)}) collective-permute-start(bf16[448,256]{1,0:T(8,128)(2,1)S(1)} %get-tuple-element.22.mine_ref), channel_id=1, source_target_pairs={{0,1},{1,0},{2,3},{3,2},{4,5},{5,4},{6,7},{7,6},{8,9},{9,8},{10,11... | collective-permute-start | bytes 688136 | tf_op jit(solution)/shard_map/ppermute | solution.py:466
  2.8 0.0 copy-done
  2.8 0.1 collective-permute-start.2
  2.9 0.0 copy-done.1
  2.9 0.4 collective-permute-start.1
  3.3 0.6 %collective-permute-done.theirs_ref = bf16[448,256]{1,0:T(8,128)(2,1)S(1)} collective-permute-done((bf16[448,256]{1,0:T(8,128)(2,1)S(1)}, bf16[448,256]{1,0:T(8,128)(2,1)S(1)}, u32[]{:S(2)}, u32[]{:S(2)}) %collective-permute-start) | collective-permute-done | bytes 229408 | tf_op jit(solution)/shard_map/ppermute | solution.py:466
  3.9 0.0 copy-done.3
  3.9 0.0 copy-done.5
  3.9 0.4 shard_map.110
  4.3 5.0 %collective-permute-start.5 = (bf16[384,128]{1,0:T(8,128)(2,1)S(1)}, bf16[384,128]{1,0:T(8,128)(2,1)S(1)}, u32[]{:S(2)}, u32[]{:S(2)}) collective-permute-start(bf16[384,128]{1,0:T(8,128)(2,1)S(1)} %get-tuple-element.28), channel_id=1, source_target_pairs={{0,12},{4,0},{8,4},{12,8},{1,13},{5,1},{9,5},{13,9},{2,14},{6,2},{... | collective-permute-start | bytes 294920 | tf_op jit(solution)/shard_map/ppermute | solution.py:444
  9.3 0.0 collective-permute-start.4
  9.3 0.0 collective-permute-start.3
  9.3 0.0 collective-permute-done.1.rest_0_.their_out_ref
  9.3 3.8 %collective-permute-start.6 = (bf16[304,128]{1,0:T(8,128)(2,1)S(1)}, bf16[304,128]{1,0:T(8,128)(2,1)S(1)}, u32[]{:S(2)}, u32[]{:S(2)}) collective-permute-start(bf16[304,128]{1,0:T(8,128)(2,1)S(1)} %get-tuple-element.24.second_ref.rest_1_.rest_3_), channel_id=1, source_target_pairs={{0,12},{4,0},{8,4},{12,8},{1,13},{5,1},{9,5},{13,9},{2,14},{6,2},{... | collective-permute-start | bytes 233480 | tf_op jit(solution)/shard_map/ppermute | solution.py:444
  13.2 0.0 copy-done.6
  13.2 0.0 copy-start.2
  13.2 0.0 copy-start.4
  13.2 0.1 copy.12
  13.3 0.0 collective-permute-done.2.rest_1_.out_w_ref
  13.3 0.7 %copy-done.2 = f32[31,256]{1,0:T(8,128)S(1)} copy-done((f32[31,256]{1,0:T(8,128)S(1)}, f32[31,256]{1,0:T(8,128)}, u32[]{:S(2)}) %copy-start.2) | copy-done | bytes 31768
  13.9 0.2 copy-done.4
  14.1 1.5 %shard_map.111 = (f32[128,512]{1,0:T(8,128)S(1)}, f32[64,512]{1,0:T(8,128)S(1)}) custom-call(s32[8,128]{1,0:T(8,128)S(1)} %get-tuple-element.21.info_ref, bf16[448,256]{1,0:T(8,128)(2,1)S(1)} %get-tuple-element.22.mine_ref, bf16[448,256]{1,0:T(8,128)(2,1)S(1)} %collective-permute-done.theirs_ref, bf16[512,128]{1,0:T(8,128)(2,1)S(1)} %copy-done.4, ...), custom_call_target="tpu_custom_call" | custom-call | flops 352321536 | bytes 917504 | tf_op jit(solution)/shard_map/pallas_call | solution.py:32
  15.6 1.6 %collective-permute-done.6.rest_5_.rest_7_ = bf16[304,128]{1,0:T(8,128)(2,1)S(1)} collective-permute-done((bf16[304,128]{1,0:T(8,128)(2,1)S(1)}, bf16[304,128]{1,0:T(8,128)(2,1)S(1)}, u32[]{:S(2)}, u32[]{:S(2)}) %collective-permute-start.6) | collective-permute-done | bytes 77856 | tf_op jit(solution)/shard_map/ppermute | solution.py:444
  17.2 4.3 %collective-permute-start.8 = (bf16[304,128]{1,0:T(8,128)(2,1)S(1)}, bf16[304,128]{1,0:T(8,128)(2,1)S(1)}, u32[]{:S(2)}, u32[]{:S(2)}) collective-permute-start(bf16[304,128]{1,0:T(8,128)(2,1)S(1)} %collective-permute-done.6.rest_5_.rest_7_), channel_id=1, source_target_pairs={{0,12},{4,0},{8,4},{12,8},{1,13},{5,1},{9,5},{13,9},{2,14},{6,2},{... | collective-permute-start | bytes 233480 | tf_op jit(solution)/shard_map/ppermute | solution.py:444
  21.4 0.0 collective-permute-done.3.rest_2_.rest_4_
  21.4 0.0 collective-permute-start.7
  21.4 0.0 collective-permute-done.4.rest_3_.rest_5_
  21.5 0.0 collective-permute-done.5.rest_4_.rest_6_
  21.5 2.2 %shard_map.112 = (bf16[512,512]{1,0:T(8,128)(2,1)S(1)}, f32[128,512]{1,0:T(8,128)S(1)}, f32[64,512]{1,0:T(8,128)S(1)}) custom-call(s32[8,128]{1,0:T(8,128)S(1)} %get-tuple-element.21.info_ref, bf16[448,256]{1,0:T(8,128)(2,1)S(1)} %get-tuple-element.22.mine_ref, bf16[448,256]{1,0:T(8,128)(2,1)S(1)} %collective-permute-done.theirs_ref, ...), custom_call_target="tpu_custom_call" | custom-call | flops 1056964608 | bytes 917504 | tf_op jit(solution)/shard_map/pallas_call | solution.py:32
  23.6 0.0 collective-permute-done.8.rest_1_
  23.6 4.0 %collective-permute-done.7.rest_0_ = bf16[320,128]{1,0:T(8,128)(2,1)S(1)} collective-permute-done((bf16[320,128]{1,0:T(8,128)(2,1)S(1)}, bf16[320,128]{1,0:T(8,128)(2,1)S(1)}, u32[]{:S(2)}, u32[]{:S(2)}) %collective-permute-start.7) | collective-permute-done | bytes 81952 | tf_op jit(solution)/shard_map/ppermute | solution.py:444
  27.7 12.4 %shard_map.113.mine_att_ref = bf16[48,512]{1,0:T(8,128)(2,1)S(1)} custom-call(s32[8,128]{1,0:T(8,128)S(1)} %get-tuple-element.21.info_ref, f32[128,512]{1,0:T(8,128)S(1)} %get-tuple-element.30.qt_ref, f32[64,512]{1,0:T(8,128)S(1)} %get-tuple-element.31.sum_in_ref, bf16[320,128]{1,0:T(8,128)(2,1)S(1)} %collective-permute-done.7.rest_0_, ...), custom_call_target="tpu_custom_call" | custom-call | flops 352321536 | bytes 917504 | tf_op jit(solution)/shard_map/pallas_call | solution.py:32
  40.1 0.1 collective-permute-start.9
  40.2 1.2 %collective-permute-done.9.their_att_ref = bf16[48,512]{1,0:T(8,128)(2,1)S(1)} collective-permute-done((bf16[48,512]{1,0:T(8,128)(2,1)S(1)}, bf16[48,512]{1,0:T(8,128)(2,1)S(1)}, u32[]{:S(2)}, u32[]{:S(2)}) %collective-permute-start.9) | collective-permute-done | bytes 49184 | tf_op jit(solution)/shard_map/ppermute | solution.py:557
  41.4 1.8 %shard_map.114 = (bf16[448,256]{1,0:T(8,128)(2,1)S(1)}, bf16[448,256]{1,0:T(8,128)(2,1)S(1)}) custom-call(s32[8,128]{1,0:T(8,128)S(1)} %get-tuple-element.21.info_ref, bf16[512,512]{1,0:T(8,128)(2,1)S(1)} %get-tuple-element.29.rows_ref, bf16[48,512]{1,0:T(8,128)(2,1)S(1)} %shard_map.113.mine_att_ref, ...), custom_call_target="tpu_custom_call" | custom-call | flops 318767104 | bytes 917504 | tf_op jit(solution)/shard_map/pallas_call | solution.py:32
  43.2 0.2 collective-permute-start.10
  43.4 0.7 %shard_map.115 = (f32[448,256]{1,0:T(8,128)S(1)}, f32[1,256]{1,0:T(1,128)S(1)}) custom-call(bf16[448,256]{1,0:T(8,128)(2,1)S(1)} %get-tuple-element.32.after_ref, bf16[448,256]{1,0:T(8,128)(2,1)S(1)} %get-tuple-element.33.hidden_ref, bf16[256,512]{1,0:T(8,128)(2,1)S(1)} %copy-done, f32[1,256]{1,0:T(1,128)} %bitcast.11), custom_call_target="tpu_custom_call" | custom-call | flops 58720256 | bytes 458752 | tf_op jit(solution)/shard_map/pallas_call | solution.py:32
  44.1 0.6 %collective-permute-done.10.hidden_ref = bf16[448,256]{1,0:T(8,128)(2,1)S(1)} collective-permute-done((bf16[448,256]{1,0:T(8,128)(2,1)S(1)}, bf16[448,256]{1,0:T(8,128)(2,1)S(1)}, u32[]{:S(2)}, u32[]{:S(2)}) %collective-permute-start.10) | collective-permute-done | bytes 229408 | tf_op jit(solution)/shard_map/ppermute | solution.py:570
  44.8 1.6 %shard_map.116 = bf16[1792,256]{1,0:T(8,128)(2,1)} custom-call(s32[8,128]{1,0:T(8,128)S(1)} %get-tuple-element.21.info_ref, f32[448,256]{1,0:T(8,128)S(1)} %get-tuple-element.34.base_ref, bf16[448,256]{1,0:T(8,128)(2,1)S(1)} %collective-permute-done.10.hidden_ref, bf16[256,512]{1,0:T(8,128)(2,1)S(1)} %collective-permute-done.2.rest_1_.out_w_ref, ...), custom_call_target="tpu_custom_call" | custom-call | flops 58720256 | bytes 1835008 | tf_op jit(solution)/shard_map/pallas_call | solution.py:32
Async XLA Ops:
  0.7 2.1 %copy-start = (bf16[256,512]{1,0:T(8,128)(2,1)S(1)}, bf16[256,512]{1,0:T(8,128)(2,1)}, u32[]{:S(2)}) copy-start(bf16[256,512]{1,0:T(8,128)(2,1)} %out_w_ref.1) | copy-start | bytes 786436
  0.7 2.2 %copy-start.1 = (bf16[48,512]{1,0:T(8,128)(2,1)S(1)}, bf16[48,512]{1,0:T(8,128)(2,1)}, u32[]{:S(2)}) copy-start(bf16[48,512]{1,0:T(8,128)(2,1)} %mine_out_ref.1) | copy-start | bytes 147460
  0.7 3.2 %copy-start.3 = (bf16[512,128]{1,0:T(8,128)(2,1)S(1)}, bf16[512,128]{1,0:T(8,128)(2,1)}, u32[]{:S(2)}) copy-start(bf16[512,128]{1,0:T(8,128)(2,1)} %wk_ref.1) | copy-start | bytes 393220
  0.7 3.2 %copy-start.5 = (bf16[512,48]{0,1:T(8,128)(2,1)S(1)}, bf16[512,48]{0,1:T(8,128)(2,1)}, u32[]{:S(2)}) copy-start(bf16[512,48]{0,1:T(8,128)(2,1)} %param.16) | copy-start | bytes 147460
  2.2 11.0 %copy-start.6 = (bf16[512,2,256]{2,1,0:T(2,128)(2,1)S(1)}, bf16[512,2,256]{2,1,0:T(2,128)(2,1)}, u32[]{:S(2)}) copy-start(bf16[512,2,256]{2,1,0:T(2,128)(2,1)} %param.18) | copy-start | bytes 1572868
  2.2 1.7 %collective-permute-start = (bf16[448,256]{1,0:T(8,128)(2,1)S(1)}, bf16[448,256]{1,0:T(8,128)(2,1)S(1)}, u32[]{:S(2)}, u32[]{:S(2)}) collective-permute-start(bf16[448,256]{1,0:T(8,128)(2,1)S(1)} %get-tuple-element.22.mine_ref), channel_id=1, source_target_pairs={{0,1},{1,0},{2,3},{3,2},{4,5},{5,4},{6,7},{7,6},{8,9},{9,8},{10,11... | collective-permute-start | bytes 688136 | tf_op jit(solution)/shard_map/ppermute | solution.py:466
  2.8 10.5 %collective-permute-start.2 = (bf16[256,512]{1,0:T(8,128)(2,1)S(1)}, bf16[256,512]{1,0:T(8,128)(2,1)S(1)}, u32[]{:S(2)}, u32[]{:S(2)}) collective-permute-start(bf16[256,512]{1,0:T(8,128)(2,1)S(1)} %copy-done), channel_id=1, source_target_pairs={{0,1},{1,0},{2,3},{3,2},{4,5},{5,4},{6,7},{7,6},{8,9},{9,8},{10,11... | collective-permute-start | bytes 786440 | tf_op jit(solution)/shard_map/ppermute | solution.py:493
  2.9 6.5 %collective-permute-start.1 = (bf16[48,512]{1,0:T(8,128)(2,1)S(1)}, bf16[48,512]{1,0:T(8,128)(2,1)S(1)}, u32[]{:S(2)}, u32[]{:S(2)}) collective-permute-start(bf16[48,512]{1,0:T(8,128)(2,1)S(1)} %copy-done.1), channel_id=1, source_target_pairs={{0,1},{1,0},{2,3},{3,2},{4,5},{5,4},{6,7},{7,6},{8,9},{9,8},{10,11... | collective-permute-start | bytes 147464 | tf_op jit(solution)/shard_map/ppermute | solution.py:492
  4.3 17.1 %collective-permute-start.5 = (bf16[384,128]{1,0:T(8,128)(2,1)S(1)}, bf16[384,128]{1,0:T(8,128)(2,1)S(1)}, u32[]{:S(2)}, u32[]{:S(2)}) collective-permute-start(bf16[384,128]{1,0:T(8,128)(2,1)S(1)} %get-tuple-element.28), channel_id=1, source_target_pairs={{0,12},{4,0},{8,4},{12,8},{1,13},{5,1},{9,5},{13,9},{2,14},{6,2},{... | collective-permute-start | bytes 294920 | tf_op jit(solution)/shard_map/ppermute | solution.py:444
  9.3 12.1 %collective-permute-start.4 = (bf16[368,128]{1,0:T(8,128)(2,1)S(1)}, bf16[368,128]{1,0:T(8,128)(2,1)S(1)}, u32[]{:S(2)}, u32[]{:S(2)}) collective-permute-start(bf16[368,128]{1,0:T(8,128)(2,1)S(1)} %get-tuple-element.27), channel_id=1, source_target_pairs={{0,4},{4,8},{8,12},{12,0},{1,5},{5,9},{9,13},{13,1},{2,6},{6,10},{... | collective-permute-start | bytes 282632 | tf_op jit(solution)/shard_map/ppermute | solution.py:444
  9.3 12.1 %collective-permute-start.3 = (bf16[320,128]{1,0:T(8,128)(2,1)S(1)}, bf16[320,128]{1,0:T(8,128)(2,1)S(1)}, u32[]{:S(2)}, u32[]{:S(2)}) collective-permute-start(bf16[320,128]{1,0:T(8,128)(2,1)S(1)} %get-tuple-element.23.first_ref.rest_0_.rest_2_), channel_id=1, source_target_pairs={{0,4},{4,8},{8,12},{12,0},{1,5},{5,9},{9,13},{13,1},{2,6},{6,10},{... | collective-permute-start | bytes 245768 | tf_op jit(solution)/shard_map/ppermute | solution.py:444
  9.3 7.8 %collective-permute-start.6 = (bf16[304,128]{1,0:T(8,128)(2,1)S(1)}, bf16[304,128]{1,0:T(8,128)(2,1)S(1)}, u32[]{:S(2)}, u32[]{:S(2)}) collective-permute-start(bf16[304,128]{1,0:T(8,128)(2,1)S(1)} %get-tuple-element.24.second_ref.rest_1_.rest_3_), channel_id=1, source_target_pairs={{0,12},{4,0},{8,4},{12,8},{1,13},{5,1},{9,5},{13,9},{2,14},{6,2},{... | collective-permute-start | bytes 233480 | tf_op jit(solution)/shard_map/ppermute | solution.py:444
  13.2 0.8 %copy-start.2 = (f32[31,256]{1,0:T(8,128)S(1)}, f32[31,256]{1,0:T(8,128)}, u32[]{:S(2)}) copy-start(f32[31,256]{1,0:T(8,128)} %taps_ref.1) | copy-start | bytes 95236
  13.2 0.9 %copy-start.4 = (bf16[512,128]{1,0:T(8,128)(2,1)S(1)}, bf16[512,128]{1,0:T(8,128)(2,1)}, u32[]{:S(2)}) copy-start(bf16[512,128]{1,0:T(8,128)(2,1)} %wq_ref.3) | copy-start | bytes 393220
  17.2 6.5 %collective-permute-start.8 = (bf16[304,128]{1,0:T(8,128)(2,1)S(1)}, bf16[304,128]{1,0:T(8,128)(2,1)S(1)}, u32[]{:S(2)}, u32[]{:S(2)}) collective-permute-start(bf16[304,128]{1,0:T(8,128)(2,1)S(1)} %collective-permute-done.6.rest_5_.rest_7_), channel_id=1, source_target_pairs={{0,12},{4,0},{8,4},{12,8},{1,13},{5,1},{9,5},{13,9},{2,14},{6,2},{... | collective-permute-start | bytes 233480 | tf_op jit(solution)/shard_map/ppermute | solution.py:444
  21.4 6.2 %collective-permute-start.7 = (bf16[320,128]{1,0:T(8,128)(2,1)S(1)}, bf16[320,128]{1,0:T(8,128)(2,1)S(1)}, u32[]{:S(2)}, u32[]{:S(2)}) collective-permute-start(bf16[320,128]{1,0:T(8,128)(2,1)S(1)} %collective-permute-done.3.rest_2_.rest_4_), channel_id=1, source_target_pairs={{0,4},{4,8},{8,12},{12,0},{1,5},{5,9},{9,13},{13,1},{2,6},{6,10},{... | collective-permute-start | bytes 245768 | tf_op jit(solution)/shard_map/ppermute | solution.py:444
  40.1 1.3 %collective-permute-start.9 = (bf16[48,512]{1,0:T(8,128)(2,1)S(1)}, bf16[48,512]{1,0:T(8,128)(2,1)S(1)}, u32[]{:S(2)}, u32[]{:S(2)}) collective-permute-start(bf16[48,512]{1,0:T(8,128)(2,1)S(1)} %shard_map.113.mine_att_ref), channel_id=1, source_target_pairs={{0,1},{1,0},{2,3},{3,2},{4,5},{5,4},{6,7},{7,6},{8,9},{9,8},{10,11... | collective-permute-start | bytes 147464 | tf_op jit(solution)/shard_map/ppermute | solution.py:557
  43.2 1.6 %collective-permute-start.10 = (bf16[448,256]{1,0:T(8,128)(2,1)S(1)}, bf16[448,256]{1,0:T(8,128)(2,1)S(1)}, u32[]{:S(2)}, u32[]{:S(2)}) collective-permute-start(bf16[448,256]{1,0:T(8,128)(2,1)S(1)} %get-tuple-element.33.hidden_ref), channel_id=1, source_target_pairs={{0,1},{1,0},{2,3},{3,2},{4,5},{5,4},{6,7},{7,6},{8,9},{9,8},{10,11... | collective-permute-start | bytes 688136 | tf_op jit(solution)/shard_map/ppermute | solution.py:570

commit v5 on v4

--- a/solution.py
+++ b/solution.py
@@ -53,7 +53,10 @@
     return mine, theirs
 
 
-def down_kernel(parts, len_ref, frames_ref, weights_hbm, out_ref, info_ref, raw, wide, weights_ref, sems):
+def down_kernel(
+    parts, len_ref, frames_ref, weights_hbm, key_hbm, value_hbm, query_hbm,
+    out_ref, info_ref, raw, key_ref, value_ref, query_ref, wide, weights_ref, sems,
+):
     frame_count, channels = raw.shape
     tiles = channels // 128
     step = frame_count // parts
@@ -67,6 +70,13 @@
     weights_copy = pltpu.make_async_copy(weights_hbm, weights_ref, sems.at[parts])
     weights_copy.start()
     for copy in copies:
+        copy.start()
+    later = [
+        pltpu.make_async_copy(key_hbm, key_ref, sems.at[parts + 1]),
+        pltpu.make_async_copy(value_hbm, value_ref, sems.at[parts + 2]),
+        pltpu.make_async_copy(query_hbm, query_ref, sems.at[parts + 3]),
+    ]
+    for copy in later:
         copy.start()
     length = len_ref[0]
     live_rows = lax.shift_right_logical(length + 3, 2)
@@ -87,6 +97,8 @@
                 part = jnp.where(row + j < length, part, 0.0) * weights_ref[j : j + 1, lanes]
                 total = part if total is None else total + part
             out_ref[i * rows : (i + 1) * rows, lanes] = total.astype(BF16)
+    for copy in later:
+        copy.wait()
 
 
 def pack_plan(quarter, width):
@@ -233,23 +245,28 @@
     return jnp.transpose(query * (math.log2(math.e) / math.sqrt(QDIM)))
 
 
-def own_kernel(heads, info_ref, mine_ref, theirs_ref, wq_ref, first_ref, second_ref, *rest):
-    qt_ref, sum_ref = rest[-2:]
+def query_kernel(mine_ref, theirs_ref, wq_ref, qt_ref):
     quarter, channels = mine_ref.shape
     queries = qt_ref.shape[1]
     blank = jnp.zeros((queries - quarter, channels), BF16)
-    q_t = scaled_queries(
+    qt_ref[...] = scaled_queries(
         jnp.concatenate([mine_ref[...], blank], axis=0),
         jnp.concatenate([theirs_ref[...], blank], axis=0),
         wq_ref,
         channels,
     )
-    qt_ref[...] = q_t
+
+
+def own_kernel(heads, quarter, info_ref, qt_ref, first_ref, second_ref, bypass_hbm, *rest):
+    sum_ref, bypass_ref, sem = rest[-3:]
+    copy = pltpu.make_async_copy(bypass_hbm, bypass_ref, sem.at[0])
+    copy.start()
     total = absorb(
-        None, q_t, [(first_ref, second_ref)], sources_of([0]), info_ref[0:1, 0:1], quarter, heads
+        None, qt_ref[...], [(first_ref, second_ref)], sources_of([0]), info_ref[0:1, 0:1], quarter, heads
     )
     lane = lax.broadcasted_iota(jnp.int32, total.shape, 1)
     sum_ref[...] = jnp.where(lane < quarter, total, 0.0)
+    copy.wait()
 
 
 def open_kernel(heads, halo, shifts, info_ref, mine_ref, theirs_ref, wq_ref, qt_in_ref, sum_in_ref, *rest):
@@ -378,17 +395,20 @@
             hidden_ref[base : base + block, lanes] = (total * jax.nn.sigmoid(total)).astype(BF16)
 
 
-def half_kernel(after_ref, hidden_ref, out_w_ref, bypass_hbm, base_ref, bypass_ref, sem):
-    copy = pltpu.make_async_copy(bypass_hbm, bypass_ref, sem.at[0])
-    copy.start()
-    channels = hidden_ref.shape[1]
+def half_kernel(info_ref, after_ref, hidden_ref, out_w_ref, frames_ref, bypass_ref, base_ref, kept_ref):
+    quarter, channels = hidden_ref.shape
     mine, _ = halves(channels)
     base_ref[...] = after_ref[...].astype(F32) + dot(hidden_ref[...], out_w_ref[:, mine])
-    copy.wait()
+    row = lax.broadcasted_iota(jnp.int32, (4 * quarter, 128), 0) + lax.axis_index("tm") * 4 * quarter
+    live = row < info_ref[1:2, 0:1]
+    for tile in range(channels // 128):
+        lanes = slice(tile * 128, tile * 128 + 128)
+        backdrop = frames_ref[:, lanes].astype(F32)
+        kept_ref[tile] = jnp.where(live, backdrop - bypass_ref[:, lanes] * backdrop, 0.0)
 
 
 def last_kernel(
-    parts, info_ref, base_ref, hidden_ref, out_w_ref, frames_ref, bypass_ref, out_ref, tall, flat, sems
+    parts, info_ref, base_ref, hidden_ref, out_w_ref, kept_ref, bypass_ref, out_ref, tall, flat, sems
 ):
     quarter, channels = base_ref.shape
     rows = quarter // parts
@@ -401,15 +421,14 @@
     for i in range(parts):
         part = slice(i * rows, (i + 1) * rows)
         span = slice(i * step, (i + 1) * step)
-        stacked = base_ref[part, :] + dot(hidden_ref[part, :], weights)
-        live = row + i * step < length
+        stacked = bypass_ref[...] * (base_ref[part, :] + dot(hidden_ref[part, :], weights))
+        live = row < length - i * step
         for tile in range(channels // 128):
             lanes = slice(tile * 128, tile * 128 + 128)
             for j in range(4):
                 tall[tile, pl.ds(i * step + j, rows, stride=4), :] = stacked[:, lanes]
-            backdrop = frames_ref[span, lanes].astype(F32)
-            result = backdrop + bypass_ref[:, lanes] * (tall[tile, span] - backdrop)
-            flat[span, lanes] = jnp.where(live, result, 0.0).astype(BF16)
+            added = jnp.where(live, tall[tile, span], 0.0)
+            flat[span, lanes] = (kept_ref[tile, span] + added).astype(BF16)
         window = pl.ds(i * step, step)
         copies.append(pltpu.make_async_copy(flat.at[window], out_ref.at[window], sems.at[i]))
         copies[-1].start()
@@ -437,6 +456,7 @@
     count = lax.axis_size("tm")
     halo = -(-(conv_taps.shape[0] // 2) // 16) * 16
     queries = -(-(quarter + 2 * halo) // 128) * 128
+    parts = quarter // 64
     frames = frames.reshape(frame_count, channels)
     swap = [(0, 1), (1, 0)]
 
@@ -446,19 +466,22 @@
     def vmem(shape, dtype):
         return pltpu.VMEM(shape, dtype)
 
-    reduced, info, kept_frames = call(
-        functools.partial(down_kernel, 4),
+    reduced, info, kept_frames, kept_key, kept_value, kept_query = call(
+        functools.partial(down_kernel, parts),
         [
             vmem((quarter, channels), BF16),
             vmem((8, 128), jnp.int32),
             vmem((frame_count, channels), BF16),
+            vmem(w_key.shape, BF16),
+            vmem(w_value.shape[::-1], BF16),
+            vmem(w_query.shape, BF16),
         ],
-        [lengths, frames, down_weights],
-        [SM, HB, HB],
+        [lengths, frames, down_weights, w_key, w_value.T, w_query],
+        [SM, HB, HB, HB, HB, HB],
         [
             pltpu.VMEM((channels // 128, frame_count, 128), F32),
             pltpu.VMEM(down_weights.shape, F32),
-            pltpu.SemaphoreType.DMA((5,)),
+            pltpu.SemaphoreType.DMA((parts + 4,)),
         ],
         flops=8 * frame_count * channels,
         moved=3 * frame_count * channels,
@@ -475,7 +498,7 @@
             vmem((first_rows + edge_rows, keys_wide), BF16),
             vmem((second_rows + edge_rows, keys_wide), BF16),
         ],
-        [reduced, theirs, w_key, w_value.T],
+        [reduced, theirs, kept_key, kept_value],
         [VM] * 4,
         flops=4 * quarter * channels * (keys_wide + width),
         moved=8 * quarter * channels,
@@ -507,11 +530,20 @@
     def shifts(stage):
         return [pack[0] for pack in stage]
 
-    q_t, total = call(
-        functools.partial(own_kernel, heads),
-        [vmem((keys_wide, queries), F32), vmem((width + 16, queries), F32)],
-        [info, reduced, theirs, w_query, first, second] + early,
-        [VM] * (6 + len(early)),
+    (q_t,) = call(
+        query_kernel,
+        [vmem((keys_wide, queries), F32)],
+        [reduced, theirs, kept_query],
+        [VM] * 3,
+        flops=4 * quarter * channels * keys_wide,
+        moved=4 * quarter * channels,
+    )
+    total, bypass_row = call(
+        functools.partial(own_kernel, heads, quarter),
+        [vmem((width + 16, queries), F32), vmem((1, channels), F32)],
+        [info, q_t, first, second, bypass.reshape(1, channels)] + early,
+        [VM] * 4 + [HB] + [VM] * len(early),
+        [pltpu.SemaphoreType.DMA((1,))],
         flops=score_flops,
         moved=quarter * queries * 4,
         exps=quarter * queries * heads,
@@ -523,7 +555,7 @@
             vmem((keys_wide, queries), F32),
             vmem((width + 16, queries), F32),
         ],
-        [info, reduced, theirs, w_query, q_t, total] + arrays(stages[0]),
+        [info, reduced, theirs, kept_query, q_t, total] + arrays(stages[0]),
         [VM] * (6 + 2 * len(stages[0])),
         flops=score_flops * len(stages[0]),
         moved=quarter * queries * 4,
@@ -568,24 +600,23 @@
         moved=quarter * channels * 8,
     )
     their_hidden = lax.ppermute(hidden, "head", swap)
-    base, kept_bypass = call(
+    base, kept = call(
         half_kernel,
-        [vmem((quarter, channels), F32), vmem((1, channels), F32)],
-        [after, hidden, conv_out, bypass.reshape(1, channels)],
-        [VM, VM, VM, HB],
-        [pltpu.SemaphoreType.DMA((1,))],
+        [vmem((quarter, channels), F32), vmem((channels // 128, frame_count, 128), F32)],
+        [info, after, hidden, conv_out, kept_frames, bypass_row],
+        [VM] * 6,
         flops=2 * quarter * channels * channels,
         moved=quarter * channels * 4,
     )
     (out,) = call(
-        functools.partial(last_kernel, 4),
+        functools.partial(last_kernel, parts),
         [jax.ShapeDtypeStruct((frame_count, channels), BF16)],
-        [info, base, their_hidden, their_conv_out, kept_frames, kept_bypass],
+        [info, base, their_hidden, their_conv_out, kept, bypass_row],
         [VM] * 6,
         [
             pltpu.VMEM((channels // 128, frame_count, 128), F32),
             pltpu.VMEM((frame_count, channels), BF16),
-            pltpu.SemaphoreType.DMA((4,)),
+            pltpu.SemaphoreType.DMA((parts,)),
         ],
         out_specs=[HB],
         flops=2 * quarter * channels * channels,

time: 46.5 us -> 46.3 us (level)
  local copies, waits for them, and re-layouts: 0.93 us -> 0.1 us
  waiting for transfers between devices: 8.09 us -> 8.88 us
    ppermute x6, waiting for transfers between devices: 5.64 us -> 6.57 us  [ring(): lax.ppermute(array, 'tm', [(i, (i + by) % count) for i in range(count)])]
    unnamed x15 -> x9, local copies, waits for them, and re-layouts: 0.93 us -> 0.1 us
    pallas_call x8 -> x9, Pallas kernels: 22 us -> 21.8 us  [call(): pl.pallas_call(kernel, out_shape=outs, in_specs=specs, out_specs=out_spec...]
where the time goes in v5:
time: 46.3 us; the launch traced here: 46.1 us
  Pallas kernels  21.8 us (47%)
  starting transfers between devices  14.5 us (31%)
  waiting for transfers between devices  8.88 us (19%)
  between operations  0.86 us (2%)
    pallas_call x9, Pallas kernels, call(): pl.pallas_call(kernel, out_shape=outs, in_specs=specs, out_specs=out_spec...  21.8 us
    ppermute x6, starting transfers between devices, ring(): lax.ppermute(array, 'tm', [(i, (i + by) % count) for i in range(count)])  13.1 us
    ppermute x6, waiting for transfers between devices, ring(): lax.ppermute(array, 'tm', [(i, (i + by) % count) for i in range(count)])  6.57 us
    ppermute x1, waiting for transfers between devices, shards(): their_attended = lax.ppermute(attended, 'head', swap)  1.22 us
  transfers between devices with their start and end apart: 11, of which 5 were waited for; matrix products, arithmetic and copies ran while one was open for 0% of the time, Pallas kernels for 10%

profile of v5, /device:TPU:0, one launch (start us, length us, event | category | flops | bytes accessed | tf_op | source)
XLA Modules:
  0.0 46.1 jit_solution(4145639354251233887)
XLA Ops:
  0.0 0.0 copy-start.3
  0.7 0.0 copy-start
  0.7 0.0 copy-start.1
  0.7 0.0 copy-start.2
  0.7 1.5 %shard_map.109 = (bf16[448,256]{1,0:T(8,128)(2,1)S(1)}, s32[8,128]{1,0:T(8,128)S(1)}, bf16[1792,256]{1,0:T(8,128)(2,1)S(1)}, bf16[512,128]{1,0:T(8,128)(2,1)S(1)...) custom-call(s32[1]{0:T(128)S(6)} %copy.13.len_ref, bf16[1792,256]{1,0:T(8,128)(2,1)} %bitcast.8, ...), custom_call_target="tpu_custom_call" | custom-call | flops 3670016 | bytes 1376256 | tf_op jit(solution)/shard_map/pallas_call | solution.py:32
  2.3 0.6 %collective-permute-start = (bf16[448,256]{1,0:T(8,128)(2,1)S(1)}, bf16[448,256]{1,0:T(8,128)(2,1)S(1)}, u32[]{:S(2)}, u32[]{:S(2)}) collective-permute-start(bf16[448,256]{1,0:T(8,128)(2,1)S(1)} %get-tuple-element.25.mine_ref), channel_id=1, source_target_pairs={{0,1},{1,0},{2,3},{3,2},{4,5},{5,4},{6,7},{7,6},{8,9},{9,8},{10,11... | collective-permute-start | bytes 688136 | tf_op jit(solution)/shard_map/ppermute | solution.py:489
  2.8 0.1 collective-permute-start.2
  2.9 0.4 collective-permute-start.1
  3.3 0.6 %collective-permute-done.theirs_ref = bf16[448,256]{1,0:T(8,128)(2,1)S(1)} collective-permute-done((bf16[448,256]{1,0:T(8,128)(2,1)S(1)}, bf16[448,256]{1,0:T(8,128)(2,1)S(1)}, u32[]{:S(2)}, u32[]{:S(2)}) %collective-permute-start) | collective-permute-done | bytes 229408 | tf_op jit(solution)/shard_map/ppermute | solution.py:489
  3.9 0.4 shard_map.111
  4.4 5.0 %collective-permute-start.5 = (bf16[384,128]{1,0:T(8,128)(2,1)S(1)}, bf16[384,128]{1,0:T(8,128)(2,1)S(1)}, u32[]{:S(2)}, u32[]{:S(2)}) collective-permute-start(bf16[384,128]{1,0:T(8,128)(2,1)S(1)} %get-tuple-element.33), channel_id=1, source_target_pairs={{0,12},{4,0},{8,4},{12,8},{1,13},{5,1},{9,5},{13,9},{2,14},{6,2},{... | collective-permute-start | bytes 294920 | tf_op jit(solution)/shard_map/ppermute | solution.py:464
  9.3 0.0 collective-permute-start.4
  9.4 0.0 collective-permute-start.3
  9.4 0.0 collective-permute-done.1.rest_0_.their_out_ref
  9.4 3.8 %collective-permute-start.6 = (bf16[304,128]{1,0:T(8,128)(2,1)S(1)}, bf16[304,128]{1,0:T(8,128)(2,1)S(1)}, u32[]{:S(2)}, u32[]{:S(2)}) collective-permute-start(bf16[304,128]{1,0:T(8,128)(2,1)S(1)} %get-tuple-element.30.second_ref.rest_1_.rest_3_), channel_id=1, source_target_pairs={{0,12},{4,0},{8,4},{12,8},{1,13},{5,1},{9,5},{13,9},{2,14},{6,2},{... | collective-permute-start | bytes 233480 | tf_op jit(solution)/shard_map/ppermute | solution.py:464
  13.2 0.0 copy-done.3
  13.2 0.1 copy.12
  13.3 0.4 shard_map.110.qt_ref.qt_in_ref
  13.7 0.0 collective-permute-done.2.rest_1_.out_w_ref
  13.7 0.0 copy-done
  13.7 0.0 copy-done.1
  13.7 0.0 copy-done.2
  13.7 1.0 %shard_map.112 = (f32[64,512]{1,0:T(8,128)S(1)}, f32[1,256]{1,0:T(1,128)S(1)}) custom-call(s32[8,128]{1,0:T(8,128)S(1)} %get-tuple-element.24.info_ref, f32[128,512]{1,0:T(8,128)S(1)} %shard_map.110.qt_ref.qt_in_ref, bf16[320,128]{1,0:T(8,128)(2,1)S(1)} %get-tuple-element.29.first_ref.rest_0_.rest_2_, ...), custom_call_target="tpu_custom_call" | custom-call | flops 352321536 | bytes 917504 | tf_op jit(solution)/shard_map/pallas_call | solution.py:32
  14.7 2.5 %collective-permute-done.6.rest_5_.rest_7_ = bf16[304,128]{1,0:T(8,128)(2,1)S(1)} collective-permute-done((bf16[304,128]{1,0:T(8,128)(2,1)S(1)}, bf16[304,128]{1,0:T(8,128)(2,1)S(1)}, u32[]{:S(2)}, u32[]{:S(2)}) %collective-permute-start.6) | collective-permute-done | bytes 77856 | tf_op jit(solution)/shard_map/ppermute | solution.py:464
  17.2 4.3 %collective-permute-start.8 = (bf16[304,128]{1,0:T(8,128)(2,1)S(1)}, bf16[304,128]{1,0:T(8,128)(2,1)S(1)}, u32[]{:S(2)}, u32[]{:S(2)}) collective-permute-start(bf16[304,128]{1,0:T(8,128)(2,1)S(1)} %collective-permute-done.6.rest_5_.rest_7_), channel_id=1, source_target_pairs={{0,12},{4,0},{8,4},{12,8},{1,13},{5,1},{9,5},{13,9},{2,14},{6,2},{... | collective-permute-start | bytes 233480 | tf_op jit(solution)/shard_map/ppermute | solution.py:464
  21.5 0.0 collective-permute-done.3.rest_2_.rest_4_
  21.5 0.0 collective-permute-start.7
  21.5 0.0 collective-permute-done.4.rest_3_.rest_5_
  21.5 0.0 collective-permute-done.5.rest_4_.rest_6_
  21.5 2.2 %shard_map.113 = (bf16[512,512]{1,0:T(8,128)(2,1)S(1)}, f32[128,512]{1,0:T(8,128)S(1)}, f32[64,512]{1,0:T(8,128)S(1)}) custom-call(s32[8,128]{1,0:T(8,128)S(1)} %get-tuple-element.24.info_ref, bf16[448,256]{1,0:T(8,128)(2,1)S(1)} %get-tuple-element.25.mine_ref, bf16[448,256]{1,0:T(8,128)(2,1)S(1)} %collective-permute-done.theirs_ref, ...), custom_call_target="tpu_custom_call" | custom-call | flops 1056964608 | bytes 917504 | tf_op jit(solution)/shard_map/pallas_call | solution.py:32
  23.6 0.0 collective-permute-done.8.rest_1_
  23.7 4.0 %collective-permute-done.7.rest_0_ = bf16[320,128]{1,0:T(8,128)(2,1)S(1)} collective-permute-done((bf16[320,128]{1,0:T(8,128)(2,1)S(1)}, bf16[320,128]{1,0:T(8,128)(2,1)S(1)}, u32[]{:S(2)}, u32[]{:S(2)}) %collective-permute-start.7) | collective-permute-done | bytes 81952 | tf_op jit(solution)/shard_map/ppermute | solution.py:464
  27.7 12.4 %shard_map.114.mine_att_ref = bf16[48,512]{1,0:T(8,128)(2,1)S(1)} custom-call(s32[8,128]{1,0:T(8,128)S(1)} %get-tuple-element.24.info_ref, f32[128,512]{1,0:T(8,128)S(1)} %get-tuple-element.35.qt_ref, f32[64,512]{1,0:T(8,128)S(1)} %get-tuple-element.36.sum_in_ref, bf16[320,128]{1,0:T(8,128)(2,1)S(1)} %collective-permute-done.7.rest_0_, ...), custom_call_target="tpu_custom_call" | custom-call | flops 352321536 | bytes 917504 | tf_op jit(solution)/shard_map/pallas_call | solution.py:32
  40.2 0.1 collective-permute-start.9
  40.2 1.2 %collective-permute-done.9.their_att_ref = bf16[48,512]{1,0:T(8,128)(2,1)S(1)} collective-permute-done((bf16[48,512]{1,0:T(8,128)(2,1)S(1)}, bf16[48,512]{1,0:T(8,128)(2,1)S(1)}, u32[]{:S(2)}, u32[]{:S(2)}) %collective-permute-start.9) | collective-permute-done | bytes 49184 | tf_op jit(solution)/shard_map/ppermute | solution.py:589
  41.4 1.8 %shard_map.115 = (bf16[448,256]{1,0:T(8,128)(2,1)S(1)}, bf16[448,256]{1,0:T(8,128)(2,1)S(1)}) custom-call(s32[8,128]{1,0:T(8,128)S(1)} %get-tuple-element.24.info_ref, bf16[512,512]{1,0:T(8,128)(2,1)S(1)} %get-tuple-element.34.rows_ref, bf16[48,512]{1,0:T(8,128)(2,1)S(1)} %shard_map.114.mine_att_ref, ...), custom_call_target="tpu_custom_call" | custom-call | flops 318767104 | bytes 917504 | tf_op jit(solution)/shard_map/pallas_call | solution.py:32
  43.2 0.2 collective-permute-start.10
  43.5 0.8 %shard_map.116 = (f32[448,256]{1,0:T(8,128)S(1)}, f32[2,1792,128]{2,1,0:T(8,128)S(1)}) custom-call(s32[8,128]{1,0:T(8,128)S(1)} %get-tuple-element.24.info_ref, bf16[448,256]{1,0:T(8,128)(2,1)S(1)} %get-tuple-element.37.after_ref, bf16[448,256]{1,0:T(8,128)(2,1)S(1)} %get-tuple-element.38.hidden_ref, bf16[256,512]{1,0:T(8,128)(2,1)S(1)} %copy-done, ...), custom_call_target="tpu_custom_call" | custom-call | flops 58720256 | bytes 458752 | tf_op jit(solution)/shard_map/pallas_call | solution.py:32
  44.3 0.5 %collective-permute-done.10.hidden_ref = bf16[448,256]{1,0:T(8,128)(2,1)S(1)} collective-permute-done((bf16[448,256]{1,0:T(8,128)(2,1)S(1)}, bf16[448,256]{1,0:T(8,128)(2,1)S(1)}, u32[]{:S(2)}, u32[]{:S(2)}) %collective-permute-start.10) | collective-permute-done | bytes 229408 | tf_op jit(solution)/shard_map/ppermute | solution.py:602
  44.8 1.3 %shard_map.117 = bf16[1792,256]{1,0:T(8,128)(2,1)} custom-call(s32[8,128]{1,0:T(8,128)S(1)} %get-tuple-element.24.info_ref, f32[448,256]{1,0:T(8,128)S(1)} %get-tuple-element.41.base_ref, bf16[448,256]{1,0:T(8,128)(2,1)S(1)} %collective-permute-done.10.hidden_ref, bf16[256,512]{1,0:T(8,128)(2,1)S(1)} %collective-permute-done.2.rest_1_.out_w_ref, ...), custom_call_target="tpu_custom_call" | custom-call | flops 58720256 | bytes 1835008 | tf_op jit(solution)/shard_map/pallas_call | solution.py:32
Async XLA Ops:
  0.0 13.2 %copy-start.3 = (bf16[512,2,256]{2,1,0:T(2,128)(2,1)S(1)}, bf16[512,2,256]{2,1,0:T(2,128)(2,1)}, u32[]{:S(2)}) copy-start(bf16[512,2,256]{2,1,0:T(2,128)(2,1)} %param.18) | copy-start | bytes 1572868
  0.7 13.0 %copy-start = (bf16[256,512]{1,0:T(8,128)(2,1)S(1)}, bf16[256,512]{1,0:T(8,128)(2,1)}, u32[]{:S(2)}) copy-start(bf16[256,512]{1,0:T(8,128)(2,1)} %out_w_ref.1) | copy-start | bytes 786436
  0.7 13.0 %copy-start.1 = (bf16[48,512]{1,0:T(8,128)(2,1)S(1)}, bf16[48,512]{1,0:T(8,128)(2,1)}, u32[]{:S(2)}) copy-start(bf16[48,512]{1,0:T(8,128)(2,1)} %mine_out_ref.1) | copy-start | bytes 147460
  0.7 13.0 %copy-start.2 = (f32[31,256]{1,0:T(8,128)S(1)}, f32[31,256]{1,0:T(8,128)}, u32[]{:S(2)}) copy-start(f32[31,256]{1,0:T(8,128)} %taps_ref.1) | copy-start | bytes 95236
  2.3 1.7 %collective-permute-start = (bf16[448,256]{1,0:T(8,128)(2,1)S(1)}, bf16[448,256]{1,0:T(8,128)(2,1)S(1)}, u32[]{:S(2)}, u32[]{:S(2)}) collective-permute-start(bf16[448,256]{1,0:T(8,128)(2,1)S(1)} %get-tuple-element.25.mine_ref), channel_id=1, source_target_pairs={{0,1},{1,0},{2,3},{3,2},{4,5},{5,4},{6,7},{7,6},{8,9},{9,8},{10,11... | collective-permute-start | bytes 688136 | tf_op jit(solution)/shard_map/ppermute | solution.py:489
  2.8 10.9 %collective-permute-start.2 = (bf16[256,512]{1,0:T(8,128)(2,1)}, bf16[256,512]{1,0:T(8,128)(2,1)S(1)}, u32[]{:S(2)}, u32[]{:S(2)}) collective-permute-start(bf16[256,512]{1,0:T(8,128)(2,1)} %out_w_ref.1), channel_id=1, source_target_pairs={{0,1},{1,0},{2,3},{3,2},{4,5},{5,4},{6,7},{7,6},{8,9},{9,8},{10,11... | collective-permute-start | bytes 786440 | tf_op jit(solution)/shard_map/ppermute | solution.py:516
  2.9 6.5 %collective-permute-start.1 = (bf16[48,512]{1,0:T(8,128)(2,1)}, bf16[48,512]{1,0:T(8,128)(2,1)S(1)}, u32[]{:S(2)}, u32[]{:S(2)}) collective-permute-start(bf16[48,512]{1,0:T(8,128)(2,1)} %mine_out_ref.1), channel_id=1, source_target_pairs={{0,1},{1,0},{2,3},{3,2},{4,5},{5,4},{6,7},{7,6},{8,9},{9,8},{10,11... | collective-permute-start | bytes 147464 | tf_op jit(solution)/shard_map/ppermute | solution.py:515
  4.4 17.1 %collective-permute-start.5 = (bf16[384,128]{1,0:T(8,128)(2,1)S(1)}, bf16[384,128]{1,0:T(8,128)(2,1)S(1)}, u32[]{:S(2)}, u32[]{:S(2)}) collective-permute-start(bf16[384,128]{1,0:T(8,128)(2,1)S(1)} %get-tuple-element.33), channel_id=1, source_target_pairs={{0,12},{4,0},{8,4},{12,8},{1,13},{5,1},{9,5},{13,9},{2,14},{6,2},{... | collective-permute-start | bytes 294920 | tf_op jit(solution)/shard_map/ppermute | solution.py:464
  9.3 12.1 %collective-permute-start.4 = (bf16[368,128]{1,0:T(8,128)(2,1)S(1)}, bf16[368,128]{1,0:T(8,128)(2,1)S(1)}, u32[]{:S(2)}, u32[]{:S(2)}) collective-permute-start(bf16[368,128]{1,0:T(8,128)(2,1)S(1)} %get-tuple-element.32), channel_id=1, source_target_pairs={{0,4},{4,8},{8,12},{12,0},{1,5},{5,9},{9,13},{13,1},{2,6},{6,10},{... | collective-permute-start | bytes 282632 | tf_op jit(solution)/shard_map/ppermute | solution.py:464
  9.4 12.1 %collective-permute-start.3 = (bf16[320,128]{1,0:T(8,128)(2,1)S(1)}, bf16[320,128]{1,0:T(8,128)(2,1)S(1)}, u32[]{:S(2)}, u32[]{:S(2)}) collective-permute-start(bf16[320,128]{1,0:T(8,128)(2,1)S(1)} %get-tuple-element.29.first_ref.rest_0_.rest_2_), channel_id=1, source_target_pairs={{0,4},{4,8},{8,12},{12,0},{1,5},{5,9},{9,13},{13,1},{2,6},{6,10},{... | collective-permute-start | bytes 245768 | tf_op jit(solution)/shard_map/ppermute | solution.py:464
  9.4 7.8 %collective-permute-start.6 = (bf16[304,128]{1,0:T(8,128)(2,1)S(1)}, bf16[304,128]{1,0:T(8,128)(2,1)S(1)}, u32[]{:S(2)}, u32[]{:S(2)}) collective-permute-start(bf16[304,128]{1,0:T(8,128)(2,1)S(1)} %get-tuple-element.30.second_ref.rest_1_.rest_3_), channel_id=1, source_target_pairs={{0,12},{4,0},{8,4},{12,8},{1,13},{5,1},{9,5},{13,9},{2,14},{6,2},{... | collective-permute-start | bytes 233480 | tf_op jit(solution)/shard_map/ppermute | solution.py:464
  17.2 6.5 %collective-permute-start.8 = (bf16[304,128]{1,0:T(8,128)(2,1)S(1)}, bf16[304,128]{1,0:T(8,128)(2,1)S(1)}, u32[]{:S(2)}, u32[]{:S(2)}) collective-permute-start(bf16[304,128]{1,0:T(8,128)(2,1)S(1)} %collective-permute-done.6.rest_5_.rest_7_), channel_id=1, source_target_pairs={{0,12},{4,0},{8,4},{12,8},{1,13},{5,1},{9,5},{13,9},{2,14},{6,2},{... | collective-permute-start | bytes 233480 | tf_op jit(solution)/shard_map/ppermute | solution.py:464
  21.5 6.2 %collective-permute-start.7 = (bf16[320,128]{1,0:T(8,128)(2,1)S(1)}, bf16[320,128]{1,0:T(8,128)(2,1)S(1)}, u32[]{:S(2)}, u32[]{:S(2)}) collective-permute-start(bf16[320,128]{1,0:T(8,128)(2,1)S(1)} %collective-permute-done.3.rest_2_.rest_4_), channel_id=1, source_target_pairs={{0,4},{4,8},{8,12},{12,0},{1,5},{5,9},{9,13},{13,1},{2,6},{6,10},{... | collective-permute-start | bytes 245768 | tf_op jit(solution)/shard_map/ppermute | solution.py:464
  40.2 1.3 %collective-permute-start.9 = (bf16[48,512]{1,0:T(8,128)(2,1)S(1)}, bf16[48,512]{1,0:T(8,128)(2,1)S(1)}, u32[]{:S(2)}, u32[]{:S(2)}) collective-permute-start(bf16[48,512]{1,0:T(8,128)(2,1)S(1)} %shard_map.114.mine_att_ref), channel_id=1, source_target_pairs={{0,1},{1,0},{2,3},{3,2},{4,5},{5,4},{6,7},{7,6},{8,9},{9,8},{10,11... | collective-permute-start | bytes 147464 | tf_op jit(solution)/shard_map/ppermute | solution.py:589
  43.2 1.6 %collective-permute-start.10 = (bf16[448,256]{1,0:T(8,128)(2,1)S(1)}, bf16[448,256]{1,0:T(8,128)(2,1)S(1)}, u32[]{:S(2)}, u32[]{:S(2)}) collective-permute-start(bf16[448,256]{1,0:T(8,128)(2,1)S(1)} %get-tuple-element.38.hidden_ref), channel_id=1, source_target_pairs={{0,1},{1,0},{2,3},{3,2},{4,5},{5,4},{6,7},{7,6},{8,9},{9,8},{10,11... | collective-permute-start | bytes 688136 | tf_op jit(solution)/shard_map/ppermute | solution.py:602

commit v6 on v5

--- a/solution.py
+++ b/solution.py
@@ -356,20 +356,25 @@
         out_ref[...] = finish(total_ref[...], heads)
 
 
+def mix_kernel(rows_ref, attended_ref, w_out_ref, part_ref):
+    channels = rows_ref.shape[1] // 2
+    for side, lanes in zip(halves(channels), (slice(0, channels), slice(channels, 2 * channels))):
+        delta = dot(attended_ref[...], w_out_ref[:, side], TN)
+        part_ref[:, lanes] = rows_ref[:, lanes].astype(F32) + delta
+
+
 def conv_kernel(
-    halo, info_ref, rows_ref, mine_att_ref, their_att_ref, mine_out_ref, their_out_ref, conv_in_ref,
-    taps_ref, after_ref, hidden_ref, gated,
+    halo, info_ref, part_ref, their_att_ref, their_out_ref, conv_in_ref, taps_ref,
+    after_ref, hidden_ref, gated,
 ):
     quarter, channels = hidden_ref.shape
     taps = taps_ref.shape[0]
     count = quarter + 2 * halo
     mine, theirs = halves(channels)
-    attended = jnp.concatenate([mine_att_ref[...], their_att_ref[...]], axis=0)
     sides = []
     for side, lanes in ((mine, slice(0, channels)), (theirs, slice(channels, 2 * channels))):
-        w_out = jnp.concatenate([mine_out_ref[:, side], their_out_ref[:, side]], axis=0)
-        delta = dot(attended, w_out, TN)
-        sides.append((rows_ref[:, lanes].astype(F32) + delta).astype(BF16)[:count])
+        delta = dot(their_att_ref[...], their_out_ref[:, side], TN)
+        sides.append((part_ref[:count, lanes] + delta[:count]).astype(BF16))
     after_ref[...] = sides[0][:quarter]
     gates = dot(sides[0], conv_in_ref[mine, :]) + dot(sides[1], conv_in_ref[theirs, :])
     value, gate = gates[:, :channels], gates[:, channels:]
@@ -587,14 +592,19 @@
         exps=quarter * queries * heads * len(stage),
     )
     their_attended = lax.ppermute(attended, "head", swap)
+    (part,) = call(
+        mix_kernel,
+        [vmem((queries, 2 * channels), F32)],
+        [rows, attended, w_out],
+        [VM] * 3,
+        flops=4 * queries * channels * width,
+        moved=queries * channels * 8,
+    )
     after, hidden = call(
         functools.partial(conv_kernel, halo),
         [vmem((quarter, channels), BF16), vmem((quarter, channels), BF16)],
-        [
-            info, rows, attended, their_attended, w_out, their_w_out,
-            gate_weights, conv_taps,
-        ],
-        [VM] * 8,
+        [info, part, their_attended, their_w_out, gate_weights, conv_taps],
+        [VM] * 6,
         [pltpu.VMEM((channels // 128, quarter + 2 * halo, 128), F32)],
         flops=2 * queries * 2 * channels * (96 + 2 * channels),
         moved=quarter * channels * 8,

time: 46.3 us -> 46.2 us (level)
    pallas_call x9 -> x10, Pallas kernels: 21.8 us -> 22.1 us  [call(): pl.pallas_call(kernel, out_shape=outs, in_specs=specs, out_specs=out_spec...]
  transfers between devices with their start and end apart: 11 -> 11, of which waited for: 5 -> 5; matrix products, arithmetic and copies ran while one was open for 0% -> 0% of each run, Pallas kernels for 10% -> 11%
where the time goes in v6:
time: 46.2 us; the launch traced here: 46.1 us
  Pallas kernels  22.1 us (48%)
  starting transfers between devices  14.5 us (31%)
  waiting for transfers between devices  8.54 us (18%)
  between operations  0.86 us (2%)
    pallas_call x10, Pallas kernels, call(): pl.pallas_call(kernel, out_shape=outs, in_specs=specs, out_specs=out_spec...  22.1 us
    ppermute x6, starting transfers between devices, ring(): lax.ppermute(array, 'tm', [(i, (i + by) % count) for i in range(count)])  13.1 us
    ppermute x6, waiting for transfers between devices, ring(): lax.ppermute(array, 'tm', [(i, (i + by) % count) for i in range(count)])  6.56 us
  transfers between devices with their start and end apart: 11, of which 5 were waited for; matrix products, arithmetic and copies ran while one was open for 0% of the time, Pallas kernels for 11%

profile of v6, /device:TPU:0, one launch (start us, length us, event | category | flops | bytes accessed | tf_op | source)
XLA Modules:
  0.0 46.1 jit_solution(14803184377140873849)
XLA Ops:
  0.0 0.0 copy-start.3
  0.7 0.0 copy-start
  0.7 0.0 copy-start.1
  0.7 0.0 copy-start.2
  0.7 1.5 %shard_map.109 = (bf16[448,256]{1,0:T(8,128)(2,1)S(1)}, s32[8,128]{1,0:T(8,128)S(1)}, bf16[1792,256]{1,0:T(8,128)(2,1)S(1)}, bf16[512,128]{1,0:T(8,128)(2,1)S(1)...) custom-call(s32[1]{0:T(128)S(6)} %copy.13.len_ref, bf16[1792,256]{1,0:T(8,128)(2,1)} %bitcast.8, ...), custom_call_target="tpu_custom_call" | custom-call | flops 3670016 | bytes 1376256 | tf_op jit(solution)/shard_map/pallas_call | solution.py:32
  2.3 0.6 %collective-permute-start = (bf16[448,256]{1,0:T(8,128)(2,1)S(1)}, bf16[448,256]{1,0:T(8,128)(2,1)S(1)}, u32[]{:S(2)}, u32[]{:S(2)}) collective-permute-start(bf16[448,256]{1,0:T(8,128)(2,1)S(1)} %get-tuple-element.25.mine_ref), channel_id=1, source_target_pairs={{0,1},{1,0},{2,3},{3,2},{4,5},{5,4},{6,7},{7,6},{8,9},{9,8},{10,11... | collective-permute-start | bytes 688136 | tf_op jit(solution)/shard_map/ppermute | solution.py:494
  2.8 0.1 collective-permute-start.2
  2.9 0.4 collective-permute-start.1
  3.3 0.6 %collective-permute-done.theirs_ref = bf16[448,256]{1,0:T(8,128)(2,1)S(1)} collective-permute-done((bf16[448,256]{1,0:T(8,128)(2,1)S(1)}, bf16[448,256]{1,0:T(8,128)(2,1)S(1)}, u32[]{:S(2)}, u32[]{:S(2)}) %collective-permute-start) | collective-permute-done | bytes 229408 | tf_op jit(solution)/shard_map/ppermute | solution.py:494
  3.9 0.4 shard_map.111
  4.4 5.0 %collective-permute-start.5 = (bf16[384,128]{1,0:T(8,128)(2,1)S(1)}, bf16[384,128]{1,0:T(8,128)(2,1)S(1)}, u32[]{:S(2)}, u32[]{:S(2)}) collective-permute-start(bf16[384,128]{1,0:T(8,128)(2,1)S(1)} %get-tuple-element.33), channel_id=1, source_target_pairs={{0,12},{4,0},{8,4},{12,8},{1,13},{5,1},{9,5},{13,9},{2,14},{6,2},{... | collective-permute-start | bytes 294920 | tf_op jit(solution)/shard_map/ppermute | solution.py:469
  9.3 0.0 collective-permute-start.4
  9.4 0.0 collective-permute-start.3
  9.4 0.0 collective-permute-done.1.rest_0_.their_out_ref
  9.4 3.8 %collective-permute-start.6 = (bf16[304,128]{1,0:T(8,128)(2,1)S(1)}, bf16[304,128]{1,0:T(8,128)(2,1)S(1)}, u32[]{:S(2)}, u32[]{:S(2)}) collective-permute-start(bf16[304,128]{1,0:T(8,128)(2,1)S(1)} %get-tuple-element.30.second_ref.rest_1_.rest_3_), channel_id=1, source_target_pairs={{0,12},{4,0},{8,4},{12,8},{1,13},{5,1},{9,5},{13,9},{2,14},{6,2},{... | collective-permute-start | bytes 233480 | tf_op jit(solution)/shard_map/ppermute | solution.py:469
  13.2 0.0 copy-done.3
  13.2 0.1 copy.12
  13.3 0.4 shard_map.110.qt_ref.qt_in_ref
  13.7 0.0 collective-permute-done.2.rest_1_.out_w_ref
  13.7 0.0 copy-done
  13.7 0.0 copy-done.1
  13.7 0.0 copy-done.2
  13.7 1.0 %shard_map.112 = (f32[64,512]{1,0:T(8,128)S(1)}, f32[1,256]{1,0:T(1,128)S(1)}) custom-call(s32[8,128]{1,0:T(8,128)S(1)} %get-tuple-element.24.info_ref, f32[128,512]{1,0:T(8,128)S(1)} %shard_map.110.qt_ref.qt_in_ref, bf16[320,128]{1,0:T(8,128)(2,1)S(1)} %get-tuple-element.29.first_ref.rest_0_.rest_2_, ...), custom_call_target="tpu_custom_call" | custom-call | flops 352321536 | bytes 917504 | tf_op jit(solution)/shard_map/pallas_call | solution.py:32
  14.7 2.5 %collective-permute-done.6.rest_5_.rest_7_ = bf16[304,128]{1,0:T(8,128)(2,1)S(1)} collective-permute-done((bf16[304,128]{1,0:T(8,128)(2,1)S(1)}, bf16[304,128]{1,0:T(8,128)(2,1)S(1)}, u32[]{:S(2)}, u32[]{:S(2)}) %collective-permute-start.6) | collective-permute-done | bytes 77856 | tf_op jit(solution)/shard_map/ppermute | solution.py:469
  17.2 4.3 %collective-permute-start.8 = (bf16[304,128]{1,0:T(8,128)(2,1)S(1)}, bf16[304,128]{1,0:T(8,128)(2,1)S(1)}, u32[]{:S(2)}, u32[]{:S(2)}) collective-permute-start(bf16[304,128]{1,0:T(8,128)(2,1)S(1)} %collective-permute-done.6.rest_5_.rest_7_), channel_id=1, source_target_pairs={{0,12},{4,0},{8,4},{12,8},{1,13},{5,1},{9,5},{13,9},{2,14},{6,2},{... | collective-permute-start | bytes 233480 | tf_op jit(solution)/shard_map/ppermute | solution.py:469
  21.5 0.0 collective-permute-done.3.rest_2_.rest_4_
  21.5 0.0 collective-permute-start.7
  21.5 0.0 collective-permute-done.4.rest_3_.rest_5_
  21.5 0.0 collective-permute-done.5.rest_4_.rest_6_
  21.5 2.2 %shard_map.113 = (bf16[512,512]{1,0:T(8,128)(2,1)S(1)}, f32[128,512]{1,0:T(8,128)S(1)}, f32[64,512]{1,0:T(8,128)S(1)}) custom-call(s32[8,128]{1,0:T(8,128)S(1)} %get-tuple-element.24.info_ref, bf16[448,256]{1,0:T(8,128)(2,1)S(1)} %get-tuple-element.25.mine_ref, bf16[448,256]{1,0:T(8,128)(2,1)S(1)} %collective-permute-done.theirs_ref, ...), custom_call_target="tpu_custom_call" | custom-call | flops 1056964608 | bytes 917504 | tf_op jit(solution)/shard_map/pallas_call | solution.py:32
  23.7 0.0 collective-permute-done.8.rest_1_
  23.7 4.0 %collective-permute-done.7.rest_0_ = bf16[320,128]{1,0:T(8,128)(2,1)S(1)} collective-permute-done((bf16[320,128]{1,0:T(8,128)(2,1)S(1)}, bf16[320,128]{1,0:T(8,128)(2,1)S(1)}, u32[]{:S(2)}, u32[]{:S(2)}) %collective-permute-start.7) | collective-permute-done | bytes 81952 | tf_op jit(solution)/shard_map/ppermute | solution.py:469
  27.7 12.4 %shard_map.114.attended_ref = bf16[48,512]{1,0:T(8,128)(2,1)S(1)} custom-call(s32[8,128]{1,0:T(8,128)S(1)} %get-tuple-element.24.info_ref, f32[128,512]{1,0:T(8,128)S(1)} %get-tuple-element.35.qt_ref, f32[64,512]{1,0:T(8,128)S(1)} %get-tuple-element.36.sum_in_ref, bf16[320,128]{1,0:T(8,128)(2,1)S(1)} %collective-permute-done.7.rest_0_, ...), custom_call_target="tpu_custom_call" | custom-call | flops 352321536 | bytes 917504 | tf_op jit(solution)/shard_map/pallas_call | solution.py:32
  40.1 0.1 collective-permute-start.9
  40.2 0.3 shard_map.115.part_ref
  40.5 0.9 %collective-permute-done.9.their_att_ref = bf16[48,512]{1,0:T(8,128)(2,1)S(1)} collective-permute-done((bf16[48,512]{1,0:T(8,128)(2,1)S(1)}, bf16[48,512]{1,0:T(8,128)(2,1)S(1)}, u32[]{:S(2)}, u32[]{:S(2)}) %collective-permute-start.9) | collective-permute-done | bytes 49184 | tf_op jit(solution)/shard_map/ppermute | solution.py:594
  41.4 1.8 %shard_map.116 = (bf16[448,256]{1,0:T(8,128)(2,1)S(1)}, bf16[448,256]{1,0:T(8,128)(2,1)S(1)}) custom-call(s32[8,128]{1,0:T(8,128)S(1)} %get-tuple-element.24.info_ref, f32[512,512]{1,0:T(8,128)S(1)} %shard_map.115.part_ref, bf16[48,512]{1,0:T(8,128)(2,1)S(1)} %collective-permute-done.9.their_att_ref, ...), custom_call_target="tpu_custom_call" | custom-call | flops 318767104 | bytes 917504 | tf_op jit(solution)/shard_map/pallas_call | solution.py:32
  43.2 0.2 collective-permute-start.10
  43.4 0.8 %shard_map.117 = (f32[448,256]{1,0:T(8,128)S(1)}, f32[2,1792,128]{2,1,0:T(8,128)S(1)}) custom-call(s32[8,128]{1,0:T(8,128)S(1)} %get-tuple-element.24.info_ref, bf16[448,256]{1,0:T(8,128)(2,1)S(1)} %get-tuple-element.37.after_ref, bf16[448,256]{1,0:T(8,128)(2,1)S(1)} %get-tuple-element.38.hidden_ref, bf16[256,512]{1,0:T(8,128)(2,1)S(1)} %copy-done, ...), custom_call_target="tpu_custom_call" | custom-call | flops 58720256 | bytes 458752 | tf_op jit(solution)/shard_map/pallas_call | solution.py:32
  44.3 0.5 %collective-permute-done.10.hidden_ref = bf16[448,256]{1,0:T(8,128)(2,1)S(1)} collective-permute-done((bf16[448,256]{1,0:T(8,128)(2,1)S(1)}, bf16[448,256]{1,0:T(8,128)(2,1)S(1)}, u32[]{:S(2)}, u32[]{:S(2)}) %collective-permute-start.10) | collective-permute-done | bytes 229408 | tf_op jit(solution)/shard_map/ppermute | solution.py:612
  44.8 1.3 %shard_map.118 = bf16[1792,256]{1,0:T(8,128)(2,1)} custom-call(s32[8,128]{1,0:T(8,128)S(1)} %get-tuple-element.24.info_ref, f32[448,256]{1,0:T(8,128)S(1)} %get-tuple-element.41.base_ref, bf16[448,256]{1,0:T(8,128)(2,1)S(1)} %collective-permute-done.10.hidden_ref, bf16[256,512]{1,0:T(8,128)(2,1)S(1)} %collective-permute-done.2.rest_1_.out_w_ref, ...), custom_call_target="tpu_custom_call" | custom-call | flops 58720256 | bytes 1835008 | tf_op jit(solution)/shard_map/pallas_call | solution.py:32
Async XLA Ops:
  0.0 13.2 %copy-start.3 = (bf16[512,2,256]{2,1,0:T(2,128)(2,1)S(1)}, bf16[512,2,256]{2,1,0:T(2,128)(2,1)}, u32[]{:S(2)}) copy-start(bf16[512,2,256]{2,1,0:T(2,128)(2,1)} %param.18) | copy-start | bytes 1572868
  0.7 13.0 %copy-start = (bf16[256,512]{1,0:T(8,128)(2,1)S(1)}, bf16[256,512]{1,0:T(8,128)(2,1)}, u32[]{:S(2)}) copy-start(bf16[256,512]{1,0:T(8,128)(2,1)} %out_w_ref.1) | copy-start | bytes 786436
  0.7 13.0 %copy-start.1 = (bf16[48,512]{1,0:T(8,128)(2,1)S(1)}, bf16[48,512]{1,0:T(8,128)(2,1)}, u32[]{:S(2)}) copy-start(bf16[48,512]{1,0:T(8,128)(2,1)} %w_out_ref.1) | copy-start | bytes 147460
  0.7 13.0 %copy-start.2 = (f32[31,256]{1,0:T(8,128)S(1)}, f32[31,256]{1,0:T(8,128)}, u32[]{:S(2)}) copy-start(f32[31,256]{1,0:T(8,128)} %taps_ref.1) | copy-start | bytes 95236
  2.3 1.7 %collective-permute-start = (bf16[448,256]{1,0:T(8,128)(2,1)S(1)}, bf16[448,256]{1,0:T(8,128)(2,1)S(1)}, u32[]{:S(2)}, u32[]{:S(2)}) collective-permute-start(bf16[448,256]{1,0:T(8,128)(2,1)S(1)} %get-tuple-element.25.mine_ref), channel_id=1, source_target_pairs={{0,1},{1,0},{2,3},{3,2},{4,5},{5,4},{6,7},{7,6},{8,9},{9,8},{10,11... | collective-permute-start | bytes 688136 | tf_op jit(solution)/shard_map/ppermute | solution.py:494
  2.8 10.9 %collective-permute-start.2 = (bf16[256,512]{1,0:T(8,128)(2,1)}, bf16[256,512]{1,0:T(8,128)(2,1)S(1)}, u32[]{:S(2)}, u32[]{:S(2)}) collective-permute-start(bf16[256,512]{1,0:T(8,128)(2,1)} %out_w_ref.1), channel_id=1, source_target_pairs={{0,1},{1,0},{2,3},{3,2},{4,5},{5,4},{6,7},{7,6},{8,9},{9,8},{10,11... | collective-permute-start | bytes 786440 | tf_op jit(solution)/shard_map/ppermute | solution.py:521
  2.9 6.5 %collective-permute-start.1 = (bf16[48,512]{1,0:T(8,128)(2,1)}, bf16[48,512]{1,0:T(8,128)(2,1)S(1)}, u32[]{:S(2)}, u32[]{:S(2)}) collective-permute-start(bf16[48,512]{1,0:T(8,128)(2,1)} %w_out_ref.1), channel_id=1, source_target_pairs={{0,1},{1,0},{2,3},{3,2},{4,5},{5,4},{6,7},{7,6},{8,9},{9,8},{10,11... | collective-permute-start | bytes 147464 | tf_op jit(solution)/shard_map/ppermute | solution.py:520
  4.4 17.1 %collective-permute-start.5 = (bf16[384,128]{1,0:T(8,128)(2,1)S(1)}, bf16[384,128]{1,0:T(8,128)(2,1)S(1)}, u32[]{:S(2)}, u32[]{:S(2)}) collective-permute-start(bf16[384,128]{1,0:T(8,128)(2,1)S(1)} %get-tuple-element.33), channel_id=1, source_target_pairs={{0,12},{4,0},{8,4},{12,8},{1,13},{5,1},{9,5},{13,9},{2,14},{6,2},{... | collective-permute-start | bytes 294920 | tf_op jit(solution)/shard_map/ppermute | solution.py:469
  9.3 12.1 %collective-permute-start.4 = (bf16[368,128]{1,0:T(8,128)(2,1)S(1)}, bf16[368,128]{1,0:T(8,128)(2,1)S(1)}, u32[]{:S(2)}, u32[]{:S(2)}) collective-permute-start(bf16[368,128]{1,0:T(8,128)(2,1)S(1)} %get-tuple-element.32), channel_id=1, source_target_pairs={{0,4},{4,8},{8,12},{12,0},{1,5},{5,9},{9,13},{13,1},{2,6},{6,10},{... | collective-permute-start | bytes 282632 | tf_op jit(solution)/shard_map/ppermute | solution.py:469
  9.4 12.1 %collective-permute-start.3 = (bf16[320,128]{1,0:T(8,128)(2,1)S(1)}, bf16[320,128]{1,0:T(8,128)(2,1)S(1)}, u32[]{:S(2)}, u32[]{:S(2)}) collective-permute-start(bf16[320,128]{1,0:T(8,128)(2,1)S(1)} %get-tuple-element.29.first_ref.rest_0_.rest_2_), channel_id=1, source_target_pairs={{0,4},{4,8},{8,12},{12,0},{1,5},{5,9},{9,13},{13,1},{2,6},{6,10},{... | collective-permute-start | bytes 245768 | tf_op jit(solution)/shard_map/ppermute | solution.py:469
  9.4 7.8 %collective-permute-start.6 = (bf16[304,128]{1,0:T(8,128)(2,1)S(1)}, bf16[304,128]{1,0:T(8,128)(2,1)S(1)}, u32[]{:S(2)}, u32[]{:S(2)}) collective-permute-start(bf16[304,128]{1,0:T(8,128)(2,1)S(1)} %get-tuple-element.30.second_ref.rest_1_.rest_3_), channel_id=1, source_target_pairs={{0,12},{4,0},{8,4},{12,8},{1,13},{5,1},{9,5},{13,9},{2,14},{6,2},{... | collective-permute-start | bytes 233480 | tf_op jit(solution)/shard_map/ppermute | solution.py:469
  17.2 6.5 %collective-permute-start.8 = (bf16[304,128]{1,0:T(8,128)(2,1)S(1)}, bf16[304,128]{1,0:T(8,128)(2,1)S(1)}, u32[]{:S(2)}, u32[]{:S(2)}) collective-permute-start(bf16[304,128]{1,0:T(8,128)(2,1)S(1)} %collective-permute-done.6.rest_5_.rest_7_), channel_id=1, source_target_pairs={{0,12},{4,0},{8,4},{12,8},{1,13},{5,1},{9,5},{13,9},{2,14},{6,2},{... | collective-permute-start | bytes 233480 | tf_op jit(solution)/shard_map/ppermute | solution.py:469
  21.5 6.2 %collective-permute-start.7 = (bf16[320,128]{1,0:T(8,128)(2,1)S(1)}, bf16[320,128]{1,0:T(8,128)(2,1)S(1)}, u32[]{:S(2)}, u32[]{:S(2)}) collective-permute-start(bf16[320,128]{1,0:T(8,128)(2,1)S(1)} %collective-permute-done.3.rest_2_.rest_4_), channel_id=1, source_target_pairs={{0,4},{4,8},{8,12},{12,0},{1,5},{5,9},{9,13},{13,1},{2,6},{6,10},{... | collective-permute-start | bytes 245768 | tf_op jit(solution)/shard_map/ppermute | solution.py:469
  40.1 1.3 %collective-permute-start.9 = (bf16[48,512]{1,0:T(8,128)(2,1)S(1)}, bf16[48,512]{1,0:T(8,128)(2,1)S(1)}, u32[]{:S(2)}, u32[]{:S(2)}) collective-permute-start(bf16[48,512]{1,0:T(8,128)(2,1)S(1)} %shard_map.114.attended_ref), channel_id=1, source_target_pairs={{0,1},{1,0},{2,3},{3,2},{4,5},{5,4},{6,7},{7,6},{8,9},{9,8},{10,11... | collective-permute-start | bytes 147464 | tf_op jit(solution)/shard_map/ppermute | solution.py:594
  43.2 1.6 %collective-permute-start.10 = (bf16[448,256]{1,0:T(8,128)(2,1)S(1)}, bf16[448,256]{1,0:T(8,128)(2,1)S(1)}, u32[]{:S(2)}, u32[]{:S(2)}) collective-permute-start(bf16[448,256]{1,0:T(8,128)(2,1)S(1)} %get-tuple-element.38.hidden_ref), channel_id=1, source_target_pairs={{0,1},{1,0},{2,3},{3,2},{4,5},{5,4},{6,7},{7,6},{8,9},{9,8},{10,11... | collective-permute-start | bytes 688136 | tf_op jit(solution)/shard_map/ppermute | solution.py:612
